TPU v7x, 512 devices: a whole 4x8x8 slice. The times are simulated.
512 devices in a mesh: dp: 32 (over x, y), tensor: 16 (over z, core).
Axes of the slice: x: 4, y: 8, z: 8, core: 2. Of those that a mesh axis runs over, the one named last changes fastest.
Arguments:
- acts: bfloat16 [4096, 4096], P('dp'), may hold values from -6 to 6
- grad_out: bfloat16 [4096, 14336], P('dp', 'tensor'), may hold values from -0.09375 to 0.09375
- selected: int32 [16, 1], P('tensor'), may hold values from 0 to 6, as said below
- owner: int32 [16, 192, 1], P('tensor'), may hold values from 0 to 31; in each aligned block of 192 rows (0 to 191, 192 to 383, ..., all dimensions but the last counted through in order) at most 9 rows name the same one
- sel_weight: float32 [4096, 2048], P('dp', 'tensor'), may hold values from -3 to 3
- sel_moment: float32 [4096, 2048], P('dp', 'tensor'), may hold values from -3 to 3
- sel_second: float32 [4096, 2048], P('dp', 'tensor'), may hold values from 0.01 to 1
- off_weight: float32 [32, 16, 9, 128, 128], P('dp', 'tensor'), may hold values from -3 to 3
- off_moment: float32 [32, 16, 9, 128, 128], P('dp', 'tensor'), may hold values from -3 to 3
- off_second: float32 [32, 16, 9, 128, 128], P('dp', 'tensor'), may hold values from 0.01 to 1
Outputs:
- column_norm: float32 [14336], P('tensor')
- sel_weight_new: float32 [4096, 2048], P('dp', 'tensor')
- sel_moment_new: float32 [4096, 2048], P('dp', 'tensor')
- sel_second_new: float32 [4096, 2048], P('dp', 'tensor')
- off_weight_new: float32 [32, 16, 9, 128, 128], P('dp', 'tensor')
- off_moment_new: float32 [32, 16, 9, 128, 128], P('dp', 'tensor')
- off_second_new: float32 [32, 16, 9, 128, 128], P('dp', 'tensor')
Inputs may be any that keep to these rules, and one draw needn't show every extreme that they name: `selected`: each row names 1 tile. For each index of tensor, no owner receives more than 9 pieces, and some owner receives exactly 9.
All inputs are finite; a program needn't handle non-finite values.
Results may differ from a plain program's by a relative error of at most 0.0017.
Values may be sent and summed in bfloat16 or wider, within the bound.
No kernel may reach another device: no remote copies, remote signals or barrier semaphores. Data moves between devices by JAX's collectives and lax.ppermute only.
A program may use at most 128 MiB of HBM per device.

v0:
```python
import jax
import jax.numpy as jnp
from jax import lax
from jax.sharding import Mesh
from jax.sharding import PartitionSpec as P

TILE = 128
DP = ("dp_0", "dp_1")


beta_one = 0.9
beta_two = 0.95
adam_eps = 1e-08
learn_rate = 0.01
decay_rate = 0.1
step_count = 10.0


def sent_to_all(array, axis):
    copies = jnp.broadcast_to(array, (lax.axis_size(axis), *array.shape))
    return lax.all_to_all(copies, axis, split_axis=0, concat_axis=0, tiled=True)


def over_copies(array, axis):
    return sent_to_all(array, axis).sum(axis=0)


def sum_by_axis(total, axes):
    for axis in axes:
        total = lax.psum_scatter(total, axis, scatter_dimension=0, tiled=True)
    return total


def adam_update(weight, moment, second, grad):
    moment_new = beta_one * moment + (1.0 - beta_one) * grad
    second_new = beta_two * second + (1.0 - beta_two) * grad * grad
    first_fix = 1.0 - beta_one**step_count
    second_fix = 1.0 - beta_two**step_count
    update = moment_new / first_fix / (jnp.sqrt(second_new / second_fix) + adam_eps)
    return (weight - learn_rate * (update + decay_rate * weight), moment_new, second_new)


def rest_tiles(selected_row, tiles_here):
    tiles = jnp.arange(tiles_here, dtype=jnp.int32)
    chosen = jnp.any(tiles[:, None] == selected_row[None, :], axis=1).astype(jnp.int32)
    order = jnp.argsort(chosen * tiles_here + tiles)
    return order[: tiles_here - selected_row.shape[0]]


def slot_numbers(owner_row):
    places = jnp.arange(owner_row.shape[0], dtype=jnp.int32)
    earlier = (owner_row[:, None] == owner_row[None, :]) & (places[:, None] > places[None, :])
    return jnp.sum(earlier.astype(jnp.int32), axis=1)


def contract_tokens(left, right):
    return lax.dot_general(
        left, right, (((0,), (0,)), ((), ())), preferred_element_type=jnp.float32
    )


def body(
    acts,
    grad_out,
    selected,
    owner,
    sel_weight,
    sel_moment,
    sel_second,
    off_weight,
    off_moment,
    off_second,
):
    group_size = lax.axis_size(DP)
    tokens_here, rows_all = acts.shape
    cols_here = grad_out.shape[1]
    tiles_here = cols_here // TILE
    sel_count = selected.shape[1]
    rest_count = tiles_here - sel_count
    row_block = rows_all // group_size
    capacity = off_weight.shape[2]
    piece_count = rest_count * group_size
    selected_row = selected[0]
    owner_row = owner[0, :, 0]
    rest_row = rest_tiles(selected_row, tiles_here)
    grad_tiles = grad_out.reshape(tokens_here, tiles_here, TILE)
    zero_half = jnp.zeros((), jnp.bfloat16)
    gram = lax.dot_general(acts, acts, (((1,), (1,)), ((), ())), preferred_element_type=jnp.float32)
    grad_wide = grad_out.astype(jnp.float32)
    squares = jnp.sum(grad_wide * jnp.dot(gram, grad_wide, precision=lax.Precision.HIGHEST), axis=0)
    column_norm = jnp.sqrt(over_copies(squares, DP))
    sel_grad = jnp.take(grad_tiles, selected_row, axis=1).reshape(tokens_here, sel_count * TILE)
    sel_sum = sum_by_axis(contract_tokens(acts, sel_grad), DP)
    new_sel = adam_update(sel_weight, sel_moment, sel_second, sel_sum)
    rest_grad = jnp.moveaxis(jnp.take(grad_tiles, rest_row, axis=1), 1, 0)

    def tile_partial(column):
        return contract_tokens(acts, column).astype(jnp.bfloat16)

    partials = lax.map(tile_partial, rest_grad).reshape(rest_count, group_size, row_block, TILE)
    slot_index = slot_numbers(owner_row)
    target = owner_row * capacity + slot_index
    source = (
        jnp.full((group_size * capacity,), piece_count, jnp.int32)
        .at[target]
        .set(jnp.arange(piece_count, dtype=jnp.int32))
    )
    filled = source < piece_count
    flat_pieces = partials.reshape(piece_count, row_block, TILE)
    outgoing = jnp.where(
        filled[:, None, None], flat_pieces[jnp.minimum(source, piece_count - 1)], zero_half
    )
    received = lax.all_to_all(
        outgoing.reshape(group_size, capacity, row_block, TILE),
        DP,
        split_axis=0,
        concat_axis=0,
        tiled=True,
    )
    offload = jnp.sum(received, axis=0, dtype=jnp.float32).astype(jnp.bfloat16)
    off_grad = offload.astype(jnp.float32).reshape(off_weight.shape)
    new_off = adam_update(off_weight, off_moment, off_second, off_grad)
    return (column_norm, new_sel[0], new_sel[1], new_sel[2], new_off[0], new_off[1], new_off[2])


def solution(mesh):
    torus = Mesh(mesh.devices.reshape(4, 8, mesh.shape["tensor"]), ("dp_0", "dp_1", "tensor"))
    in_specs = (
        P(DP, None),
        P(DP, "tensor"),
        P("tensor", None),
        P("tensor", None, None),
        P(DP, "tensor"),
        P(DP, "tensor"),
        P(DP, "tensor"),
        P(DP, "tensor", None, None, None),
        P(DP, "tensor", None, None, None),
        P(DP, "tensor", None, None, None),
    )
    out_specs = (
        P("tensor"),
        P(DP, "tensor"),
        P(DP, "tensor"),
        P(DP, "tensor"),
        P(DP, "tensor", None, None, None),
        P(DP, "tensor", None, None, None),
        P(DP, "tensor", None, None, None),
    )
    return jax.shard_map(body, mesh=torus, in_specs=in_specs, out_specs=out_specs, check_vma=False)
```

profile of v0, /device:TPU:412, one launch (start us, length us, event | category | flops | bytes accessed | tf_op | source)
XLA Modules:
  0.0 313.8 jit_solution(4075800452341468061)
XLA Ops:
  7.2 2.1 fusion.22
  9.3 1.4 fusion.4
  11.4 9.9 %all-to-all-start = ((f32[32,1,896]{2,1,0:T(1,128)}), f32[32,1,896]{2,1,0:T(1,128)S(1)}, u32[]{:S(2)}, u32[]{:S(2)}) async-start(f32[32,1,896]{2,1,0:T(1,128)} %broadcast_in_dim.56), calls=%async_computation | async-start | bytes 229376 | tf_op jit(solution)/shard_map/all_to_all | solution.py:21
  21.3 1.1 copy.48
  24.1 1.2 scatter_custom_fusion
  27.8 20.6 %while.11 = (s32[]{:T(128)}, bf16[6,4096,128]{2,1,0:T(8,128)(2,1)}, bf16[6,128,128]{2,1,0:T(8,128)(2,1)S(1)}, bf16[128,4096]{1,0:T(8,128)(2,1)}, s32[]{:T(128)}) while((s32[]{:T(128)}, bf16[6,4096,128]{2,1,0:T(8,128)(2,1)}, bf16[6,128,128]{2,1,0:T(8,128)(2,1)S(1)}, bf16[128,4096]{1,0:T(8,128)(2,1)}, s32[]{:T(128)}) %tuple.36), condition=%wide.region_8.9_spmd, body=%wide.region_7.8_spmd.sunk | while | flops 134742016 | bytes 6324801 | solution.py:100
  27.8 1.7 fusion.34
  30.2 1.1 constant_dynamic-update-slice_fusion.2
  31.2 1.7 fusion.34
  33.6 1.1 constant_dynamic-update-slice_fusion.2
  34.7 1.7 fusion.34
  38.1 1.7 fusion.34
  41.5 1.7 fusion.34
  44.9 1.7 fusion.34
  47.3 1.1 constant_dynamic-update-slice_fusion.2
  48.5 13.0 %gather_fusion.1 = bf16[288,128,128]{2,1,0:T(8,128)(2,1)} fusion(bf16[192,128,128]{2,1,0:T(8,128)(2,1)} %bitcast.50, s32[1024]{0:T(1024)S(1)} %pad_clamp_fusion), kind=kCustom, calls=%fused_computation.1 | custom fusion | bytes 18875520 | tf_op jit(solution)/shard_map/gather | solution.py:111
  61.5 8.0 %broadcast_select_fusion = bf16[32,9,128,128]{3,2,1,0:T(8,128)(2,1)} fusion(bf16[32,9,128,128]{3,2,1,0:T(8,128)(2,1)} %bitcast.49, pred[32,9]{1,0:T(8,128)(4,1)S(1)} %broadcast_in_dim.60), kind=kLoop, calls=%fused_computation.9 | loop fusion | flops 4718592 | bytes 18874656 | tf_op jit(solution)/shard_map/jit(_where)/select_n | solution.py:110
  69.5 10.0 %all-to-all-start.1 = ((bf16[32,9,128,128]{3,2,1,0:T(8,128)(2,1)}), bf16[32,9,128,128]{3,2,1,0:T(8,128)(2,1)}, u32[]{:S(2)}, u32[]{:S(2)}) async-start(bf16[32,9,128,128]{3,2,1,0:T(8,128)(2,1)} %broadcast_select_fusion), calls=%async_computation.3 | async-start | bytes 18874368 | tf_op jit(solution)/shard_map/all_to_all | solution.py:113
  79.6 1.7 convolution_bitcast_fusion
  81.4 62.6 %reduce-scatter.3.cloned.1.call-done = f32[1024,128]{0,1:T(8,128)} async-done(((f32[4096,128]{0,1:T(8,128)}), f32[1024,128]{0,1:T(8,128)}) %reduce-scatter.3.cloned.1.call-update) | async-done | bytes 524304 | tf_op jit(solution)/shard_map/reduce_scatter | solution.py:30
  145.1 74.8 %reduce-scatter.5.cloned.1.call-done = f32[128,128]{0,1:T(8,128)} async-done(((f32[1024,128]{0,1:T(8,128)}), f32[128,128]{0,1:T(8,128)}) %reduce-scatter.5.cloned.1.call-update) | async-done | bytes 65552 | tf_op jit(solution)/shard_map/reduce_scatter | solution.py:30
  223.0 76.4 %all-to-all-done.1 = bf16[32,9,128,128]{3,2,1,0:T(8,128)(2,1)} async-done(((bf16[32,9,128,128]{3,2,1,0:T(8,128)(2,1)}), bf16[32,9,128,128]{3,2,1,0:T(8,128)(2,1)}, u32[]{:S(2)}, u32[]{:S(2)}) %all-to-all-start.1) | async-done | bytes 9437216 | tf_op jit(solution)/shard_map/all_to_all | solution.py:113
  299.5 6.0 %reduce_sum.45 = bf16[9,128,128]{2,1,0:T(8,128)(2,1)S(1)} reduce(bf16[32,9,128,128]{3,2,1,0:T(8,128)(2,1)} %all-to-all-done.1, bf16[]{:T(256)} %constant.53.clone.1), dimensions={0}, to_apply=%region_9.10 | reduce | flops 4571136 | bytes 9732098 | tf_op jit(solution)/shard_map/reduce_sum | solution.py:120
  305.5 1.5 multiply_subtract_fusion
  (54 shorter events, 15.6 us)
Async XLA Ops:
  11.4 58.1 %all-to-all-start = ((f32[32,1,896]{2,1,0:T(1,128)}), f32[32,1,896]{2,1,0:T(1,128)S(1)}, u32[]{:S(2)}, u32[]{:S(2)}) async-start(f32[32,1,896]{2,1,0:T(1,128)} %broadcast_in_dim.56), calls=%async_computation | async-start | bytes 229376 | tf_op jit(solution)/shard_map/all_to_all | solution.py:21
  69.5 10.1 %copy-start = (bf16[128,4096]{1,0:T(8,128)(2,1)S(1)}, bf16[128,4096]{1,0:T(8,128)(2,1)}, u32[]{:S(2)}) copy-start(bf16[128,4096]{1,0:T(8,128)(2,1)} %get-tuple-element.129) | copy-start | bytes 3145732
  69.5 74.6 %copy-start.4 = (f32[128,128]{1,0:T(8,128)S(1)}, f32[128,128]{1,0:T(8,128)}, u32[]{:S(2)}) copy-start(f32[128,128]{1,0:T(8,128)} %param.17) | copy-start | bytes 196612
  69.5 74.7 %copy-start.5 = (f32[128,128]{1,0:T(8,128)S(1)}, f32[128,128]{1,0:T(8,128)}, u32[]{:S(2)}) copy-start(f32[128,128]{1,0:T(8,128)} %param.18) | copy-start | bytes 196612
  69.5 74.8 %copy-start.6 = (f32[128,128]{1,0:T(8,128)S(1)}, f32[128,128]{1,0:T(8,128)}, u32[]{:S(2)}) copy-start(f32[128,128]{1,0:T(8,128)} %param.16) | copy-start | bytes 196612
  69.5 229.9 %all-to-all-start.1 = ((bf16[32,9,128,128]{3,2,1,0:T(8,128)(2,1)}), bf16[32,9,128,128]{3,2,1,0:T(8,128)(2,1)}, u32[]{:S(2)}, u32[]{:S(2)}) async-start(bf16[32,9,128,128]{3,2,1,0:T(8,128)(2,1)} %broadcast_select_fusion), calls=%async_computation.3 | async-start | bytes 18874368 | tf_op jit(solution)/shard_map/all_to_all | solution.py:113
  79.5 64.5 %reduce-scatter.3.cloned.1.call-start = ((), (), s32[]{:S(2)}) async-start(), calls=%async_computation.4 | async-start | bytes 2621440 | tf_op jit(solution)/shard_map/reduce_scatter | solution.py:30
  81.4 224.1 %copy-start.1 = (f32[1,1,9,128,128]{4,3,2,1,0:T(8,128)S(1)}, f32[1,1,9,128,128]{4,3,2,1,0:T(8,128)}, u32[]{:S(2)}) copy-start(f32[1,1,9,128,128]{4,3,2,1,0:T(8,128)} %param.19) | copy-start | bytes 1769476
  81.4 224.1 %copy-start.2 = (f32[1,1,9,128,128]{4,3,2,1,0:T(8,128)S(1)}, f32[1,1,9,128,128]{4,3,2,1,0:T(8,128)}, u32[]{:S(2)}) copy-start(f32[1,1,9,128,128]{4,3,2,1,0:T(8,128)} %param.20) | copy-start | bytes 1769476
  81.4 224.1 %copy-start.3 = (f32[1,1,9,128,128]{4,3,2,1,0:T(8,128)S(1)}, f32[1,1,9,128,128]{4,3,2,1,0:T(8,128)}, u32[]{:S(2)}) copy-start(f32[1,1,9,128,128]{4,3,2,1,0:T(8,128)} %param.21) | copy-start | bytes 1769476
  81.4 138.5 %reduce-scatter.5.cloned.1.call-start = ((), (), s32[]{:S(2)}) async-start(), calls=%async_computation.5 | async-start | bytes 589824 | tf_op jit(solution)/shard_map/reduce_scatter | solution.py:30
Sparse Core Ops, SparseCore 0:
  83.2 60.8 reduce-scatter.2
  147.1 72.7 reduce-scatter.4
where the time goes:
time: 316 us; the launch traced here: 314 us
  waiting for transfers between devices  214 us (68%)
  local copies, waits for them, and re-layouts  30.4 us (10%)
  starting transfers between devices  20 us (6%)
  other arithmetic  19.2 us (6%)
  matrix products  15.3 us (5%)
  between operations  14.9 us (5%)
    reduce_scatter x2, waiting for transfers between devices, sum_by_axis(): total = lax.psum_scatter(total, axis, scatter_dimension=0, tiled=True)  137 us
    all_to_all x1, waiting for transfers between devices, body(): lax.all_to_all(outgoing.reshape(group_size, capacity, row_block, TILE), D...  76.4 us
    gather x1, local copies, waits for them, and re-layouts, body(): flat_pieces[jnp.minimum(source, piece_count - 1)]  13 us
    dot_general x7, matrix products, contract_tokens(): lax.dot_general(left, right, (((0,), (0,)), ((), ())), preferred_element_...  11.8 us
    dynamic_update_slice x12, local copies, waits for them, and re-layouts, body(): lax.map(tile_partial, rest_grad)  10.4 us
    all_to_all x1, starting transfers between devices, body(): lax.all_to_all(outgoing.reshape(group_size, capacity, row_block, TILE), D...  9.98 us
    all_to_all x1, starting transfers between devices, sent_to_all(): return lax.all_to_all(copies, axis, split_axis=0, concat_axis=0, tiled=True)  9.89 us
    select_n x1, other arithmetic, body(): jnp.where(filled[:, None, None], flat_pieces[jnp.minimum(source, piece_co...  8.03 us
  transfers between devices with their start and end apart: 4, of which 3 were waited for; matrix products, arithmetic and copies ran while one was open for 17% of the time, Pallas kernels for 0%

commit v1 on v0

v1 whole, which is shorter than its diff:
```python
import jax
import jax.numpy as jnp
from jax import lax
from jax.experimental import pallas as pl
from jax.experimental.pallas import tpu as pltpu
from jax.sharding import Mesh
from jax.sharding import PartitionSpec as P

TILE = 128
DP = ("dp_0", "dp_1")


beta_one = 0.9
beta_two = 0.95
adam_eps = 1e-08
learn_rate = 0.01
decay_rate = 0.1
step_count = 10.0


def adam_update(weight, moment, second, grad):
    moment_new = beta_one * moment + (1.0 - beta_one) * grad
    second_new = beta_two * second + (1.0 - beta_two) * grad * grad
    first_fix = 1.0 - beta_one**step_count
    second_fix = 1.0 - beta_two**step_count
    update = moment_new / first_fix / (jnp.sqrt(second_new / second_fix) + adam_eps)
    return (weight - learn_rate * (update + decay_rate * weight), moment_new, second_new)


def slot_numbers(owner_row):
    places = jnp.arange(owner_row.shape[0], dtype=jnp.int32)
    earlier = (owner_row[:, None] == owner_row[None, :]) & (places[:, None] > places[None, :])
    return jnp.sum(earlier.astype(jnp.int32), axis=1)


def replica_sums(
    selected_ref, target_ref, acts_ref, grads_ref, slots_ref, sel_ref, sums, places, *, per_step
):
    step = pl.program_id(0)
    steps = pl.num_programs(0)
    rows, tokens = acts_ref.shape[1:]
    rest_count = sums.shape[0] - 1
    selected = selected_ref[0]

    @pl.when(step == 0)
    def _():
        sums[...] = jnp.zeros_like(sums)

    for k in range(rest_count + 1):
        tile = k + (k >= selected).astype(jnp.int32) if k < rest_count else selected
        column = pl.ds(pl.multiple_of(tile * TILE, TILE), TILE)
        total = sums[k]
        for s in range(per_step):
            partial = jnp.dot(
                acts_ref[s],
                grads_ref[pl.ds(s * tokens, tokens), column],
                preferred_element_type=jnp.float32,
            )
            if k < rest_count:
                partial = partial.astype(jnp.bfloat16).astype(jnp.float32)
            total = total + partial
        sums[k] = total

    @pl.when(step == steps - 1)
    def _():
        blocks, part, _ = sel_ref.shape
        places[...] = jnp.zeros_like(places)
        for k in range(rest_count):
            for b in range(blocks):
                places[target_ref[k * blocks + b]] = sums[k, b * part : (b + 1) * part, :]
        slots_ref[...] = places[...].astype(slots_ref.dtype)
        for b in range(blocks):
            sel_ref[b] = sums[rest_count, b * part : (b + 1) * part, :]


def body(
    acts,
    grad_out,
    selected,
    owner,
    sel_weight,
    sel_moment,
    sel_second,
    off_weight,
    off_moment,
    off_second,
):
    group_size = lax.axis_size(DP)
    tokens_here, rows_all = acts.shape
    cols_here = grad_out.shape[1]
    rest_count = cols_here // TILE - 1
    row_block = rows_all // group_size
    part = row_block // group_size
    capacity = off_weight.shape[2]
    owner_row = owner[0, :, 0]

    strided = acts.T.reshape(group_size, group_size, part, tokens_here)
    strided = jnp.swapaxes(strided, 0, 1).reshape(group_size, row_block, tokens_here)
    acts_rows = lax.all_to_all(strided, DP, split_axis=0, concat_axis=0, tiled=True)
    grads = lax.all_gather(grad_out, DP, axis=0, tiled=True)

    gram = lax.dot_general(acts, acts, (((1,), (1,)), ((), ())), preferred_element_type=jnp.float32)
    grad_wide = grad_out.astype(jnp.float32)
    squares = jnp.sum(grad_wide * jnp.dot(gram, grad_wide, precision=lax.Precision.HIGHEST), axis=0)
    copies = jnp.broadcast_to(squares, (group_size, 1, cols_here))
    squares = lax.all_to_all(copies, DP, split_axis=0, concat_axis=0, tiled=True)
    column_norm = jnp.sqrt(squares.sum(axis=(0, 1)))

    target = owner_row * capacity + slot_numbers(owner_row)
    per_step = 4
    steps = group_size // per_step
    slots, sel_part = pl.pallas_call(
        lambda *refs: replica_sums(*refs, per_step=per_step),
        grid=(steps,),
        in_specs=[
            pl.BlockSpec(memory_space=pltpu.SMEM),
            pl.BlockSpec(memory_space=pltpu.SMEM),
            pl.BlockSpec((per_step, row_block, tokens_here), lambda i: (i, 0, 0)),
            pl.BlockSpec((per_step * tokens_here, cols_here), lambda i: (i, 0)),
        ],
        out_specs=[
            pl.BlockSpec((group_size * capacity, part, TILE), lambda i: (0, 0, 0)),
            pl.BlockSpec((group_size, part, TILE), lambda i: (0, 0, 0)),
        ],
        out_shape=[
            jax.ShapeDtypeStruct((group_size * capacity, part, TILE), jnp.bfloat16),
            jax.ShapeDtypeStruct((group_size, part, TILE), jnp.float32),
        ],
        scratch_shapes=[
            pltpu.VMEM((rest_count + 1, row_block, TILE), jnp.float32),
            pltpu.VMEM((group_size * capacity, part, TILE), jnp.float32),
        ],
        cost_estimate=pl.CostEstimate(
            flops=2 * group_size * tokens_here * row_block * cols_here,
            bytes_accessed=2 * group_size * tokens_here * (row_block + cols_here),
            transcendentals=0,
        ),
        name="replica_sums",
    )(selected[0], target, acts_rows, grads)

    received = lax.all_to_all(
        slots.reshape(group_size, capacity, part, TILE), DP, split_axis=0, concat_axis=0, tiled=True
    )
    sel_sum = lax.all_to_all(sel_part, DP, split_axis=0, concat_axis=0, tiled=True)
    new_sel = adam_update(sel_weight, sel_moment, sel_second, sel_sum.reshape(row_block, TILE))
    offload = jnp.swapaxes(received, 0, 1).reshape(off_weight.shape).astype(jnp.float32)
    new_off = adam_update(off_weight, off_moment, off_second, offload)
    return (column_norm, new_sel[0], new_sel[1], new_sel[2], new_off[0], new_off[1], new_off[2])


def solution(mesh):
    torus = Mesh(mesh.devices.reshape(4, 8, mesh.shape["tensor"]), ("dp_0", "dp_1", "tensor"))
    in_specs = (
        P(DP, None),
        P(DP, "tensor"),
        P("tensor", None),
        P("tensor", None, None),
        P(DP, "tensor"),
        P(DP, "tensor"),
        P(DP, "tensor"),
        P(DP, "tensor", None, None, None),
        P(DP, "tensor", None, None, None),
        P(DP, "tensor", None, None, None),
    )
    out_specs = (
        P("tensor"),
        P(DP, "tensor"),
        P(DP, "tensor"),
        P(DP, "tensor"),
        P(DP, "tensor", None, None, None),
        P(DP, "tensor", None, None, None),
        P(DP, "tensor", None, None, None),
    )
    return jax.shard_map(body, mesh=torus, in_specs=in_specs, out_specs=out_specs, check_vma=False)
```

time: 316 us -> 168 us (0.53)
  the two profiles are of different devices: /device:TPU:412 before, /device:TPU:8 now
where the time goes in v1:
time: 168 us; the launch traced here: 167 us
  waiting for transfers between devices  96.6 us (58%)
  starting transfers between devices  20.5 us (12%)
  blocking collectives  15.9 us (9%)
  between operations  14.9 us (9%)
  Pallas kernels  8.4 us (5%)
  local copies, waits for them, and re-layouts  4.75 us (3%)
  other arithmetic  3.84 us (2%)
  matrix products  2.37 us (1%)
    all_gather x1, waiting for transfers between devices, body(): grads = lax.all_gather(grad_out, DP, axis=0, tiled=True)  56.8 us
    all_to_all x1, waiting for transfers between devices, body(): lax.all_to_all(strided, DP, split_axis=0, concat_axis=0, tiled=True)  29 us
    all_to_all x1, blocking collectives, body(): lax.all_to_all(sel_part, DP, split_axis=0, concat_axis=0, tiled=True)  15.9 us
    all_to_all x1, starting transfers between devices, body(): lax.all_to_all(strided, DP, split_axis=0, concat_axis=0, tiled=True)  10.3 us
    all_to_all x1, waiting for transfers between devices, body(): lax.all_to_all(slots.reshape(group_size, capacity, part, TILE), DP, split...  10.1 us
    pallas_call x1, Pallas kernels, body(): pl.pallas_call(lambda *refs: replica_sums(*refs, per_step=per_step), grid...  8.4 us
    all_to_all x1, starting transfers between devices, body(): lax.all_to_all(copies, DP, split_axis=0, concat_axis=0, tiled=True)  5.55 us
    all_to_all x1, starting transfers between devices, body(): lax.all_to_all(slots.reshape(group_size, capacity, part, TILE), DP, split...  4.67 us
  transfers between devices with their start and end apart: 4, of which 3 were waited for; matrix products, arithmetic and copies ran while one was open for 6% of the time, Pallas kernels for 5%

profile of v1, /device:TPU:8, one launch (start us, length us, event | category | flops | bytes accessed | tf_op | source)
XLA Modules:
  0.0 167.3 jit_solution(10067598978109031895)
XLA Ops:
  7.2 0.0 copy-start.8
  7.2 0.0 all-gather.2.cloned.1.call-start
  7.2 0.7 all-gather.2.cloned.1.call-update
  7.9 1.6 copy.26
  9.5 1.6 copy.27
  11.1 10.3 %all-to-all-start.1 = ((bf16[32,128,128]{2,1,0:T(8,128)(2,1)}), bf16[32,128,128]{2,1,0:T(8,128)(2,1)S(1)}, u32[]{:S(2)}, u32[]{:S(2)}) async-start(bf16[32,128,128]{2,1,0:T(8,128)(2,1)} %bitcast.5), calls=%async_computation.1 | async-start | bytes 2097152 | tf_op jit(solution)/shard_map/all_to_all | solution.py:99
  21.4 0.0 copy-start.3
  22.2 0.9 convert_reduce_fusion
  23.2 2.0 %fusion.6 = f32[128,128]{1,0:T(8,128)S(1)} fusion(bf16[128,4096]{1,0:T(8,128)(2,1)} %param.10), kind=kOutput, calls=%fused_computation.15 | convolution fusion | flops 134217728 | bytes 1114112 | tf_op jit(solution)/shard_map/dot_general | solution.py:102
  25.2 0.4 fusion
  25.6 29.0 %all-to-all-done.1.refs_2_ = bf16[32,128,128]{2,1,0:T(8,128)(2,1)S(1)} async-done(((bf16[32,128,128]{2,1,0:T(8,128)(2,1)}), bf16[32,128,128]{2,1,0:T(8,128)(2,1)S(1)}, u32[]{:S(2)}, u32[]{:S(2)}) %all-to-all-start.1) | async-done | bytes 1048608 | tf_op jit(solution)/shard_map/all_to_all | solution.py:99
  54.6 0.8 broadcast_in_dim.2
  55.4 5.5 %all-to-all-start = ((f32[32,1,896]{2,1,0:T(1,128)}), f32[32,1,896]{2,1,0:T(1,128)S(1)}, u32[]{:S(2)}, u32[]{:S(2)}) async-start(f32[32,1,896]{2,1,0:T(1,128)} %broadcast_in_dim.2), calls=%async_computation | async-start | bytes 229376 | tf_op jit(solution)/shard_map/all_to_all | solution.py:106
  61.0 0.6 multiply_add_fusion.2.refs_1_
  61.5 56.8 %all-gather.2.cloned.1.call-done.refs_3_ = bf16[4096,896]{1,0:T(8,128)(2,1)} async-done(((bf16[128,896]{1,0:T(8,128)(2,1)}), bf16[4096,896]{1,0:T(8,128)(2,1)}) %all-gather.2.cloned.1.call-update) | async-done | bytes 7340048 | tf_op jit(solution)/shard_map/all_gather | solution.py:100
  118.3 8.4 %replica_sums.1 = (bf16[288,4,128]{2,1,0:T(4,128)(2,1)}, f32[32,4,128]{2,1,0:T(4,128)}) custom-call(s32[1]{0:T(128)} %bitcast.17.refs_0_, s32[192]{0:T(256)} %multiply_add_fusion.2.refs_1_, bf16[32,128,128]{2,1,0:T(8,128)(2,1)} %copy-done, bf16[4096,896]{1,0:T(8,128)(2,1)} %all-gather.2.cloned.1.call-done.refs_3_), custom_call_target="tpu_custom_call" | custom-call | flops 939524096 | bytes 8388608 | tf_op jit(solution)/shard_map/replica_sums/pallas_call | solution.py:112
  126.7 15.9 %all_to_all.20 = f32[32,4,128]{2,1,0:T(4,128)S(1)} all-to-all(f32[32,4,128]{2,1,0:T(4,128)} %get-tuple-element.9), channel_id=1, replica_groups=mesh['dp_0'=4,'dp_1'=8,'tensor'=16] {'dp_0','dp_1'}, dimensions={0} | all-to-all | bytes 131072 | tf_op jit(solution)/shard_map/all_to_all | solution.py:144
  142.6 4.7 %all-to-all-start.3 = ((bf16[32,9,4,128]{3,2,1,0:T(4,128)(2,1)}), bf16[32,9,4,128]{3,2,1,0:T(4,128)(2,1)S(1)}, u32[]{:S(2)}, u32[]{:S(2)}) async-start(bf16[32,9,4,128]{3,2,1,0:T(4,128)(2,1)} %bitcast.20), calls=%async_computation.3 | async-start | bytes 589824 | tf_op jit(solution)/shard_map/all_to_all | solution.py:141
  147.3 0.1 reduce_sum.28
  147.4 0.6 sqrt.9
  148.0 0.7 multiply_subtract_fusion.1
  148.7 10.1 %all-to-all-done.3 = bf16[32,9,4,128]{3,2,1,0:T(4,128)(2,1)S(1)} async-done(((bf16[32,9,4,128]{3,2,1,0:T(4,128)(2,1)}), bf16[32,9,4,128]{3,2,1,0:T(4,128)(2,1)S(1)}, u32[]{:S(2)}, u32[]{:S(2)}) %all-to-all-start.3) | async-done | bytes 294944 | tf_op jit(solution)/shard_map/all_to_all | solution.py:141
  158.8 0.1 copy.28
  159.0 1.5 multiply_subtract_fusion
  (18 shorter events, 0.1 us)
Async XLA Ops:
  7.2 18.0 %copy-start.4 = (bf16[128,896]{1,0:T(8,128)(2,1)S(1)}, bf16[128,896]{1,0:T(8,128)(2,1)}, u32[]{:S(2)}) copy-start(bf16[128,896]{1,0:T(8,128)(2,1)} %param.11) | copy-start | bytes 688132
  7.2 53.8 %copy-start.8 = (s32[1,192,1]{1,2,0:T(1,128)S(1)}, s32[1,192,1]{1,2,0:T(1,128)}, u32[]{:S(2)}) copy-start(s32[1,192,1]{1,2,0:T(1,128)} %param.13) | copy-start | bytes 2308
  7.2 111.1 %all-gather.2.cloned.1.call-start = ((), (), s32[]{:S(2)}) async-start(), calls=%async_computation.4 | async-start | bytes 7569408 | tf_op jit(solution)/shard_map/all_gather | solution.py:100
  11.1 136.9 %copy-start.5 = (f32[128,128]{1,0:T(8,128)S(1)}, f32[128,128]{1,0:T(8,128)}, u32[]{:S(2)}) copy-start(f32[128,128]{1,0:T(8,128)} %param.14) | copy-start | bytes 196612
  11.1 136.9 %copy-start.6 = (f32[128,128]{1,0:T(8,128)S(1)}, f32[128,128]{1,0:T(8,128)}, u32[]{:S(2)}) copy-start(f32[128,128]{1,0:T(8,128)} %param.15) | copy-start | bytes 196612
  11.1 136.9 %copy-start.7 = (f32[128,128]{1,0:T(8,128)S(1)}, f32[128,128]{1,0:T(8,128)}, u32[]{:S(2)}) copy-start(f32[128,128]{1,0:T(8,128)} %param.16) | copy-start | bytes 196612
  11.1 43.5 %all-to-all-start.1 = ((bf16[32,128,128]{2,1,0:T(8,128)(2,1)}), bf16[32,128,128]{2,1,0:T(8,128)(2,1)S(1)}, u32[]{:S(2)}, u32[]{:S(2)}) async-start(bf16[32,128,128]{2,1,0:T(8,128)(2,1)} %bitcast.5), calls=%async_computation.1 | async-start | bytes 2097152 | tf_op jit(solution)/shard_map/all_to_all | solution.py:99
  21.4 137.5 %copy-start.1 = (f32[1,1,9,128,128]{4,3,2,1,0:T(8,128)S(1)}, f32[1,1,9,128,128]{4,3,2,1,0:T(8,128)}, u32[]{:S(2)}) copy-start(f32[1,1,9,128,128]{4,3,2,1,0:T(8,128)} %param.17) | copy-start | bytes 1769476
  21.4 137.5 %copy-start.2 = (f32[1,1,9,128,128]{4,3,2,1,0:T(8,128)S(1)}, f32[1,1,9,128,128]{4,3,2,1,0:T(8,128)}, u32[]{:S(2)}) copy-start(f32[1,1,9,128,128]{4,3,2,1,0:T(8,128)} %param.18) | copy-start | bytes 1769476
  21.4 137.5 %copy-start.3 = (f32[1,1,9,128,128]{4,3,2,1,0:T(8,128)S(1)}, f32[1,1,9,128,128]{4,3,2,1,0:T(8,128)}, u32[]{:S(2)}) copy-start(f32[1,1,9,128,128]{4,3,2,1,0:T(8,128)} %param.19) | copy-start | bytes 1769476
  54.6 63.7 %copy-start = (bf16[32,128,128]{2,1,0:T(8,128)(2,1)}, bf16[32,128,128]{2,1,0:T(8,128)(2,1)S(1)}, u32[]{:S(2)}) copy-start(bf16[32,128,128]{2,1,0:T(8,128)(2,1)S(1)} %all-to-all-done.1.refs_2_) | copy-start | bytes 3145732
  55.4 71.3 %all-to-all-start = ((f32[32,1,896]{2,1,0:T(1,128)}), f32[32,1,896]{2,1,0:T(1,128)S(1)}, u32[]{:S(2)}, u32[]{:S(2)}) async-start(f32[32,1,896]{2,1,0:T(1,128)} %broadcast_in_dim.2), calls=%async_computation | async-start | bytes 229376 | tf_op jit(solution)/shard_map/all_to_all | solution.py:106
  142.6 16.2 %all-to-all-start.3 = ((bf16[32,9,4,128]{3,2,1,0:T(4,128)(2,1)}), bf16[32,9,4,128]{3,2,1,0:T(4,128)(2,1)S(1)}, u32[]{:S(2)}, u32[]{:S(2)}) async-start(bf16[32,9,4,128]{3,2,1,0:T(4,128)(2,1)} %bitcast.20), calls=%async_computation.3 | async-start | bytes 589824 | tf_op jit(solution)/shard_map/all_to_all | solution.py:141
Sparse Core Ops, SparseCore 0:
  11.2 107.0 all-gather.1

commit v2 on v0

v2 whole, which is shorter than its diff:
```python
import jax
import jax.numpy as jnp
from jax import lax
from jax.experimental import pallas as pl
from jax.experimental.pallas import tpu as pltpu
from jax.sharding import Mesh
from jax.sharding import PartitionSpec as P

TILE = 128
EARLY_TILES = 3
DP = ("dp_0", "dp_1")


beta_one = 0.9
beta_two = 0.95
adam_eps = 1e-08
learn_rate = 0.01
decay_rate = 0.1
step_count = 10.0


def adam_update(weight, moment, second, grad):
    moment_new = beta_one * moment + (1.0 - beta_one) * grad
    second_new = beta_two * second + (1.0 - beta_two) * grad * grad
    first_fix = 1.0 - beta_one**step_count
    second_fix = 1.0 - beta_two**step_count
    update = moment_new / first_fix / (jnp.sqrt(second_new / second_fix) + adam_eps)
    return (weight - learn_rate * (update + decay_rate * weight), moment_new, second_new)


def slot_numbers(owner_row):
    places = jnp.arange(owner_row.shape[0], dtype=jnp.int32)
    earlier = (owner_row[:, None] == owner_row[None, :]) & (places[:, None] > places[None, :])
    return jnp.sum(earlier.astype(jnp.int32), axis=1)


def split_three(value):
    high = value.astype(jnp.bfloat16).astype(jnp.float32)
    rest = value - high
    middle = rest.astype(jnp.bfloat16).astype(jnp.float32)
    return high, middle, (rest - middle).astype(jnp.bfloat16).astype(jnp.float32)


def add_replicas(order_ref, selected, mine_ref, other_ref, grads_ref, start, first_tile, sums_ref):
    tokens = mine_ref.shape[2]
    replicas, width = grads_ref.shape[0] // tokens, grads_ref.shape[1]
    unroll = 4
    for low in range(0, width, 2 * TILE):
        wide = min(2 * TILE, width - low)

        def step(j, totals, low=low, wide=wide):
            for u in range(unroll):
                at = j * unroll + u
                source = order_ref[start + at]
                rows = jnp.concatenate([mine_ref[source], other_ref[source]], axis=0)
                place = pl.ds(pl.multiple_of(at * tokens, tokens), tokens)
                partial = jnp.dot(
                    rows, grads_ref[place, low : low + wide], preferred_element_type=jnp.float32
                )
                added = []
                for n, total in enumerate(totals):
                    tile = first_tile + low // TILE + n
                    whole = partial[:, n * TILE : (n + 1) * TILE]
                    rounded = whole.astype(jnp.bfloat16).astype(jnp.float32)
                    added.append(total + jnp.where(selected == tile, whole, rounded))
                totals = tuple(added)
            return totals

        at_tile = low // TILE
        totals = tuple(sums_ref[at_tile + n] for n in range(wide // TILE))
        totals = lax.fori_loop(0, replicas // unroll, step, totals)
        for n, total in enumerate(totals):
            sums_ref[at_tile + n] = total


def chunk_kernel(scalars_ref, mine_ref, other_ref, *refs, starts, first_tile, fresh):
    grads_refs, sums_ref = refs[: len(starts)], refs[-1]
    if fresh:
        sums_ref[...] = jnp.zeros_like(sums_ref)
    else:
        sums_ref[...] = refs[len(starts)][...]
    for grads_ref, start in zip(grads_refs, starts):
        add_replicas(
            scalars_ref, scalars_ref[0], mine_ref, other_ref, grads_ref, start, first_tile, sums_ref
        )


def place_kernel(
    scalars_ref, target_ref, mine_ref, other_ref, *refs, starts, first_tile, owners, slots
):
    grads_refs = refs[: len(starts)]
    early_ref, late_ref, slots_ref, sums, places = refs[len(starts) :]
    selected, flip = scalars_ref[0], scalars_ref[1]
    sums[...] = late_ref[...]
    for grads_ref, start in zip(grads_refs, starts):
        add_replicas(
            scalars_ref, selected, mine_ref, other_ref, grads_ref, start, first_tile, sums
        )
    places[...] = jnp.zeros_like(places)
    part = slots_ref.shape[1]
    for tile in range(first_tile + sums.shape[0]):
        held, at = (early_ref, tile) if tile < first_tile else (sums, tile - first_tile)
        rest = tile - (tile > selected).astype(jnp.int32)

        @pl.when(tile != selected)
        def _(held=held, at=at, rest=rest):
            for q in range(owners):
                places[target_ref[rest * owners + q]] = held[at, q * part : (q + 1) * part, :]

        @pl.when(tile == selected)
        def _(held=held, at=at):
            for q in range(owners):
                owner = jnp.bitwise_xor(q, flip * (owners // 2))
                for n, term in enumerate(split_three(held[at, q * part : (q + 1) * part, :])):
                    places[owner * slots + slots - 3 + n] = term

    slots_ref[...] = places[...].astype(slots_ref.dtype)


def shift(array, axis, by):
    size = lax.axis_size(axis)
    return lax.ppermute(array, axis, [(i, (i + by) % size) for i in range(size)])


def body(
    acts,
    grad_out,
    selected,
    owner,
    sel_weight,
    sel_moment,
    sel_second,
    off_weight,
    off_moment,
    off_second,
):
    group_size = lax.axis_size(DP)
    size_x, size_y = lax.axis_size(DP[0]), lax.axis_size(DP[1])
    at_x, at_y = lax.axis_index(DP[0]), lax.axis_index(DP[1])
    core = lax.rem(lax.axis_index("tensor"), 2)
    tokens_here, rows_all = acts.shape
    cols_here = grad_out.shape[1]
    tiles_here = cols_here // TILE
    early_tiles = EARLY_TILES
    row_block = rows_all // group_size
    part = row_block // group_size
    capacity = off_weight.shape[2]
    slots = capacity + 3
    owner_row = owner[0, :, 0]

    early = lax.all_gather(grad_out[:, : early_tiles * TILE], DP, axis=0, tiled=True)
    late = grad_out[:, early_tiles * TILE :]
    column = jnp.concatenate([late] + [shift(late, DP[1], k) for k in range(1, size_y)], axis=0)
    half = column.shape[0] // 2
    from_left = shift(column, DP[0], 1)
    from_right = shift(column, DP[0], -1)
    far_low = shift(from_left[:half], DP[0], 1)
    far_high = shift(from_right[half:], DP[0], -1)

    half_rows = lax.dynamic_slice_in_dim(acts, core * (rows_all // 2), rows_all // 2, axis=1)
    strided = half_rows.T.reshape(group_size // 2, group_size, part, tokens_here)
    strided = jnp.swapaxes(strided, 0, 1).reshape(group_size, row_block // 2, tokens_here)
    mine = lax.all_to_all(strided, DP, split_axis=0, concat_axis=0, tiled=True)
    other = lax.ppermute(mine, "tensor", [(i, i ^ 1) for i in range(lax.axis_size("tensor"))])

    gram = lax.dot_general(acts, acts, (((1,), (1,)), ((), ())), preferred_element_type=jnp.float32)
    grad_wide = grad_out.astype(jnp.float32)
    squares = jnp.sum(grad_wide * jnp.dot(gram, grad_wide, precision=lax.Precision.HIGHEST), axis=0)
    copies = jnp.broadcast_to(squares, (group_size, 1, cols_here))
    squares = lax.all_to_all(copies, DP, split_axis=0, concat_axis=0, tiled=True)
    column_norm = jnp.sqrt(squares.sum(axis=(0, 1)))

    target = owner_row * slots + slot_numbers(owner_row)
    target = target.reshape(tiles_here - 1, 2, group_size // 2)
    target = jnp.where(core == 0, target, target[:, ::-1]).reshape(-1)
    ys = lax.rem(at_y - jnp.arange(size_y, dtype=jnp.int32) + size_y, size_y)
    xs = [lax.rem(at_x + step + size_x, size_x) for step in (0, -1, 1, 2)]
    order = [jnp.arange(group_size, dtype=jnp.int32)] + [x * size_y + ys for x in xs]
    scalars = jnp.concatenate([jnp.stack([selected[0, 0], core]).astype(jnp.int32)] + order)
    whole = pl.BlockSpec(memory_space=pltpu.VMEM)
    small = pl.BlockSpec(memory_space=pltpu.SMEM)

    def cost(replicas, width):
        return pl.CostEstimate(
            flops=2 * replicas * tokens_here * row_block * width,
            bytes_accessed=2 * replicas * tokens_here * (row_block + width),
            transcendentals=0,
        )

    def chunk(name, grads, start, first_tile, sums=None):
        replicas, width = grads.shape[0] // tokens_here, grads.shape[1]
        extra = [] if sums is None else [sums]
        return pl.pallas_call(
            lambda *refs: chunk_kernel(
                *refs, starts=[start], first_tile=first_tile, fresh=sums is None
            ),
            in_specs=[small] + [whole] * (3 + len(extra)),
            out_specs=whole,
            out_shape=jax.ShapeDtypeStruct((width // TILE, row_block, TILE), jnp.float32),
            cost_estimate=cost(replicas, width),
            compiler_params=pltpu.CompilerParams(vmem_limit_bytes=24 << 20),
            name=name,
        )(scalars, mine, other, grads, *extra)

    early_sums = chunk("early_columns", early, 2, 0)
    base = 2 + group_size
    late_sums = chunk("own_x", column, base, early_tiles)
    late_sums = chunk("left_x", from_left, base + size_y, early_tiles, late_sums)
    late_sums = chunk("right_x", from_right, base + 2 * size_y, early_tiles, late_sums)
    late_tiles = tiles_here - early_tiles
    starts = [base + 3 * size_y, base + 3 * size_y + size_y // 2]
    outgoing = pl.pallas_call(
        lambda *refs: place_kernel(
            *refs, starts=starts, first_tile=early_tiles, owners=group_size, slots=slots
        ),
        in_specs=[small] * 2 + [whole] * 6,
        out_specs=whole,
        out_shape=jax.ShapeDtypeStruct((group_size * slots, part, TILE), jnp.bfloat16),
        scratch_shapes=[
            pltpu.VMEM((late_tiles, row_block, TILE), jnp.float32),
            pltpu.VMEM((group_size * slots, part, TILE), jnp.float32),
        ],
        cost_estimate=cost(size_y, late_tiles * TILE),
        compiler_params=pltpu.CompilerParams(vmem_limit_bytes=24 << 20),
        name="far_x_and_slots",
    )(scalars, target, mine, other, far_low, far_high, early_sums, late_sums)

    received = lax.all_to_all(
        outgoing.reshape(group_size, slots, part, TILE), DP, split_axis=0, concat_axis=0, tiled=True
    ).astype(jnp.float32)
    sel_sum = received[:, capacity] + received[:, capacity + 1] + received[:, capacity + 2]
    new_sel = adam_update(sel_weight, sel_moment, sel_second, sel_sum.reshape(row_block, TILE))
    offload = jnp.swapaxes(received[:, :capacity], 0, 1).reshape(off_weight.shape)
    new_off = adam_update(off_weight, off_moment, off_second, offload)
    return (column_norm, new_sel[0], new_sel[1], new_sel[2], new_off[0], new_off[1], new_off[2])


def solution(mesh):
    torus = Mesh(mesh.devices.reshape(4, 8, mesh.shape["tensor"]), ("dp_0", "dp_1", "tensor"))
    in_specs = (
        P(DP, None),
        P(DP, "tensor"),
        P("tensor", None),
        P("tensor", None, None),
        P(DP, "tensor"),
        P(DP, "tensor"),
        P(DP, "tensor"),
        P(DP, "tensor", None, None, None),
        P(DP, "tensor", None, None, None),
        P(DP, "tensor", None, None, None),
    )
    out_specs = (
        P("tensor"),
        P(DP, "tensor"),
        P(DP, "tensor"),
        P(DP, "tensor"),
        P(DP, "tensor", None, None, None),
        P(DP, "tensor", None, None, None),
        P(DP, "tensor", None, None, None),
    )
    return jax.shard_map(body, mesh=torus, in_specs=in_specs, out_specs=out_specs, check_vma=False)
```

time: 316 us -> 170 us (0.54)
  the two profiles are of different devices: /device:TPU:412 before, /device:TPU:72 now
where the time goes in v2:
time: 170 us; the launch traced here: 169 us
  starting transfers between devices  73.9 us (43%)
  waiting for transfers between devices  47.7 us (28%)
  local copies, waits for them, and re-layouts  15.7 us (9%)
  between operations  15.1 us (9%)
  Pallas kernels  12.5 us (7%)
  other arithmetic  3.52 us (2%)
    ppermute x11, starting transfers between devices, shift(): lax.ppermute(array, axis, [(i, (i + by) % size) for i in range(size)])  41 us
    ppermute x11, waiting for transfers between devices, shift(): lax.ppermute(array, axis, [(i, (i + by) % size) for i in range(size)])  34.1 us
    all_to_all x1, starting transfers between devices, body(): lax.all_to_all(outgoing.reshape(group_size, slots, part, TILE), DP, split...  14.3 us
    all_to_all x1, waiting for transfers between devices, body(): lax.all_to_all(outgoing.reshape(group_size, slots, part, TILE), DP, split...  13.6 us
    all_to_all x1, starting transfers between devices, body(): lax.all_to_all(copies, DP, split_axis=0, concat_axis=0, tiled=True)  9.99 us
    pallas_call x4, Pallas kernels, chunk(): pl.pallas_call(lambda *refs: chunk_kernel(*refs, starts=[start], first_ti...  9.6 us
    all_to_all x1, starting transfers between devices, body(): mine = lax.all_to_all(strided, DP, split_axis=0, concat_axis=0, tiled=True)  6.59 us
    unnamed x21, local copies, waits for them, and re-layouts  6.15 us
  transfers between devices with their start and end apart: 16, of which 3 were waited for; matrix products, arithmetic and copies ran while one was open for 8% of the time, Pallas kernels for 7%

profile of v2, /device:TPU:72, one launch (start us, length us, event | category | flops | bytes accessed | tf_op | source)
XLA Modules:
  0.0 169.2 jit_solution(7743725290158233664)
XLA Ops:
  10.4 2.5 %collective-permute-start.7 = (bf16[128,512]{1,0:T(8,128)(2,1)S(1)}, bf16[128,512]{1,0:T(8,128)(2,1)S(1)}, u32[]{:S(2)}, u32[]{:S(2)}) collective-permute-start(bf16[128,512]{1,0:T(8,128)(2,1)S(1)} %get-tuple-element.13), channel_id=1, source_target_pairs={{0,112},{16,0},{32,16},{48,32},{64,48},{80,64},{96,80},{112,96},{1... | collective-permute-start | bytes 393224 | tf_op jit(solution)/shard_map/ppermute | solution.py:122
  12.9 6.2 %collective-permute-start.6 = (bf16[128,512]{1,0:T(8,128)(2,1)S(1)}, bf16[128,512]{1,0:T(8,128)(2,1)S(1)}, u32[]{:S(2)}, u32[]{:S(2)}) collective-permute-start(bf16[128,512]{1,0:T(8,128)(2,1)S(1)} %get-tuple-element.13), channel_id=1, source_target_pairs={{0,96},{16,112},{32,0},{48,16},{64,32},{80,48},{96,64},{112,80},{1... | collective-permute-start | bytes 393224 | tf_op jit(solution)/shard_map/ppermute | solution.py:122
  19.1 3.9 %collective-permute-start.5 = (bf16[128,512]{1,0:T(8,128)(2,1)S(1)}, bf16[128,512]{1,0:T(8,128)(2,1)S(1)}, u32[]{:S(2)}, u32[]{:S(2)}) collective-permute-start(bf16[128,512]{1,0:T(8,128)(2,1)S(1)} %get-tuple-element.13), channel_id=1, source_target_pairs={{0,80},{16,96},{32,112},{48,0},{64,16},{80,32},{96,48},{112,64},{1... | collective-permute-start | bytes 393224 | tf_op jit(solution)/shard_map/ppermute | solution.py:122
  23.0 3.6 %collective-permute-start.2 = (bf16[128,512]{1,0:T(8,128)(2,1)S(1)}, bf16[128,512]{1,0:T(8,128)(2,1)S(1)}, u32[]{:S(2)}, u32[]{:S(2)}) collective-permute-start(bf16[128,512]{1,0:T(8,128)(2,1)S(1)} %get-tuple-element.13), channel_id=1, source_target_pairs={{0,32},{16,48},{32,64},{48,80},{64,96},{80,112},{96,0},{112,16},{1... | collective-permute-start | bytes 393224 | tf_op jit(solution)/shard_map/ppermute | solution.py:122
  26.6 3.8 %collective-permute-start.1 = (bf16[128,512]{1,0:T(8,128)(2,1)S(1)}, bf16[128,512]{1,0:T(8,128)(2,1)S(1)}, u32[]{:S(2)}, u32[]{:S(2)}) collective-permute-start(bf16[128,512]{1,0:T(8,128)(2,1)S(1)} %get-tuple-element.13), channel_id=1, source_target_pairs={{0,16},{16,32},{32,48},{48,64},{64,80},{80,96},{96,112},{112,0},{1... | collective-permute-start | bytes 393224 | tf_op jit(solution)/shard_map/ppermute | solution.py:122
  31.9 6.6 %all-to-all-start.1 = ((bf16[32,64,128]{2,1,0:T(8,128)(2,1)}), bf16[32,64,128]{2,1,0:T(8,128)(2,1)S(1)}, u32[]{:S(2)}, u32[]{:S(2)}) async-start(bf16[32,64,128]{2,1,0:T(8,128)(2,1)} %bitcast.6), calls=%async_computation.1 | async-start | bytes 1048576 | tf_op jit(solution)/shard_map/all_to_all | solution.py:163
  38.5 6.4 %collective-permute-start.3 = (bf16[128,512]{1,0:T(8,128)(2,1)S(1)}, bf16[128,512]{1,0:T(8,128)(2,1)S(1)}, u32[]{:S(2)}, u32[]{:S(2)}) collective-permute-start(bf16[128,512]{1,0:T(8,128)(2,1)S(1)} %get-tuple-element.13), channel_id=1, source_target_pairs={{0,48},{16,64},{32,80},{48,96},{64,112},{80,0},{96,16},{112,32},{1... | collective-permute-start | bytes 393224 | tf_op jit(solution)/shard_map/ppermute | solution.py:122
  45.6 2.1 %collective-permute-start.4 = (bf16[128,512]{1,0:T(8,128)(2,1)S(1)}, bf16[128,512]{1,0:T(8,128)(2,1)S(1)}, u32[]{:S(2)}, u32[]{:S(2)}) collective-permute-start(bf16[128,512]{1,0:T(8,128)(2,1)S(1)} %get-tuple-element.13), channel_id=1, source_target_pairs={{0,64},{16,80},{32,96},{48,112},{64,0},{80,16},{96,32},{112,48},{1... | collective-permute-start | bytes 393224 | tf_op jit(solution)/shard_map/ppermute | solution.py:122
  48.3 16.7 %collective-permute-done.3 = bf16[128,512]{1,0:T(8,128)(2,1)S(1)} collective-permute-done((bf16[128,512]{1,0:T(8,128)(2,1)S(1)}, bf16[128,512]{1,0:T(8,128)(2,1)S(1)}, u32[]{:S(2)}, u32[]{:S(2)}) %collective-permute-start.3) | collective-permute-done | bytes 131104 | tf_op jit(solution)/shard_map/ppermute | solution.py:122
  68.3 4.8 %collective-permute-start.10 = (bf16[1024,512]{1,0:T(8,128)(2,1)}, bf16[1024,512]{1,0:T(8,128)(2,1)S(1)}, u32[]{:S(2)}, u32[]{:S(2)}) collective-permute-start(bf16[1024,512]{1,0:T(8,128)(2,1)} %constant_dynamic-update-slice_fusion.refs_3_), channel_id=1, source_target_pairs={{0,384},{128,0},{256,128},{384,256},{1,385},{129,1},{257,129},{385... | collective-permute-start | bytes 3145736 | tf_op jit(solution)/shard_map/ppermute | solution.py:122
  73.1 1.9 %collective-permute-start.8 = (bf16[1024,512]{1,0:T(8,128)(2,1)}, bf16[1024,512]{1,0:T(8,128)(2,1)}, u32[]{:S(2)}, u32[]{:S(2)}) collective-permute-start(bf16[1024,512]{1,0:T(8,128)(2,1)} %constant_dynamic-update-slice_fusion.refs_3_), channel_id=1, source_target_pairs={{0,128},{128,256},{256,384},{384,0},{1,129},{129,257},{257,385},{3... | collective-permute-start | bytes 3145736 | tf_op jit(solution)/shard_map/ppermute | solution.py:122
  76.7 10.0 %all-to-all-start = ((f32[32,1,896]{2,1,0:T(1,128)}), f32[32,1,896]{2,1,0:T(1,128)S(1)}, u32[]{:S(2)}, u32[]{:S(2)}) async-start(f32[32,1,896]{2,1,0:T(1,128)} %broadcast_in_dim.2), calls=%async_computation | async-start | bytes 229376 | tf_op jit(solution)/shard_map/all_to_all | solution.py:170
  86.7 1.9 %collective-permute-start = (bf16[32,64,128]{2,1,0:T(8,128)(2,1)S(1)}, bf16[32,64,128]{2,1,0:T(8,128)(2,1)S(1)}, u32[]{:S(2)}, u32[]{:S(2)}) collective-permute-start(bf16[32,64,128]{2,1,0:T(8,128)(2,1)S(1)} %all-to-all-done.1.refs_1_.refs_2_), channel_id=1, source_target_pairs={{0,1},{1,0},{2,3},{3,2},{4,5},{5,4},{6,7},{7,6},{8,9},{9,8},{10,11... | collective-permute-start | bytes 1572872 | tf_op jit(solution)/shard_map/ppermute | solution.py:164
  88.9 17.5 %collective-permute-done.10.refs_3_ = bf16[1024,512]{1,0:T(8,128)(2,1)S(1)} collective-permute-done((bf16[1024,512]{1,0:T(8,128)(2,1)}, bf16[1024,512]{1,0:T(8,128)(2,1)S(1)}, u32[]{:S(2)}, u32[]{:S(2)}) %collective-permute-start.10) | collective-permute-done | bytes 1048608 | tf_op jit(solution)/shard_map/ppermute | solution.py:122
  107.2 4.0 %collective-permute-start.11 = (bf16[512,512]{1,0:T(8,128)(2,1)}, bf16[512,512]{1,0:T(8,128)(2,1)}, u32[]{:S(2)}, u32[]{:S(2)}) collective-permute-start(bf16[512,512]{1,0:T(8,128)(2,1)} %slice.33), channel_id=1, source_target_pairs={{0,384},{128,0},{256,128},{384,256},{1,385},{129,1},{257,129},{385... | collective-permute-start | bytes 1572872 | tf_op jit(solution)/shard_map/ppermute | solution.py:122
  111.2 1.9 %slice.32 = bf16[512,512]{1,0:T(8,128)(2,1)} slice(bf16[1024,512]{1,0:T(8,128)(2,1)} %collective-permute-done.8.refs_3_), slice={[0:512], [0:512]} | slice | bytes 1048576 | tf_op jit(solution)/shard_map/slice | solution.py:157
  113.1 1.9 %collective-permute-start.9 = (bf16[512,512]{1,0:T(8,128)(2,1)}, bf16[512,512]{1,0:T(8,128)(2,1)}, u32[]{:S(2)}, u32[]{:S(2)}) collective-permute-start(bf16[512,512]{1,0:T(8,128)(2,1)} %slice.32), channel_id=1, source_target_pairs={{0,128},{128,256},{256,384},{384,0},{1,129},{129,257},{257,385},{3... | collective-permute-start | bytes 1572872 | tf_op jit(solution)/shard_map/ppermute | solution.py:122
  115.9 2.2 %own_x.1.refs_4_ = f32[4,128,128]{2,1,0:T(8,128)S(1)} custom-call(s32[66]{0:T(128)S(1)} %concatenate.6.refs_0_, bf16[32,64,128]{2,1,0:T(8,128)(2,1)S(1)} %all-to-all-done.1.refs_1_.refs_2_, bf16[32,64,128]{2,1,0:T(8,128)(2,1)S(1)} %collective-permute-done.refs_2_.refs_3_, bf16[1024,512]{1,0:T(8,128)(2,1)} %constant_dynamic-update-slice_fusion.refs_3_), custom_call_target="tpu_custom_call" | custom-call | flops 134217728 | bytes 1310720 | tf_op jit(solution)/shard_map/own_x/pallas_call | solution.py:193
  118.1 2.2 %left_x.1.refs_4_ = f32[4,128,128]{2,1,0:T(8,128)S(1)} custom-call(s32[66]{0:T(128)S(1)} %concatenate.6.refs_0_, bf16[32,64,128]{2,1,0:T(8,128)(2,1)S(1)} %all-to-all-done.1.refs_1_.refs_2_, bf16[32,64,128]{2,1,0:T(8,128)(2,1)S(1)} %collective-permute-done.refs_2_.refs_3_, bf16[1024,512]{1,0:T(8,128)(2,1)} %collective-permute-done.8.refs_3_, ...), custom_call_target="tpu_custom_call" | custom-call | flops 134217728 | bytes 1310720 | tf_op jit(solution)/shard_map/left_x/pallas_call | solution.py:193
  121.7 1.9 %copy-done.1 = bf16[4096,384]{1,0:T(8,128)(2,1)S(1)} copy-done((bf16[4096,384]{1,0:T(8,128)(2,1)S(1)}, bf16[4096,384]{1,0:T(8,128)(2,1)}, u32[]{:S(2)}) %copy-start.1) | copy-done | bytes 3145752
  123.6 3.8 %early_columns.1.refs_6_ = f32[3,128,128]{2,1,0:T(8,128)S(1)} custom-call(s32[66]{0:T(128)S(1)} %concatenate.6.refs_0_, bf16[32,64,128]{2,1,0:T(8,128)(2,1)S(1)} %all-to-all-done.1.refs_1_.refs_2_, bf16[32,64,128]{2,1,0:T(8,128)(2,1)S(1)} %collective-permute-done.refs_2_.refs_3_, bf16[4096,384]{1,0:T(8,128)(2,1)S(1)} %copy-done.1), custom_call_target="tpu_custom_call" | custom-call | flops 402653184 | bytes 4194304 | tf_op jit(solution)/shard_map/early_columns/pallas_call | solution.py:193
  127.5 2.9 %far_x_and_slots.1 = bf16[384,4,128]{2,1,0:T(4,128)(2,1)} custom-call(s32[66]{0:T(128)S(1)} %concatenate.6.refs_0_, s32[192]{0:T(256)S(1)} %reshape.78.refs_1_, bf16[32,64,128]{2,1,0:T(8,128)(2,1)S(1)} %all-to-all-done.1.refs_1_.refs_2_, bf16[32,64,128]{2,1,0:T(8,128)(2,1)S(1)} %collective-permute-done.refs_2_.refs_3_, ...), custom_call_target="tpu_custom_call" | custom-call | flops 134217728 | bytes 1310720 | tf_op jit(solution)/shard_map/far_x_and_slots/pallas_call | solution.py:212
  130.4 14.3 %all-to-all-start.2 = ((bf16[32,12,4,128]{3,2,1,0:T(4,128)(2,1)}), bf16[32,12,4,128]{3,2,1,0:T(4,128)(2,1)S(1)}, u32[]{:S(2)}, u32[]{:S(2)}) async-start(bf16[32,12,4,128]{3,2,1,0:T(4,128)(2,1)} %bitcast.7), calls=%async_computation.2 | async-start | bytes 786432 | tf_op jit(solution)/shard_map/all_to_all | solution.py:228
  145.4 13.6 %all-to-all-done.2 = bf16[32,12,4,128]{3,2,1,0:T(4,128)(2,1)S(1)} async-done(((bf16[32,12,4,128]{3,2,1,0:T(4,128)(2,1)}), bf16[32,12,4,128]{3,2,1,0:T(4,128)(2,1)S(1)}, u32[]{:S(2)}, u32[]{:S(2)}) %all-to-all-start.2) | async-done | bytes 393248 | tf_op jit(solution)/shard_map/all_to_all | solution.py:228
  (65 shorter events, 17.8 us)
Async XLA Ops:
  7.2 23.3 %copy-start = (bf16[128,4096]{1,0:T(8,128)(2,1)S(1)}, bf16[128,4096]{1,0:T(8,128)(2,1)}, u32[]{:S(2)}) copy-start(bf16[128,4096]{1,0:T(8,128)(2,1)} %param.10) | copy-start | bytes 3145732
  7.2 114.5 %all-gather.2.cloned.1.call-start = ((), (), s32[]{:S(2)}) async-start(), calls=%async_computation.3 | async-start | bytes 3244032 | tf_op jit(solution)/shard_map/all_gather | solution.py:151
  10.4 64.6 %copy-start.6 = (s32[1,192,1]{1,2,0:T(1,128)S(1)}, s32[1,192,1]{1,2,0:T(1,128)}, u32[]{:S(2)}) copy-start(s32[1,192,1]{1,2,0:T(1,128)} %param.13) | copy-start | bytes 2308
  10.4 57.2 %collective-permute-start.7 = (bf16[128,512]{1,0:T(8,128)(2,1)S(1)}, bf16[128,512]{1,0:T(8,128)(2,1)S(1)}, u32[]{:S(2)}, u32[]{:S(2)}) collective-permute-start(bf16[128,512]{1,0:T(8,128)(2,1)S(1)} %get-tuple-element.13), channel_id=1, source_target_pairs={{0,112},{16,0},{32,16},{48,32},{64,48},{80,64},{96,80},{112,96},{1... | collective-permute-start | bytes 393224 | tf_op jit(solution)/shard_map/ppermute | solution.py:122
  12.9 54.1 %collective-permute-start.6 = (bf16[128,512]{1,0:T(8,128)(2,1)S(1)}, bf16[128,512]{1,0:T(8,128)(2,1)S(1)}, u32[]{:S(2)}, u32[]{:S(2)}) collective-permute-start(bf16[128,512]{1,0:T(8,128)(2,1)S(1)} %get-tuple-element.13), channel_id=1, source_target_pairs={{0,96},{16,112},{32,0},{48,16},{64,32},{80,48},{96,64},{112,80},{1... | collective-permute-start | bytes 393224 | tf_op jit(solution)/shard_map/ppermute | solution.py:122
  19.1 47.2 %collective-permute-start.5 = (bf16[128,512]{1,0:T(8,128)(2,1)S(1)}, bf16[128,512]{1,0:T(8,128)(2,1)S(1)}, u32[]{:S(2)}, u32[]{:S(2)}) collective-permute-start(bf16[128,512]{1,0:T(8,128)(2,1)S(1)} %get-tuple-element.13), channel_id=1, source_target_pairs={{0,80},{16,96},{32,112},{48,0},{64,16},{80,32},{96,48},{112,64},{1... | collective-permute-start | bytes 393224 | tf_op jit(solution)/shard_map/ppermute | solution.py:122
  23.0 22.5 %collective-permute-start.2 = (bf16[128,512]{1,0:T(8,128)(2,1)S(1)}, bf16[128,512]{1,0:T(8,128)(2,1)S(1)}, u32[]{:S(2)}, u32[]{:S(2)}) collective-permute-start(bf16[128,512]{1,0:T(8,128)(2,1)S(1)} %get-tuple-element.13), channel_id=1, source_target_pairs={{0,32},{16,48},{32,64},{48,80},{64,96},{80,112},{96,0},{112,16},{1... | collective-permute-start | bytes 393224 | tf_op jit(solution)/shard_map/ppermute | solution.py:122
  26.6 11.8 %collective-permute-start.1 = (bf16[128,512]{1,0:T(8,128)(2,1)S(1)}, bf16[128,512]{1,0:T(8,128)(2,1)S(1)}, u32[]{:S(2)}, u32[]{:S(2)}) collective-permute-start(bf16[128,512]{1,0:T(8,128)(2,1)S(1)} %get-tuple-element.13), channel_id=1, source_target_pairs={{0,16},{16,32},{32,48},{48,64},{64,80},{80,96},{96,112},{112,0},{1... | collective-permute-start | bytes 393224 | tf_op jit(solution)/shard_map/ppermute | solution.py:122
  30.8 44.8 %copy-start.5 = (bf16[128,896]{1,0:T(8,128)(2,1)S(1)}, bf16[128,896]{1,0:T(8,128)(2,1)}, u32[]{:S(2)}) copy-start(bf16[128,896]{1,0:T(8,128)(2,1)} %param.11) | copy-start | bytes 688132
  31.9 44.1 %all-to-all-start.1 = ((bf16[32,64,128]{2,1,0:T(8,128)(2,1)}), bf16[32,64,128]{2,1,0:T(8,128)(2,1)S(1)}, u32[]{:S(2)}, u32[]{:S(2)}) async-start(bf16[32,64,128]{2,1,0:T(8,128)(2,1)} %bitcast.6), calls=%async_computation.1 | async-start | bytes 1048576 | tf_op jit(solution)/shard_map/all_to_all | solution.py:163
  38.5 26.5 %collective-permute-start.3 = (bf16[128,512]{1,0:T(8,128)(2,1)S(1)}, bf16[128,512]{1,0:T(8,128)(2,1)S(1)}, u32[]{:S(2)}, u32[]{:S(2)}) collective-permute-start(bf16[128,512]{1,0:T(8,128)(2,1)S(1)} %get-tuple-element.13), channel_id=1, source_target_pairs={{0,48},{16,64},{32,80},{48,96},{64,112},{80,0},{96,16},{112,32},{1... | collective-permute-start | bytes 393224 | tf_op jit(solution)/shard_map/ppermute | solution.py:122
  45.6 20.1 %collective-permute-start.4 = (bf16[128,512]{1,0:T(8,128)(2,1)S(1)}, bf16[128,512]{1,0:T(8,128)(2,1)S(1)}, u32[]{:S(2)}, u32[]{:S(2)}) collective-permute-start(bf16[128,512]{1,0:T(8,128)(2,1)S(1)} %get-tuple-element.13), channel_id=1, source_target_pairs={{0,64},{16,80},{32,96},{48,112},{64,0},{80,16},{96,32},{112,48},{1... | collective-permute-start | bytes 393224 | tf_op jit(solution)/shard_map/ppermute | solution.py:122
  68.3 38.1 %collective-permute-start.10 = (bf16[1024,512]{1,0:T(8,128)(2,1)}, bf16[1024,512]{1,0:T(8,128)(2,1)S(1)}, u32[]{:S(2)}, u32[]{:S(2)}) collective-permute-start(bf16[1024,512]{1,0:T(8,128)(2,1)} %constant_dynamic-update-slice_fusion.refs_3_), channel_id=1, source_target_pairs={{0,384},{128,0},{256,128},{384,256},{1,385},{129,1},{257,129},{385... | collective-permute-start | bytes 3145736 | tf_op jit(solution)/shard_map/ppermute | solution.py:122
  73.1 38.1 %collective-permute-start.8 = (bf16[1024,512]{1,0:T(8,128)(2,1)}, bf16[1024,512]{1,0:T(8,128)(2,1)}, u32[]{:S(2)}, u32[]{:S(2)}) collective-permute-start(bf16[1024,512]{1,0:T(8,128)(2,1)} %constant_dynamic-update-slice_fusion.refs_3_), channel_id=1, source_target_pairs={{0,128},{128,256},{256,384},{384,0},{1,129},{129,257},{257,385},{3... | collective-permute-start | bytes 3145736 | tf_op jit(solution)/shard_map/ppermute | solution.py:122
  76.7 53.7 %all-to-all-start = ((f32[32,1,896]{2,1,0:T(1,128)}), f32[32,1,896]{2,1,0:T(1,128)S(1)}, u32[]{:S(2)}, u32[]{:S(2)}) async-start(f32[32,1,896]{2,1,0:T(1,128)} %broadcast_in_dim.2), calls=%async_computation | async-start | bytes 229376 | tf_op jit(solution)/shard_map/all_to_all | solution.py:170
  86.7 29.2 %collective-permute-start = (bf16[32,64,128]{2,1,0:T(8,128)(2,1)S(1)}, bf16[32,64,128]{2,1,0:T(8,128)(2,1)S(1)}, u32[]{:S(2)}, u32[]{:S(2)}) collective-permute-start(bf16[32,64,128]{2,1,0:T(8,128)(2,1)S(1)} %all-to-all-done.1.refs_1_.refs_2_), channel_id=1, source_target_pairs={{0,1},{1,0},{2,3},{3,2},{4,5},{5,4},{6,7},{7,6},{8,9},{9,8},{10,11... | collective-permute-start | bytes 1572872 | tf_op jit(solution)/shard_map/ppermute | solution.py:164
  107.2 20.2 %collective-permute-start.11 = (bf16[512,512]{1,0:T(8,128)(2,1)}, bf16[512,512]{1,0:T(8,128)(2,1)}, u32[]{:S(2)}, u32[]{:S(2)}) collective-permute-start(bf16[512,512]{1,0:T(8,128)(2,1)} %slice.33), channel_id=1, source_target_pairs={{0,384},{128,0},{256,128},{384,256},{1,385},{129,1},{257,129},{385... | collective-permute-start | bytes 1572872 | tf_op jit(solution)/shard_map/ppermute | solution.py:122
  113.1 14.4 %collective-permute-start.9 = (bf16[512,512]{1,0:T(8,128)(2,1)}, bf16[512,512]{1,0:T(8,128)(2,1)}, u32[]{:S(2)}, u32[]{:S(2)}) collective-permute-start(bf16[512,512]{1,0:T(8,128)(2,1)} %slice.32), channel_id=1, source_target_pairs={{0,128},{128,256},{256,384},{384,0},{1,129},{129,257},{257,385},{3... | collective-permute-start | bytes 1572872 | tf_op jit(solution)/shard_map/ppermute | solution.py:122
  121.7 1.9 %copy-start.1 = (bf16[4096,384]{1,0:T(8,128)(2,1)S(1)}, bf16[4096,384]{1,0:T(8,128)(2,1)}, u32[]{:S(2)}) copy-start(bf16[4096,384]{1,0:T(8,128)(2,1)} %all-gather.2.cloned.1.call-done.refs_3_) | copy-start | bytes 9437188
  130.4 30.5 %copy-start.2 = (f32[1,1,9,128,128]{4,3,2,1,0:T(8,128)S(1)}, f32[1,1,9,128,128]{4,3,2,1,0:T(8,128)}, u32[]{:S(2)}) copy-start(f32[1,1,9,128,128]{4,3,2,1,0:T(8,128)} %param.17) | copy-start | bytes 1769476
  130.4 30.5 %copy-start.3 = (f32[1,1,9,128,128]{4,3,2,1,0:T(8,128)S(1)}, f32[1,1,9,128,128]{4,3,2,1,0:T(8,128)}, u32[]{:S(2)}) copy-start(f32[1,1,9,128,128]{4,3,2,1,0:T(8,128)} %param.18) | copy-start | bytes 1769476
  130.4 30.5 %copy-start.4 = (f32[1,1,9,128,128]{4,3,2,1,0:T(8,128)S(1)}, f32[1,1,9,128,128]{4,3,2,1,0:T(8,128)}, u32[]{:S(2)}) copy-start(f32[1,1,9,128,128]{4,3,2,1,0:T(8,128)} %param.19) | copy-start | bytes 1769476
  130.4 28.6 %all-to-all-start.2 = ((bf16[32,12,4,128]{3,2,1,0:T(4,128)(2,1)}), bf16[32,12,4,128]{3,2,1,0:T(4,128)(2,1)S(1)}, u32[]{:S(2)}, u32[]{:S(2)}) async-start(bf16[32,12,4,128]{3,2,1,0:T(4,128)(2,1)} %bitcast.7), calls=%async_computation.2 | async-start | bytes 786432 | tf_op jit(solution)/shard_map/all_to_all | solution.py:228
Sparse Core Ops, SparseCore 0:
  11.2 98.4 all-gather.1

commit v3 on v0

v3 whole, which is shorter than its diff:
```python
import jax
import jax.numpy as jnp
from jax import lax
from jax.experimental import pallas as pl
from jax.experimental.pallas import tpu as pltpu
from jax.sharding import Mesh
from jax.sharding import PartitionSpec as P

TILE = 128
DP = ("dp_0", "dp_1")


beta_one = 0.9
beta_two = 0.95
adam_eps = 1e-08
learn_rate = 0.01
decay_rate = 0.1
step_count = 10.0


def adam_update(weight, moment, second, grad):
    moment_new = beta_one * moment + (1.0 - beta_one) * grad
    second_new = beta_two * second + (1.0 - beta_two) * grad * grad
    first_fix = 1.0 - beta_one**step_count
    second_fix = 1.0 - beta_two**step_count
    update = moment_new / first_fix / (jnp.sqrt(second_new / second_fix) + adam_eps)
    return (weight - learn_rate * (update + decay_rate * weight), moment_new, second_new)


def slot_numbers(owner_row):
    places = jnp.arange(owner_row.shape[0], dtype=jnp.int32)
    earlier = (owner_row[:, None] == owner_row[None, :]) & (places[:, None] > places[None, :])
    return jnp.sum(earlier.astype(jnp.int32), axis=1)


def split_three(value):
    high = value.astype(jnp.bfloat16).astype(jnp.float32)
    rest = value - high
    middle = rest.astype(jnp.bfloat16).astype(jnp.float32)
    return high, middle, (rest - middle).astype(jnp.bfloat16).astype(jnp.float32)


def lane_groups(array, group, lanes):
    return array[:, group * lanes : (group + 1) * lanes]


def spread_kernel(grads_ref, spread_ref):
    groups, tokens, width = spread_ref.shape
    lanes = TILE // groups
    tiles = grads_ref.shape[1] // TILE
    grads = grads_ref[...]
    padding = [jnp.zeros((tokens, width - tiles * lanes), grads.dtype)]
    for x in range(groups):
        parts = [lane_groups(grads, t * groups + x, lanes) for t in range(tiles)]
        spread_ref[x] = jnp.concatenate(parts + padding, axis=1)


def sums_kernel(scalars_ref, target_ref, grads_ref, *refs, chunks, tiles, owners, slots):
    pairs = [(refs[2 * n], refs[2 * n + 1]) for n in range(len(chunks))]
    slots_ref, sums, places = refs[2 * len(chunks) :]
    selected, flip, at_x = scalars_ref[0], scalars_ref[1], scalars_ref[2]
    groups, group_rows, width = sums.shape
    tokens = pairs[0][0].shape[2]
    lanes = TILE // groups
    lane = lax.broadcasted_iota(jnp.int32, (group_rows, width), 1)
    kept = lane // lanes == selected
    half = group_rows // 2
    for g in range(groups):
        total = jnp.zeros((group_rows, width), jnp.float32)
        for (step_x, first_y), (mine_ref, other_ref) in zip(chunks, pairs):
            x = lax.rem(at_x + step_x, groups)

            def step(j, total, x=x, first_y=first_y, mine_ref=mine_ref, other_ref=other_ref):
                for u in range(4):
                    y = j * 4 + u
                    rows = jnp.concatenate(
                        [ref[y, g * half : (g + 1) * half, :] for ref in (mine_ref, other_ref)],
                        axis=0,
                    )
                    place = ((first_y + y) * groups + x) * tokens
                    partial = jnp.dot(
                        rows,
                        grads_ref[pl.ds(pl.multiple_of(place, tokens), tokens), :],
                        preferred_element_type=jnp.float32,
                    )
                    rounded = partial.astype(jnp.bfloat16).astype(jnp.float32)
                    total = total + jnp.where(kept, partial, rounded)
                return total

            total = lax.fori_loop(0, mine_ref.shape[0] // 4, step, total)
        sums[g] = total

    places[...] = jnp.zeros_like(places)
    part = slots_ref.shape[1]
    for tile in range(tiles):
        rest = tile - (tile > selected).astype(jnp.int32)
        held = jnp.concatenate([lane_groups(sums[g], tile, lanes) for g in range(groups)], axis=1)

        @pl.when(tile != selected)
        def _(held=held, rest=rest):
            for q in range(owners):
                places[target_ref[rest * owners + q]] = held[q * part : (q + 1) * part, :]

        @pl.when(tile == selected)
        def _(held=held):
            for q in range(owners):
                owner = jnp.bitwise_xor(q, flip * (owners // 2))
                for n, term in enumerate(split_three(held[q * part : (q + 1) * part, :])):
                    places[owner * slots + slots - 3 + n] = term

    slots_ref[...] = places[...].astype(slots_ref.dtype)


def owner_kernel(received_ref, *refs, size_x, size_y, part):
    sel_in, off_in, sel_out, off_out = refs[:3], refs[3:6], refs[6:9], refs[9:12]
    grads = refs[12]
    slots = grads.shape[0]
    capacity = slots - 3
    lanes = TILE // size_x
    rows = received_ref.shape[0] // size_x
    sources = [received_ref[pl.ds(x * rows, rows), :].astype(jnp.float32) for x in range(size_x)]
    for g in range(size_x):
        whole = jnp.concatenate([lane_groups(source, g, lanes) for source in sources], axis=1)
        for y in range(size_y):
            for n in range(slots):
                row = (y * slots + n) * part
                place = (y * size_x + g) * part
                grads[n, place : place + part, :] = whole[row : row + part, :]
    sel_sum = grads[capacity] + grads[capacity + 1] + grads[capacity + 2]
    for ref, new in zip(sel_out, adam_update(*(ref[...] for ref in sel_in), sel_sum)):
        ref[...] = new
    for n in range(capacity):
        for ref, new in zip(off_out, adam_update(*(ref[n] for ref in off_in), grads[n])):
            ref[n] = new


def shift(array, axis, by):
    size = lax.axis_size(axis)
    return lax.ppermute(array, axis, [(i, (i + by) % size) for i in range(size)])


def body(
    acts,
    grad_out,
    selected,
    owner,
    sel_weight,
    sel_moment,
    sel_second,
    off_weight,
    off_moment,
    off_second,
):
    group_size = lax.axis_size(DP)
    size_x, size_y = lax.axis_size(DP[0]), lax.axis_size(DP[1])
    at_x = lax.axis_index(DP[0])
    core = lax.rem(lax.axis_index("tensor"), 2)
    tokens_here, rows_all = acts.shape
    cols_here = grad_out.shape[1]
    tiles_here = cols_here // TILE
    row_block = rows_all // group_size
    part = row_block // group_size
    capacity = off_weight.shape[2]
    slots = capacity + 3
    owner_row = owner[0, :, 0]
    width = 2 * TILE
    whole = pl.BlockSpec(memory_space=pltpu.VMEM)
    small = pl.BlockSpec(memory_space=pltpu.SMEM)

    spread = pl.pallas_call(
        spread_kernel,
        in_specs=[whole],
        out_specs=whole,
        out_shape=jax.ShapeDtypeStruct((size_x, tokens_here, width), grad_out.dtype),
        name="spread",
    )(grad_out)
    spread = lax.all_to_all(spread, DP[0], split_axis=0, concat_axis=0, tiled=True)
    grads = lax.all_gather(spread.reshape(size_x * tokens_here, width), DP[1], axis=0, tiled=True)

    halved = lax.dynamic_slice_in_dim(acts, core * (rows_all // 2), rows_all // 2, axis=1)
    halved = halved.T.reshape(group_size // 2, size_y, size_x, part, tokens_here)
    halved = jnp.transpose(halved, (1, 2, 0, 3, 4)).reshape(size_y, -1, tokens_here)
    own = lax.all_to_all(halved, DP[1], split_axis=0, concat_axis=0, tiled=True)
    left, right = shift(own, DP[0], 1), shift(own, DP[0], -1)
    half_y = size_y // 2
    far_low, far_high = shift(left[:half_y], DP[0], 1), shift(right[half_y:], DP[0], -1)
    swap = [(i, i ^ 1) for i in range(lax.axis_size("tensor"))]
    chunks = [(0, 0), (size_x - 1, 0), (1, 0), (2, 0), (2, half_y)]
    acts_rows = []
    for array in (own, left, right, far_low, far_high):
        acts_rows += [array, lax.ppermute(array, "tensor", swap)]

    gram = lax.dot_general(acts, acts, (((1,), (1,)), ((), ())), preferred_element_type=jnp.float32)
    grad_wide = grad_out.astype(jnp.float32)
    squares = jnp.sum(grad_wide * jnp.dot(gram, grad_wide, precision=lax.Precision.HIGHEST), axis=0)
    copies = jnp.broadcast_to(squares, (group_size, 1, cols_here))
    squares = lax.all_to_all(copies, DP, split_axis=0, concat_axis=0, tiled=True)
    column_norm = jnp.sqrt(squares.sum(axis=(0, 1)))

    target = owner_row * slots + slot_numbers(owner_row)
    target = target.reshape(tiles_here - 1, 2, group_size // 2)
    target = jnp.where(core == 0, target, target[:, ::-1]).reshape(-1)
    scalars = jnp.stack([selected[0, 0], core, at_x]).astype(jnp.int32)
    outgoing = pl.pallas_call(
        lambda *refs: sums_kernel(
            *refs, chunks=chunks, tiles=tiles_here, owners=group_size, slots=slots
        ),
        in_specs=[small] * 2 + [whole] * 11,
        out_specs=whole,
        out_shape=jax.ShapeDtypeStruct((group_size * slots, part, TILE), jnp.bfloat16),
        scratch_shapes=[
            pltpu.VMEM((size_x, row_block, width), jnp.float32),
            pltpu.VMEM((group_size * slots, part, TILE), jnp.float32),
        ],
        cost_estimate=pl.CostEstimate(
            flops=2 * group_size * tokens_here * size_x * row_block * width,
            bytes_accessed=2 * group_size * tokens_here * (size_x * row_block + width),
            transcendentals=0,
        ),
        compiler_params=pltpu.CompilerParams(vmem_limit_bytes=32 << 20),
        name="replica_sums",
    )(scalars, target, grads, *acts_rows)

    received = lax.all_to_all(
        outgoing.reshape(group_size, slots * part, TILE), DP, split_axis=0, concat_axis=0, tiled=True
    )
    block = (row_block, TILE)
    outs = pl.pallas_call(
        lambda *refs: owner_kernel(*refs, size_x=size_x, size_y=size_y, part=part),
        in_specs=[whole] * 7,
        out_specs=[whole] * 6,
        out_shape=[jax.ShapeDtypeStruct(block, jnp.float32)] * 3
        + [jax.ShapeDtypeStruct((capacity, *block), jnp.float32)] * 3,
        scratch_shapes=[pltpu.VMEM((slots, *block), jnp.float32)],
        compiler_params=pltpu.CompilerParams(vmem_limit_bytes=24 << 20),
        name="owner_adam",
    )(
        received.reshape(-1, TILE),
        sel_weight,
        sel_moment,
        sel_second,
        *(state.reshape(capacity, *block) for state in (off_weight, off_moment, off_second)),
    )
    return (column_norm, *outs[:3], *(new.reshape(off_weight.shape) for new in outs[3:]))


def solution(mesh):
    torus = Mesh(mesh.devices.reshape(4, 8, mesh.shape["tensor"]), ("dp_0", "dp_1", "tensor"))
    in_specs = (
        P(DP, None),
        P(DP, "tensor"),
        P("tensor", None),
        P("tensor", None, None),
        P(DP, "tensor"),
        P(DP, "tensor"),
        P(DP, "tensor"),
        P(DP, "tensor", None, None, None),
        P(DP, "tensor", None, None, None),
        P(DP, "tensor", None, None, None),
    )
    out_specs = (
        P("tensor"),
        P(DP, "tensor"),
        P(DP, "tensor"),
        P(DP, "tensor"),
        P(DP, "tensor", None, None, None),
        P(DP, "tensor", None, None, None),
        P(DP, "tensor", None, None, None),
    )
    return jax.shard_map(body, mesh=torus, in_specs=in_specs, out_specs=out_specs, check_vma=False)
```

time: 316 us -> 141 us (0.45)
  the two profiles are of different devices: /device:TPU:412 before, /device:TPU:456 now
where the time goes in v3:
time: 141 us; the launch traced here: 140 us
  starting transfers between devices  38.6 us (27%)
  blocking collectives  37.5 us (27%)
  waiting for transfers between devices  21.5 us (15%)
  between operations  14.9 us (11%)
  Pallas kernels  14 us (10%)
  local copies, waits for them, and re-layouts  10.9 us (8%)
    all_to_all x1, blocking collectives, body(): own = lax.all_to_all(halved, DP[1], split_axis=0, concat_axis=0, tiled=True)  26.4 us
    ppermute x4, starting transfers between devices, shift(): lax.ppermute(array, axis, [(i, (i + by) % size) for i in range(size)])  14.2 us
    all_to_all x1, waiting for transfers between devices, body(): lax.all_to_all(outgoing.reshape(group_size, slots * part, TILE), DP, spli...  13.8 us
    all_to_all x1, blocking collectives, body(): lax.all_to_all(spread, DP[0], split_axis=0, concat_axis=0, tiled=True)  11.1 us
    ppermute x5, starting transfers between devices, body(): acts_rows += [array, lax.ppermute(array, 'tensor', swap)]  10.6 us
    pallas_call x1, Pallas kernels, body(): pl.pallas_call(lambda *refs: sums_kernel(*refs, chunks=chunks, tiles=tile...  9.87 us
    all_to_all x1, starting transfers between devices, body(): lax.all_to_all(outgoing.reshape(group_size, slots * part, TILE), DP, spli...  9.45 us
    unnamed x25, local copies, waits for them, and re-layouts  7.52 us
  transfers between devices with their start and end apart: 12, of which 3 were waited for; matrix products, arithmetic and copies ran while one was open for 4% of the time, Pallas kernels for 7%

profile of v3, /device:TPU:456, one launch (start us, length us, event | category | flops | bytes accessed | tf_op | source)
XLA Modules:
  0.0 139.6 jit_solution(8231184281934894978)
XLA Ops:
  7.2 2.0 %spread.1 = bf16[4,128,256]{2,1,0:T(8,128)(2,1)} custom-call(bf16[128,896]{1,0:T(8,128)(2,1)} %grads_ref.1), custom_call_target="tpu_custom_call" | custom-call | tf_op jit(solution)/shard_map/spread/pallas_call | solution.py:170
  9.2 11.1 %all_to_all.20 = bf16[4,128,256]{2,1,0:T(8,128)(2,1)} all-to-all(bf16[4,128,256]{2,1,0:T(8,128)(2,1)} %spread.1), channel_id=1, replica_groups=mesh['dp_0'=4,'dp_1'=8,'tensor'=16] {'dp_0'}, dimensions={0} | all-to-all | bytes 524288 | tf_op jit(solution)/shard_map/all_to_all | solution.py:177
  20.9 26.4 %all_to_all.21.refs_3_ = bf16[8,256,128]{2,1,0:T(8,128)(2,1)S(1)} all-to-all(bf16[8,256,128]{2,1,0:T(8,128)(2,1)S(1)} %bitcast.29), channel_id=1, replica_groups=mesh['dp_0'=4,'dp_1'=8,'tensor'=16] {'dp_1'}, dimensions={0} | all-to-all | bytes 1048576 | tf_op jit(solution)/shard_map/all_to_all | solution.py:183
  47.4 2.3 %collective-permute-start.1 = (bf16[8,256,128]{2,1,0:T(8,128)(2,1)S(1)}, bf16[8,256,128]{2,1,0:T(8,128)(2,1)S(1)}, u32[]{:S(2)}, u32[]{:S(2)}) collective-permute-start(bf16[8,256,128]{2,1,0:T(8,128)(2,1)S(1)} %all_to_all.21.refs_3_), channel_id=1, source_target_pairs={{0,128},{128,256},{256,384},{384,0},{1,129},{129,257},{257,385},{3... | collective-permute-start | bytes 1572872 | tf_op jit(solution)/shard_map/ppermute | solution.py:139
  49.7 4.9 %collective-permute-start.3 = (bf16[8,256,128]{2,1,0:T(8,128)(2,1)S(1)}, bf16[8,256,128]{2,1,0:T(8,128)(2,1)S(1)}, u32[]{:S(2)}, u32[]{:S(2)}) collective-permute-start(bf16[8,256,128]{2,1,0:T(8,128)(2,1)S(1)} %all_to_all.21.refs_3_), channel_id=1, source_target_pairs={{0,384},{128,0},{256,128},{384,256},{1,385},{129,1},{257,129},{385... | collective-permute-start | bytes 1572872 | tf_op jit(solution)/shard_map/ppermute | solution.py:139
  55.0 7.5 %collective-permute-done.1.refs_5_ = bf16[8,256,128]{2,1,0:T(8,128)(2,1)S(1)} collective-permute-done((bf16[8,256,128]{2,1,0:T(8,128)(2,1)S(1)}, bf16[8,256,128]{2,1,0:T(8,128)(2,1)S(1)}, u32[]{:S(2)}, u32[]{:S(2)}) %collective-permute-start.1) | collective-permute-done | bytes 524320 | tf_op jit(solution)/shard_map/ppermute | solution.py:139
  63.2 1.9 %collective-permute-start.5 = (bf16[4,256,128]{2,1,0:T(8,128)(2,1)}, bf16[4,256,128]{2,1,0:T(8,128)(2,1)S(1)}, u32[]{:S(2)}, u32[]{:S(2)}) collective-permute-start(bf16[4,256,128]{2,1,0:T(8,128)(2,1)} %slice.8), channel_id=1, source_target_pairs={{0,128},{128,256},{256,384},{384,0},{1,129},{129,257},{257,385},{3... | collective-permute-start | bytes 786440 | tf_op jit(solution)/shard_map/ppermute | solution.py:139
  65.8 5.1 %collective-permute-start.7 = (bf16[4,256,128]{2,1,0:T(8,128)(2,1)}, bf16[4,256,128]{2,1,0:T(8,128)(2,1)}, u32[]{:S(2)}, u32[]{:S(2)}) collective-permute-start(bf16[4,256,128]{2,1,0:T(8,128)(2,1)} %slice.9), channel_id=1, source_target_pairs={{0,384},{128,0},{256,128},{384,256},{1,385},{129,1},{257,129},{385... | collective-permute-start | bytes 786440 | tf_op jit(solution)/shard_map/ppermute | solution.py:139
  72.1 4.3 %all-to-all-start = ((f32[32,1,896]{2,1,0:T(1,128)}), f32[32,1,896]{2,1,0:T(1,128)}, u32[]{:S(2)}, u32[]{:S(2)}) async-start(f32[32,1,896]{2,1,0:T(1,128)} %broadcast_in_dim.2), calls=%async_computation | async-start | bytes 229376 | tf_op jit(solution)/shard_map/all_to_all | solution.py:197
  76.4 1.9 %collective-permute-start = (bf16[8,256,128]{2,1,0:T(8,128)(2,1)S(1)}, bf16[8,256,128]{2,1,0:T(8,128)(2,1)S(1)}, u32[]{:S(2)}, u32[]{:S(2)}) collective-permute-start(bf16[8,256,128]{2,1,0:T(8,128)(2,1)S(1)} %all_to_all.21.refs_3_), channel_id=1, source_target_pairs={{0,1},{1,0},{2,3},{3,2},{4,5},{5,4},{6,7},{7,6},{8,9},{9,8},{10,11... | collective-permute-start | bytes 1572872 | tf_op jit(solution)/shard_map/ppermute | solution.py:191
  78.3 2.4 %collective-permute-start.2 = (bf16[8,256,128]{2,1,0:T(8,128)(2,1)S(1)}, bf16[8,256,128]{2,1,0:T(8,128)(2,1)}, u32[]{:S(2)}, u32[]{:S(2)}) collective-permute-start(bf16[8,256,128]{2,1,0:T(8,128)(2,1)S(1)} %collective-permute-done.1.refs_5_), channel_id=1, source_target_pairs={{0,1},{1,0},{2,3},{3,2},{4,5},{5,4},{6,7},{7,6},{8,9},{9,8},{10,11... | collective-permute-start | bytes 1572872 | tf_op jit(solution)/shard_map/ppermute | solution.py:191
  80.8 1.9 %collective-permute-start.4 = (bf16[8,256,128]{2,1,0:T(8,128)(2,1)S(1)}, bf16[8,256,128]{2,1,0:T(8,128)(2,1)}, u32[]{:S(2)}, u32[]{:S(2)}) collective-permute-start(bf16[8,256,128]{2,1,0:T(8,128)(2,1)S(1)} %collective-permute-done.3.refs_7_), channel_id=1, source_target_pairs={{0,1},{1,0},{2,3},{3,2},{4,5},{5,4},{6,7},{7,6},{8,9},{9,8},{10,11... | collective-permute-start | bytes 1572872 | tf_op jit(solution)/shard_map/ppermute | solution.py:191
  83.1 2.4 %collective-permute-start.6 = (bf16[4,256,128]{2,1,0:T(8,128)(2,1)S(1)}, bf16[4,256,128]{2,1,0:T(8,128)(2,1)}, u32[]{:S(2)}, u32[]{:S(2)}) collective-permute-start(bf16[4,256,128]{2,1,0:T(8,128)(2,1)S(1)} %collective-permute-done.5.refs_9_), channel_id=1, source_target_pairs={{0,1},{1,0},{2,3},{3,2},{4,5},{5,4},{6,7},{7,6},{8,9},{9,8},{10,11... | collective-permute-start | bytes 786440 | tf_op jit(solution)/shard_map/ppermute | solution.py:191
  85.6 1.9 %collective-permute-start.8 = (bf16[4,256,128]{2,1,0:T(8,128)(2,1)}, bf16[4,256,128]{2,1,0:T(8,128)(2,1)}, u32[]{:S(2)}, u32[]{:S(2)}) collective-permute-start(bf16[4,256,128]{2,1,0:T(8,128)(2,1)} %collective-permute-done.7.refs_11_), channel_id=1, source_target_pairs={{0,1},{1,0},{2,3},{3,2},{4,5},{5,4},{6,7},{7,6},{8,9},{9,8},{10,11... | collective-permute-start | bytes 786440 | tf_op jit(solution)/shard_map/ppermute | solution.py:191
  89.4 1.6 %copy-done.1 = bf16[4096,256]{1,0:T(8,128)(2,1)S(1)} copy-done((bf16[4096,256]{1,0:T(8,128)(2,1)S(1)}, bf16[4096,256]{1,0:T(8,128)(2,1)}, u32[]{:S(2)}) %copy-start.1) | copy-done | bytes 2097176
  91.0 1.0 copy-done.6
  92.0 9.9 %replica_sums.1 = bf16[384,4,128]{2,1,0:T(4,128)(2,1)} custom-call(s32[3]{0:T(128)S(1)} %pad_add_fusion.refs_0_, s32[192]{0:T(256)S(1)} %reshape.57.refs_1_, bf16[4096,256]{1,0:T(8,128)(2,1)S(1)} %copy-done.1, bf16[8,256,128]{2,1,0:T(8,128)(2,1)S(1)} %all_to_all.21.refs_3_, bf16[8,256,128]{2,1,0:T(8,128)(2,1)S(1)} %copy-done.6, ...), custom_call_target="tpu_custom_call" | custom-call | flops 1073741824 | bytes 6291456 | tf_op jit(solution)/shard_map/replica_sums/pallas_call | solution.py:204
  101.9 9.4 %all-to-all-start.3 = ((bf16[32,48,128]{2,1,0:T(8,128)(2,1)}), bf16[32,48,128]{2,1,0:T(8,128)(2,1)S(1)}, u32[]{:S(2)}, u32[]{:S(2)}) async-start(bf16[32,48,128]{2,1,0:T(8,128)(2,1)} %bitcast.9), calls=%async_computation.3 | async-start | bytes 786432 | tf_op jit(solution)/shard_map/all_to_all | solution.py:224
  111.3 1.0 reduce_sum.30
  112.9 13.8 %all-to-all-done.3 = bf16[32,48,128]{2,1,0:T(8,128)(2,1)S(1)} async-done(((bf16[32,48,128]{2,1,0:T(8,128)(2,1)}), bf16[32,48,128]{2,1,0:T(8,128)(2,1)S(1)}, u32[]{:S(2)}, u32[]{:S(2)}) %all-to-all-start.3) | async-done | bytes 393248 | tf_op jit(solution)/shard_map/all_to_all | solution.py:224
  126.7 1.1 copy-done.3
  127.8 1.1 copy-done.4
  128.9 0.8 copy-done.8
  130.5 2.2 %owner_adam.1 = (f32[128,128]{1,0:T(8,128)}, f32[128,128]{1,0:T(8,128)}, f32[128,128]{1,0:T(8,128)}, f32[9,128,128]{2,1,0:T(8,128)}, f32[9,128,128]{2,1,0:T(8,128)}, /*index=5*/f32[9,128,128]{2,1,0:T(8,128)}) custom-call(bf16[1536,128]{1,0:T(8,128)(2,1)S(1)} %bitcast.24, f32[128,128]{1,0:T(8,128)S(1)} %copy-done.7, f32[128,128]{1,0:T(8,128)S(1)} %copy-done.8, ...), custom_call_target="tpu_custom_call" | custom-call | tf_op jit(solution)/shard_map/owner_adam/pallas_call | solution.py:228
  (49 shorter events, 6.7 us)
Async XLA Ops:
  7.2 13.1 %copy-start = (bf16[128,4096]{1,0:T(8,128)(2,1)S(1)}, bf16[128,4096]{1,0:T(8,128)(2,1)}, u32[]{:S(2)}) copy-start(bf16[128,4096]{1,0:T(8,128)(2,1)} %param.10) | copy-start | bytes 3145732
  7.2 82.2 %all-gather.2.cloned.1.call-start = ((), (), s32[]{:S(2)}) async-start(), calls=%async_computation.4 | async-start | bytes 2359296 | tf_op jit(solution)/shard_map/all_gather | solution.py:178
  20.9 50.1 %copy-start.10 = (bf16[128,896]{1,0:T(8,128)(2,1)S(1)}, bf16[128,896]{1,0:T(8,128)(2,1)}, u32[]{:S(2)}) copy-start(bf16[128,896]{1,0:T(8,128)(2,1)} %grads_ref.1) | copy-start | bytes 688132
  47.4 35.3 %copy-start.11 = (s32[1,192,1]{1,2,0:T(1,128)S(1)}, s32[1,192,1]{1,2,0:T(1,128)}, u32[]{:S(2)}) copy-start(s32[1,192,1]{1,2,0:T(1,128)} %param.13) | copy-start | bytes 2308
  47.4 15.1 %collective-permute-start.1 = (bf16[8,256,128]{2,1,0:T(8,128)(2,1)S(1)}, bf16[8,256,128]{2,1,0:T(8,128)(2,1)S(1)}, u32[]{:S(2)}, u32[]{:S(2)}) collective-permute-start(bf16[8,256,128]{2,1,0:T(8,128)(2,1)S(1)} %all_to_all.21.refs_3_), channel_id=1, source_target_pairs={{0,128},{128,256},{256,384},{384,0},{1,129},{129,257},{257,385},{3... | collective-permute-start | bytes 1572872 | tf_op jit(solution)/shard_map/ppermute | solution.py:139
  49.7 15.4 %collective-permute-start.3 = (bf16[8,256,128]{2,1,0:T(8,128)(2,1)S(1)}, bf16[8,256,128]{2,1,0:T(8,128)(2,1)S(1)}, u32[]{:S(2)}, u32[]{:S(2)}) collective-permute-start(bf16[8,256,128]{2,1,0:T(8,128)(2,1)S(1)} %all_to_all.21.refs_3_), channel_id=1, source_target_pairs={{0,384},{128,0},{256,128},{384,256},{1,385},{129,1},{257,129},{385... | collective-permute-start | bytes 1572872 | tf_op jit(solution)/shard_map/ppermute | solution.py:139
  63.2 19.9 %collective-permute-start.5 = (bf16[4,256,128]{2,1,0:T(8,128)(2,1)}, bf16[4,256,128]{2,1,0:T(8,128)(2,1)S(1)}, u32[]{:S(2)}, u32[]{:S(2)}) collective-permute-start(bf16[4,256,128]{2,1,0:T(8,128)(2,1)} %slice.8), channel_id=1, source_target_pairs={{0,128},{128,256},{256,384},{384,0},{1,129},{129,257},{257,385},{3... | collective-permute-start | bytes 786440 | tf_op jit(solution)/shard_map/ppermute | solution.py:139
  65.8 19.7 %collective-permute-start.7 = (bf16[4,256,128]{2,1,0:T(8,128)(2,1)}, bf16[4,256,128]{2,1,0:T(8,128)(2,1)}, u32[]{:S(2)}, u32[]{:S(2)}) collective-permute-start(bf16[4,256,128]{2,1,0:T(8,128)(2,1)} %slice.9), channel_id=1, source_target_pairs={{0,384},{128,0},{256,128},{384,256},{1,385},{129,1},{257,129},{385... | collective-permute-start | bytes 786440 | tf_op jit(solution)/shard_map/ppermute | solution.py:139
  72.1 29.8 %all-to-all-start = ((f32[32,1,896]{2,1,0:T(1,128)}), f32[32,1,896]{2,1,0:T(1,128)}, u32[]{:S(2)}, u32[]{:S(2)}) async-start(f32[32,1,896]{2,1,0:T(1,128)} %broadcast_in_dim.2), calls=%async_computation | async-start | bytes 229376 | tf_op jit(solution)/shard_map/all_to_all | solution.py:197
  76.4 11.9 %collective-permute-start = (bf16[8,256,128]{2,1,0:T(8,128)(2,1)S(1)}, bf16[8,256,128]{2,1,0:T(8,128)(2,1)S(1)}, u32[]{:S(2)}, u32[]{:S(2)}) collective-permute-start(bf16[8,256,128]{2,1,0:T(8,128)(2,1)S(1)} %all_to_all.21.refs_3_), channel_id=1, source_target_pairs={{0,1},{1,0},{2,3},{3,2},{4,5},{5,4},{6,7},{7,6},{8,9},{9,8},{10,11... | collective-permute-start | bytes 1572872 | tf_op jit(solution)/shard_map/ppermute | solution.py:191
  78.3 11.0 %collective-permute-start.2 = (bf16[8,256,128]{2,1,0:T(8,128)(2,1)S(1)}, bf16[8,256,128]{2,1,0:T(8,128)(2,1)}, u32[]{:S(2)}, u32[]{:S(2)}) collective-permute-start(bf16[8,256,128]{2,1,0:T(8,128)(2,1)S(1)} %collective-permute-done.1.refs_5_), channel_id=1, source_target_pairs={{0,1},{1,0},{2,3},{3,2},{4,5},{5,4},{6,7},{7,6},{8,9},{9,8},{10,11... | collective-permute-start | bytes 1572872 | tf_op jit(solution)/shard_map/ppermute | solution.py:191
  80.8 8.6 %collective-permute-start.4 = (bf16[8,256,128]{2,1,0:T(8,128)(2,1)S(1)}, bf16[8,256,128]{2,1,0:T(8,128)(2,1)}, u32[]{:S(2)}, u32[]{:S(2)}) collective-permute-start(bf16[8,256,128]{2,1,0:T(8,128)(2,1)S(1)} %collective-permute-done.3.refs_7_), channel_id=1, source_target_pairs={{0,1},{1,0},{2,3},{3,2},{4,5},{5,4},{6,7},{7,6},{8,9},{9,8},{10,11... | collective-permute-start | bytes 1572872 | tf_op jit(solution)/shard_map/ppermute | solution.py:191
  83.1 6.0 %collective-permute-start.6 = (bf16[4,256,128]{2,1,0:T(8,128)(2,1)S(1)}, bf16[4,256,128]{2,1,0:T(8,128)(2,1)}, u32[]{:S(2)}, u32[]{:S(2)}) collective-permute-start(bf16[4,256,128]{2,1,0:T(8,128)(2,1)S(1)} %collective-permute-done.5.refs_9_), channel_id=1, source_target_pairs={{0,1},{1,0},{2,3},{3,2},{4,5},{5,4},{6,7},{7,6},{8,9},{9,8},{10,11... | collective-permute-start | bytes 786440 | tf_op jit(solution)/shard_map/ppermute | solution.py:191
  85.6 3.8 %collective-permute-start.8 = (bf16[4,256,128]{2,1,0:T(8,128)(2,1)}, bf16[4,256,128]{2,1,0:T(8,128)(2,1)}, u32[]{:S(2)}, u32[]{:S(2)}) collective-permute-start(bf16[4,256,128]{2,1,0:T(8,128)(2,1)} %collective-permute-done.7.refs_11_), channel_id=1, source_target_pairs={{0,1},{1,0},{2,3},{3,2},{4,5},{5,4},{6,7},{7,6},{8,9},{9,8},{10,11... | collective-permute-start | bytes 786440 | tf_op jit(solution)/shard_map/ppermute | solution.py:191
  88.3 0.8 copy-start.5
  89.4 1.6 %copy-start.1 = (bf16[4096,256]{1,0:T(8,128)(2,1)S(1)}, bf16[4096,256]{1,0:T(8,128)(2,1)}, u32[]{:S(2)}) copy-start(bf16[4096,256]{1,0:T(8,128)(2,1)} %all-gather.2.cloned.1.call-done.refs_2_) | copy-start | bytes 6291460
  91.0 1.0 copy-start.6
  92.0 34.7 %copy-start.2 = (f32[1,1,9,128,128]{4,3,2,1,0:T(8,128)S(1)}, f32[1,1,9,128,128]{4,3,2,1,0:T(8,128)}, u32[]{:S(2)}) copy-start(f32[1,1,9,128,128]{4,3,2,1,0:T(8,128)} %param.17) | copy-start | bytes 1769476
  92.0 34.7 %copy-start.7 = (f32[128,128]{1,0:T(8,128)S(1)}, f32[128,128]{1,0:T(8,128)}, u32[]{:S(2)}) copy-start(f32[128,128]{1,0:T(8,128)} %refs_1_.1) | copy-start | bytes 196612
  101.9 24.8 %all-to-all-start.3 = ((bf16[32,48,128]{2,1,0:T(8,128)(2,1)}), bf16[32,48,128]{2,1,0:T(8,128)(2,1)S(1)}, u32[]{:S(2)}, u32[]{:S(2)}) async-start(bf16[32,48,128]{2,1,0:T(8,128)(2,1)} %bitcast.9), calls=%async_computation.3 | async-start | bytes 786432 | tf_op jit(solution)/shard_map/all_to_all | solution.py:224
  126.7 1.1 copy-start.3
  127.8 1.1 copy-start.4
  128.9 0.8 copy-start.8
  129.7 0.8 copy-start.9
Sparse Core Ops, SparseCore 0:
  20.4 45.3 all-gather.1

commit v4 on v3

--- a/solution.py
+++ b/solution.py
@@ -55,43 +55,41 @@
         spread_ref[x] = jnp.concatenate(parts + padding, axis=1)
 
 
-def sums_kernel(scalars_ref, target_ref, grads_ref, *refs, chunks, tiles, owners, slots):
-    pairs = [(refs[2 * n], refs[2 * n + 1]) for n in range(len(chunks))]
-    slots_ref, sums, places = refs[2 * len(chunks) :]
+def sums_kernel(scalars_ref, target_ref, grads_ref, *refs, steps_x, tiles, owners, slots):
+    pairs = [(refs[2 * n], refs[2 * n + 1]) for n in range(len(steps_x))]
+    slots_ref, sums, places = refs[2 * len(steps_x) :]
     selected, flip, at_x = scalars_ref[0], scalars_ref[1], scalars_ref[2]
     groups, group_rows, width = sums.shape
     tokens = pairs[0][0].shape[2]
     lanes = TILE // groups
-    lane = lax.broadcasted_iota(jnp.int32, (group_rows, width), 1)
-    kept = lane // lanes == selected
     half = group_rows // 2
-    for g in range(groups):
-        total = jnp.zeros((group_rows, width), jnp.float32)
-        for (step_x, first_y), (mine_ref, other_ref) in zip(chunks, pairs):
-            x = lax.rem(at_x + step_x, groups)
-
-            def step(j, total, x=x, first_y=first_y, mine_ref=mine_ref, other_ref=other_ref):
-                for u in range(4):
-                    y = j * 4 + u
-                    rows = jnp.concatenate(
-                        [ref[y, g * half : (g + 1) * half, :] for ref in (mine_ref, other_ref)],
-                        axis=0,
-                    )
-                    place = ((first_y + y) * groups + x) * tokens
-                    partial = jnp.dot(
-                        rows,
-                        grads_ref[pl.ds(pl.multiple_of(place, tokens), tokens), :],
-                        preferred_element_type=jnp.float32,
-                    )
-                    rounded = partial.astype(jnp.bfloat16).astype(jnp.float32)
-                    total = total + jnp.where(kept, partial, rounded)
-                return total
-
-            total = lax.fori_loop(0, mine_ref.shape[0] // 4, step, total)
-        sums[g] = total
-
+
+    @pl.when(pl.program_id(0) == 0)
+    def _():
+        sums[...] = jnp.zeros_like(sums)
+
+    kept = lax.broadcasted_iota(jnp.int32, (group_rows, width), 1) // lanes == selected
+    for step_x, pair in zip(steps_x, pairs):
+        x = lax.rem(at_x + step_x, groups)
+        grads = grads_ref[pl.ds(pl.multiple_of(x * tokens, tokens), tokens), :]
+        for g in range(groups):
+            rows = [ref[0, g * half : (g + 1) * half, :] for ref in pair]
+            partial = jnp.dot(
+                jnp.concatenate(rows, axis=0), grads, preferred_element_type=jnp.float32
+            )
+            rounded = partial.astype(jnp.bfloat16).astype(jnp.float32)
+            sums[g] = sums[g] + jnp.where(kept, partial, rounded)
+
+    @pl.when(pl.program_id(0) == pl.num_programs(0) - 1)
+    def _():
+        place_parts(selected, flip, target_ref, sums, places, slots_ref, tiles, owners, slots)
+
+
+def place_parts(selected, flip, target_ref, sums, places, slots_ref, tiles, owners, slots):
+    groups = sums.shape[0]
+    lanes = TILE // groups
+    part = slots_ref.shape[1]
     places[...] = jnp.zeros_like(places)
-    part = slots_ref.shape[1]
     for tile in range(tiles):
         rest = tile - (tile > selected).astype(jnp.int32)
         held = jnp.concatenate([lane_groups(sums[g], tile, lanes) for g in range(groups)], axis=1)
@@ -112,13 +110,20 @@
 
 
 def owner_kernel(received_ref, *refs, size_x, size_y, part):
-    sel_in, off_in, sel_out, off_out = refs[:3], refs[3:6], refs[6:9], refs[9:12]
-    grads = refs[12]
+    states, outs, grads = refs[:6], refs[6:12], refs[12]
+    held, new, parts, arrived, sent = refs[13:19], refs[19:25], refs[25], refs[26], refs[27]
+    fetch = pltpu.make_async_copy(received_ref, parts, arrived.at[6])
+    fetch.start()
+    loads = [pltpu.make_async_copy(states[n], held[n], arrived.at[n]) for n in range(6)]
+    stores = [pltpu.make_async_copy(new[n], outs[n], sent.at[n]) for n in range(6)]
+    for load in loads:
+        load.start()
     slots = grads.shape[0]
     capacity = slots - 3
     lanes = TILE // size_x
     rows = received_ref.shape[0] // size_x
-    sources = [received_ref[pl.ds(x * rows, rows), :].astype(jnp.float32) for x in range(size_x)]
+    fetch.wait()
+    sources = [parts[pl.ds(x * rows, rows), :].astype(jnp.float32) for x in range(size_x)]
     for g in range(size_x):
         whole = jnp.concatenate([lane_groups(source, g, lanes) for source in sources], axis=1)
         for y in range(size_y):
@@ -126,12 +131,18 @@
                 row = (y * slots + n) * part
                 place = (y * size_x + g) * part
                 grads[n, place : place + part, :] = whole[row : row + part, :]
+    for load in loads:
+        load.wait()
     sel_sum = grads[capacity] + grads[capacity + 1] + grads[capacity + 2]
-    for ref, new in zip(sel_out, adam_update(*(ref[...] for ref in sel_in), sel_sum)):
-        ref[...] = new
+    for ref, value in zip(new[:3], adam_update(*(ref[...] for ref in held[:3]), sel_sum)):
+        ref[...] = value
     for n in range(capacity):
-        for ref, new in zip(off_out, adam_update(*(ref[n] for ref in off_in), grads[n])):
-            ref[n] = new
+        for ref, value in zip(new[3:], adam_update(*(ref[n] for ref in held[3:]), grads[n])):
+            ref[n] = value
+    for store in stores:
+        store.start()
+    for store in stores:
+        store.wait()
 
 
 def shift(array, axis, by):
@@ -181,15 +192,13 @@
     halved = halved.T.reshape(group_size // 2, size_y, size_x, part, tokens_here)
     halved = jnp.transpose(halved, (1, 2, 0, 3, 4)).reshape(size_y, -1, tokens_here)
     own = lax.all_to_all(halved, DP[1], split_axis=0, concat_axis=0, tiled=True)
-    left, right = shift(own, DP[0], 1), shift(own, DP[0], -1)
-    half_y = size_y // 2
-    far_low, far_high = shift(left[:half_y], DP[0], 1), shift(right[half_y:], DP[0], -1)
+    steps_x = [0, size_x - 1, 1, 2]
     swap = [(i, i ^ 1) for i in range(lax.axis_size("tensor"))]
-    chunks = [(0, 0), (size_x - 1, 0), (1, 0), (2, 0), (2, half_y)]
     acts_rows = []
-    for array in (own, left, right, far_low, far_high):
+    for array in (own, shift(own, DP[0], 1), shift(own, DP[0], -1), shift(own, DP[0], 2)):
         acts_rows += [array, lax.ppermute(array, "tensor", swap)]
 
+    acts, grad_out, _ = lax.optimization_barrier((acts, grad_out, own))
     gram = lax.dot_general(acts, acts, (((1,), (1,)), ((), ())), preferred_element_type=jnp.float32)
     grad_wide = grad_out.astype(jnp.float32)
     squares = jnp.sum(grad_wide * jnp.dot(gram, grad_wide, precision=lax.Precision.HIGHEST), axis=0)
@@ -201,12 +210,16 @@
     target = target.reshape(tiles_here - 1, 2, group_size // 2)
     target = jnp.where(core == 0, target, target[:, ::-1]).reshape(-1)
     scalars = jnp.stack([selected[0, 0], core, at_x]).astype(jnp.int32)
+    rows_spec = pl.BlockSpec((1, size_x * row_block // 2, tokens_here), lambda y: (y, 0, 0))
     outgoing = pl.pallas_call(
         lambda *refs: sums_kernel(
-            *refs, chunks=chunks, tiles=tiles_here, owners=group_size, slots=slots
+            *refs, steps_x=steps_x, tiles=tiles_here, owners=group_size, slots=slots
         ),
-        in_specs=[small] * 2 + [whole] * 11,
-        out_specs=whole,
+        grid=(size_y,),
+        in_specs=[small] * 2
+        + [pl.BlockSpec((size_x * tokens_here, width), lambda y: (y, 0))]
+        + [rows_spec] * len(acts_rows),
+        out_specs=pl.BlockSpec((group_size * slots, part, TILE), lambda y: (0, 0, 0)),
         out_shape=jax.ShapeDtypeStruct((group_size * slots, part, TILE), jnp.bfloat16),
         scratch_shapes=[
             pltpu.VMEM((size_x, row_block, width), jnp.float32),
@@ -217,7 +230,7 @@
             bytes_accessed=2 * group_size * tokens_here * (size_x * row_block + width),
             transcendentals=0,
         ),
-        compiler_params=pltpu.CompilerParams(vmem_limit_bytes=32 << 20),
+        compiler_params=pltpu.CompilerParams(vmem_limit_bytes=56 << 20),
         name="replica_sums",
     )(scalars, target, grads, *acts_rows)
 
@@ -225,14 +238,18 @@
         outgoing.reshape(group_size, slots * part, TILE), DP, split_axis=0, concat_axis=0, tiled=True
     )
     block = (row_block, TILE)
+    states = [block] * 3 + [(capacity, *block)] * 3
+    anywhere = pl.BlockSpec(memory_space=pl.ANY)
     outs = pl.pallas_call(
         lambda *refs: owner_kernel(*refs, size_x=size_x, size_y=size_y, part=part),
-        in_specs=[whole] * 7,
-        out_specs=[whole] * 6,
-        out_shape=[jax.ShapeDtypeStruct(block, jnp.float32)] * 3
-        + [jax.ShapeDtypeStruct((capacity, *block), jnp.float32)] * 3,
-        scratch_shapes=[pltpu.VMEM((slots, *block), jnp.float32)],
-        compiler_params=pltpu.CompilerParams(vmem_limit_bytes=24 << 20),
+        in_specs=[anywhere] * 7,
+        out_specs=[anywhere] * 6,
+        out_shape=[jax.ShapeDtypeStruct(state, jnp.float32) for state in states],
+        scratch_shapes=[pltpu.VMEM((slots, *block), jnp.float32)]
+        + [pltpu.VMEM(state, jnp.float32) for state in states] * 2
+        + [pltpu.VMEM((group_size * slots * part, TILE), jnp.bfloat16)]
+        + [pltpu.SemaphoreType.DMA((7,)), pltpu.SemaphoreType.DMA((6,))],
+        compiler_params=pltpu.CompilerParams(vmem_limit_bytes=56 << 20),
         name="owner_adam",
     )(
         received.reshape(-1, TILE),

time: 141 us -> 131 us (0.929)
  local copies, waits for them, and re-layouts: 10.9 us -> 3.51 us
  starting transfers between devices: 38.6 us -> 34.8 us
  waiting for transfers between devices: 21.5 us -> 24.2 us
    unnamed x25 -> x17, local copies, waits for them, and re-layouts: 7.52 us -> 1.05 us
    ppermute x4 -> x3, starting transfers between devices: 14.2 us -> 8.96 us  [shift(): lax.ppermute(array, axis, [(i, (i + by) % size) for i in range(size)])]
    all_to_all x1, starting transfers between devices: 4.34 us -> 7.83 us  [body(): lax.all_to_all(copies, DP, split_axis=0, concat_axis=0, tiled=True)]
    ppermute x4 -> x3, waiting for transfers between devices: 7.47 us -> 10.2 us  [shift(): lax.ppermute(array, axis, [(i, (i + by) % size) for i in range(size)])]
    ppermute x5 -> x4, starting transfers between devices: 10.6 us -> 8.16 us  [body(): acts_rows += [array, lax.ppermute(array, 'tensor', swap)]]
    slice x2 -> x0, local copies, waits for them, and re-layouts: 1.44 us -> none  [the longest x1 0.72 us: body(): right[half_y:]]
  transfers between devices with their start and end apart: 12 -> 10, of which waited for: 3 -> 2; matrix products, arithmetic and copies ran while one was open for 4% -> 3% of each run, Pallas kernels for 7% -> 7%
where the time goes in v4:
time: 131 us
  blocking collectives  37.3 us (28%)
  starting transfers between devices  34.8 us (27%)
  waiting for transfers between devices  24.2 us (18%)
  between operations  15 us (11%)
  Pallas kernels  14.1 us (11%)
  local copies, waits for them, and re-layouts  3.51 us (3%)
    all_to_all x1, blocking collectives, body(): own = lax.all_to_all(halved, DP[1], split_axis=0, concat_axis=0, tiled=True)  26.2 us
    all_to_all x1, waiting for transfers between devices, body(): lax.all_to_all(outgoing.reshape(group_size, slots * part, TILE), DP, spli...  13.9 us
    all_to_all x1, blocking collectives, body(): lax.all_to_all(spread, DP[0], split_axis=0, concat_axis=0, tiled=True)  11.1 us
    ppermute x3, waiting for transfers between devices, shift(): lax.ppermute(array, axis, [(i, (i + by) % size) for i in range(size)])  10.2 us
    all_to_all x1, starting transfers between devices, body(): lax.all_to_all(outgoing.reshape(group_size, slots * part, TILE), DP, spli...  9.8 us
    ppermute x3, starting transfers between devices, shift(): lax.ppermute(array, axis, [(i, (i + by) % size) for i in range(size)])  8.96 us
    pallas_call x1, Pallas kernels, body(): pl.pallas_call(lambda *refs: sums_kernel(*refs, steps_x=steps_x, tiles=ti...  8.65 us
    ppermute x4, starting transfers between devices, body(): acts_rows += [array, lax.ppermute(array, 'tensor', swap)]  8.16 us
  transfers between devices with their start and end apart: 10, of which 2 were waited for; matrix products, arithmetic and copies ran while one was open for 3% of the time, Pallas kernels for 7%

profile of v4, /device:TPU:456, one launch (start us, length us, event | category | flops | bytes accessed | tf_op | source)
XLA Modules:
  0.0 130.6 jit_solution(7027727703305219555)
XLA Ops:
  7.2 2.0 %spread.1 = bf16[4,128,256]{2,1,0:T(8,128)(2,1)} custom-call(bf16[128,896]{1,0:T(8,128)(2,1)} %grads_ref.1), custom_call_target="tpu_custom_call" | custom-call | tf_op jit(solution)/shard_map/spread/pallas_call | solution.py:181
  9.2 11.1 %all_to_all.20 = bf16[4,128,256]{2,1,0:T(8,128)(2,1)} all-to-all(bf16[4,128,256]{2,1,0:T(8,128)(2,1)} %spread.1), channel_id=1, replica_groups=mesh['dp_0'=4,'dp_1'=8,'tensor'=16] {'dp_0'}, dimensions={0} | all-to-all | bytes 524288 | tf_op jit(solution)/shard_map/all_to_all | solution.py:188
  20.4 0.3 copy.26
  20.9 26.2 %all_to_all.21.refs_3_ = bf16[8,256,128]{2,1,0:T(8,128)(2,1)S(1)} all-to-all(bf16[8,256,128]{2,1,0:T(8,128)(2,1)S(1)} %bitcast.25), channel_id=1, replica_groups=mesh['dp_0'=4,'dp_1'=8,'tensor'=16] {'dp_1'}, dimensions={0} | all-to-all | bytes 1048576 | tf_op jit(solution)/shard_map/all_to_all | solution.py:194
  47.2 2.2 %collective-permute-start.1 = (bf16[8,256,128]{2,1,0:T(8,128)(2,1)S(1)}, bf16[8,256,128]{2,1,0:T(8,128)(2,1)S(1)}, u32[]{:S(2)}, u32[]{:S(2)}) collective-permute-start(bf16[8,256,128]{2,1,0:T(8,128)(2,1)S(1)} %all_to_all.21.refs_3_), channel_id=1, source_target_pairs={{0,128},{128,256},{256,384},{384,0},{1,129},{129,257},{257,385},{3... | collective-permute-start | bytes 1572872 | tf_op jit(solution)/shard_map/ppermute | solution.py:150
  49.4 4.8 %collective-permute-start.3 = (bf16[8,256,128]{2,1,0:T(8,128)(2,1)S(1)}, bf16[8,256,128]{2,1,0:T(8,128)(2,1)S(1)}, u32[]{:S(2)}, u32[]{:S(2)}) collective-permute-start(bf16[8,256,128]{2,1,0:T(8,128)(2,1)S(1)} %all_to_all.21.refs_3_), channel_id=1, source_target_pairs={{0,384},{128,0},{256,128},{384,256},{1,385},{129,1},{257,129},{385... | collective-permute-start | bytes 1572872 | tf_op jit(solution)/shard_map/ppermute | solution.py:150
  54.2 1.9 %collective-permute-start.5 = (bf16[8,256,128]{2,1,0:T(8,128)(2,1)S(1)}, bf16[8,256,128]{2,1,0:T(8,128)(2,1)S(1)}, u32[]{:S(2)}, u32[]{:S(2)}) collective-permute-start(bf16[8,256,128]{2,1,0:T(8,128)(2,1)S(1)} %all_to_all.21.refs_3_), channel_id=1, source_target_pairs={{0,256},{128,384},{256,0},{384,128},{1,257},{129,385},{257,1},{385... | collective-permute-start | bytes 1572872 | tf_op jit(solution)/shard_map/ppermute | solution.py:150
  56.6 1.9 %collective-permute-start = (bf16[8,256,128]{2,1,0:T(8,128)(2,1)S(1)}, bf16[8,256,128]{2,1,0:T(8,128)(2,1)}, u32[]{:S(2)}, u32[]{:S(2)}) collective-permute-start(bf16[8,256,128]{2,1,0:T(8,128)(2,1)S(1)} %all_to_all.21.refs_3_), channel_id=1, source_target_pairs={{0,1},{1,0},{2,3},{3,2},{4,5},{5,4},{6,7},{7,6},{8,9},{9,8},{10,11... | collective-permute-start | bytes 1572872 | tf_op jit(solution)/shard_map/ppermute | solution.py:199
  58.5 10.2 %collective-permute-done.1.refs_5_ = bf16[8,256,128]{2,1,0:T(8,128)(2,1)S(1)} collective-permute-done((bf16[8,256,128]{2,1,0:T(8,128)(2,1)S(1)}, bf16[8,256,128]{2,1,0:T(8,128)(2,1)S(1)}, u32[]{:S(2)}, u32[]{:S(2)}) %collective-permute-start.1) | collective-permute-done | bytes 524320 | tf_op jit(solution)/shard_map/ppermute | solution.py:150
  68.7 1.9 %collective-permute-start.2 = (bf16[8,256,128]{2,1,0:T(8,128)(2,1)S(1)}, bf16[8,256,128]{2,1,0:T(8,128)(2,1)}, u32[]{:S(2)}, u32[]{:S(2)}) collective-permute-start(bf16[8,256,128]{2,1,0:T(8,128)(2,1)S(1)} %collective-permute-done.1.refs_5_), channel_id=1, source_target_pairs={{0,1},{1,0},{2,3},{3,2},{4,5},{5,4},{6,7},{7,6},{8,9},{9,8},{10,11... | collective-permute-start | bytes 1572872 | tf_op jit(solution)/shard_map/ppermute | solution.py:199
  70.7 2.4 %collective-permute-start.4 = (bf16[8,256,128]{2,1,0:T(8,128)(2,1)S(1)}, bf16[8,256,128]{2,1,0:T(8,128)(2,1)}, u32[]{:S(2)}, u32[]{:S(2)}) collective-permute-start(bf16[8,256,128]{2,1,0:T(8,128)(2,1)S(1)} %collective-permute-done.3.refs_7_), channel_id=1, source_target_pairs={{0,1},{1,0},{2,3},{3,2},{4,5},{5,4},{6,7},{7,6},{8,9},{9,8},{10,11... | collective-permute-start | bytes 1572872 | tf_op jit(solution)/shard_map/ppermute | solution.py:199
  73.1 1.9 %collective-permute-start.6 = (bf16[8,256,128]{2,1,0:T(8,128)(2,1)S(1)}, bf16[8,256,128]{2,1,0:T(8,128)(2,1)}, u32[]{:S(2)}, u32[]{:S(2)}) collective-permute-start(bf16[8,256,128]{2,1,0:T(8,128)(2,1)S(1)} %collective-permute-done.5.refs_9_), channel_id=1, source_target_pairs={{0,1},{1,0},{2,3},{3,2},{4,5},{5,4},{6,7},{7,6},{8,9},{9,8},{10,11... | collective-permute-start | bytes 1572872 | tf_op jit(solution)/shard_map/ppermute | solution.py:199
  75.1 0.4 fusion.2
  75.5 0.4 fusion
  75.9 0.7 broadcast_in_dim.2
  76.6 7.8 %all-to-all-start.1 = ((f32[32,1,896]{2,1,0:T(1,128)}), f32[32,1,896]{2,1,0:T(1,128)S(1)}, u32[]{:S(2)}, u32[]{:S(2)}) async-start(f32[32,1,896]{2,1,0:T(1,128)} %broadcast_in_dim.2), calls=%async_computation.1 | async-start | bytes 229376 | tf_op jit(solution)/shard_map/all_to_all | solution.py:206
  84.4 0.6 reshape.59.refs_1_
  85.7 0.7 pad_add_fusion.refs_0_
  86.5 8.6 %replica_sums.1 = bf16[384,4,128]{2,1,0:T(4,128)(2,1)} custom-call(s32[3]{0:T(128)} %pad_add_fusion.refs_0_, s32[192]{0:T(256)} %reshape.59.refs_1_, bf16[4096,256]{1,0:T(8,128)(2,1)} %all-gather.2.cloned.1.call-done.refs_2_, bf16[8,256,128]{2,1,0:T(8,128)(2,1)} %copy-done.1, bf16[8,256,128]{2,1,0:T(8,128)(2,1)} %collective-permute-done.refs_4_, ...), custom_call_target="tpu_custom_call" | custom-call | flops 1073741824 | bytes 6291456 | tf_op jit(solution)/shard_map/replica_sums/pallas_call | solution.py:214
  95.1 9.8 %all-to-all-start.3 = ((bf16[32,48,128]{2,1,0:T(8,128)(2,1)}), bf16[32,48,128]{2,1,0:T(8,128)(2,1)S(1)}, u32[]{:S(2)}, u32[]{:S(2)}) async-start(bf16[32,48,128]{2,1,0:T(8,128)(2,1)} %bitcast.26), calls=%async_computation.3 | async-start | bytes 786432 | tf_op jit(solution)/shard_map/all_to_all | solution.py:237
  105.0 0.6 sqrt.3
  105.6 13.9 %all-to-all-done.3 = bf16[32,48,128]{2,1,0:T(8,128)(2,1)S(1)} async-done(((bf16[32,48,128]{2,1,0:T(8,128)(2,1)}), bf16[32,48,128]{2,1,0:T(8,128)(2,1)S(1)}, u32[]{:S(2)}, u32[]{:S(2)}) %all-to-all-start.3) | async-done | bytes 393248 | tf_op jit(solution)/shard_map/all_to_all | solution.py:237
  119.5 0.7 copy-done.2
  120.3 3.4 %owner_adam.1 = (f32[128,128]{1,0:T(8,128)}, f32[128,128]{1,0:T(8,128)}, f32[128,128]{1,0:T(8,128)}, f32[9,128,128]{2,1,0:T(8,128)}, f32[9,128,128]{2,1,0:T(8,128)}, /*index=5*/f32[9,128,128]{2,1,0:T(8,128)}) custom-call(bf16[1536,128]{1,0:T(8,128)(2,1)} %bitcast.27, f32[128,128]{1,0:T(8,128)} %refs_1_.1, f32[128,128]{1,0:T(8,128)} %refs_2_.1, ...), custom_call_target="tpu_custom_call" | custom-call | tf_op jit(solution)/shard_map/owner_adam/pallas_call | solution.py:243
  (35 shorter events, 1.0 us)
Async XLA Ops:
  7.2 13.1 %copy-start = (bf16[128,4096]{1,0:T(8,128)(2,1)S(1)}, bf16[128,4096]{1,0:T(8,128)(2,1)}, u32[]{:S(2)}) copy-start(bf16[128,4096]{1,0:T(8,128)(2,1)} %param.10) | copy-start | bytes 3145732
  7.2 79.2 %all-gather.2.cloned.1.call-start = ((), (), s32[]{:S(2)}) async-start(), calls=%async_computation.4 | async-start | bytes 2359296 | tf_op jit(solution)/shard_map/all_gather | solution.py:189
  20.3 35.8 %copy-start.7 = (s32[1,192,1]{1,2,0:T(1,128)S(1)}, s32[1,192,1]{1,2,0:T(1,128)}, u32[]{:S(2)}) copy-start(s32[1,192,1]{1,2,0:T(1,128)} %param.13) | copy-start | bytes 2308
  20.7 54.8 %copy-start.6 = (bf16[128,896]{1,0:T(8,128)(2,1)S(1)}, bf16[128,896]{1,0:T(8,128)(2,1)}, u32[]{:S(2)}) copy-start(bf16[128,896]{1,0:T(8,128)(2,1)} %grads_ref.1) | copy-start | bytes 688132
  47.2 39.3 %copy-start.1 = (bf16[8,256,128]{2,1,0:T(8,128)(2,1)}, bf16[8,256,128]{2,1,0:T(8,128)(2,1)S(1)}, u32[]{:S(2)}) copy-start(bf16[8,256,128]{2,1,0:T(8,128)(2,1)S(1)} %all_to_all.21.refs_3_) | copy-start | bytes 1572868
  47.2 21.6 %collective-permute-start.1 = (bf16[8,256,128]{2,1,0:T(8,128)(2,1)S(1)}, bf16[8,256,128]{2,1,0:T(8,128)(2,1)S(1)}, u32[]{:S(2)}, u32[]{:S(2)}) collective-permute-start(bf16[8,256,128]{2,1,0:T(8,128)(2,1)S(1)} %all_to_all.21.refs_3_), channel_id=1, source_target_pairs={{0,128},{128,256},{256,384},{384,0},{1,129},{129,257},{257,385},{3... | collective-permute-start | bytes 1572872 | tf_op jit(solution)/shard_map/ppermute | solution.py:150
  49.4 21.3 %collective-permute-start.3 = (bf16[8,256,128]{2,1,0:T(8,128)(2,1)S(1)}, bf16[8,256,128]{2,1,0:T(8,128)(2,1)S(1)}, u32[]{:S(2)}, u32[]{:S(2)}) collective-permute-start(bf16[8,256,128]{2,1,0:T(8,128)(2,1)S(1)} %all_to_all.21.refs_3_), channel_id=1, source_target_pairs={{0,384},{128,0},{256,128},{384,256},{1,385},{129,1},{257,129},{385... | collective-permute-start | bytes 1572872 | tf_op jit(solution)/shard_map/ppermute | solution.py:150
  54.2 18.9 %collective-permute-start.5 = (bf16[8,256,128]{2,1,0:T(8,128)(2,1)S(1)}, bf16[8,256,128]{2,1,0:T(8,128)(2,1)S(1)}, u32[]{:S(2)}, u32[]{:S(2)}) collective-permute-start(bf16[8,256,128]{2,1,0:T(8,128)(2,1)S(1)} %all_to_all.21.refs_3_), channel_id=1, source_target_pairs={{0,256},{128,384},{256,0},{384,128},{1,257},{129,385},{257,1},{385... | collective-permute-start | bytes 1572872 | tf_op jit(solution)/shard_map/ppermute | solution.py:150
  56.6 29.8 %collective-permute-start = (bf16[8,256,128]{2,1,0:T(8,128)(2,1)S(1)}, bf16[8,256,128]{2,1,0:T(8,128)(2,1)}, u32[]{:S(2)}, u32[]{:S(2)}) collective-permute-start(bf16[8,256,128]{2,1,0:T(8,128)(2,1)S(1)} %all_to_all.21.refs_3_), channel_id=1, source_target_pairs={{0,1},{1,0},{2,3},{3,2},{4,5},{5,4},{6,7},{7,6},{8,9},{9,8},{10,11... | collective-permute-start | bytes 1572872 | tf_op jit(solution)/shard_map/ppermute | solution.py:199
  68.7 17.7 %copy-start.3 = (bf16[8,256,128]{2,1,0:T(8,128)(2,1)}, bf16[8,256,128]{2,1,0:T(8,128)(2,1)S(1)}, u32[]{:S(2)}) copy-start(bf16[8,256,128]{2,1,0:T(8,128)(2,1)S(1)} %collective-permute-done.1.refs_5_) | copy-start | bytes 1572868
  68.7 17.6 %collective-permute-start.2 = (bf16[8,256,128]{2,1,0:T(8,128)(2,1)S(1)}, bf16[8,256,128]{2,1,0:T(8,128)(2,1)}, u32[]{:S(2)}, u32[]{:S(2)}) collective-permute-start(bf16[8,256,128]{2,1,0:T(8,128)(2,1)S(1)} %collective-permute-done.1.refs_5_), channel_id=1, source_target_pairs={{0,1},{1,0},{2,3},{3,2},{4,5},{5,4},{6,7},{7,6},{8,9},{9,8},{10,11... | collective-permute-start | bytes 1572872 | tf_op jit(solution)/shard_map/ppermute | solution.py:199
  70.7 15.8 %copy-start.4 = (bf16[8,256,128]{2,1,0:T(8,128)(2,1)}, bf16[8,256,128]{2,1,0:T(8,128)(2,1)S(1)}, u32[]{:S(2)}) copy-start(bf16[8,256,128]{2,1,0:T(8,128)(2,1)S(1)} %collective-permute-done.3.refs_7_) | copy-start | bytes 1572868
  70.7 15.7 %collective-permute-start.4 = (bf16[8,256,128]{2,1,0:T(8,128)(2,1)S(1)}, bf16[8,256,128]{2,1,0:T(8,128)(2,1)}, u32[]{:S(2)}, u32[]{:S(2)}) collective-permute-start(bf16[8,256,128]{2,1,0:T(8,128)(2,1)S(1)} %collective-permute-done.3.refs_7_), channel_id=1, source_target_pairs={{0,1},{1,0},{2,3},{3,2},{4,5},{5,4},{6,7},{7,6},{8,9},{9,8},{10,11... | collective-permute-start | bytes 1572872 | tf_op jit(solution)/shard_map/ppermute | solution.py:199
  73.1 13.3 %copy-start.5 = (bf16[8,256,128]{2,1,0:T(8,128)(2,1)}, bf16[8,256,128]{2,1,0:T(8,128)(2,1)S(1)}, u32[]{:S(2)}) copy-start(bf16[8,256,128]{2,1,0:T(8,128)(2,1)S(1)} %collective-permute-done.5.refs_9_) | copy-start | bytes 1572868
  73.1 13.3 %collective-permute-start.6 = (bf16[8,256,128]{2,1,0:T(8,128)(2,1)S(1)}, bf16[8,256,128]{2,1,0:T(8,128)(2,1)}, u32[]{:S(2)}, u32[]{:S(2)}) collective-permute-start(bf16[8,256,128]{2,1,0:T(8,128)(2,1)S(1)} %collective-permute-done.5.refs_9_), channel_id=1, source_target_pairs={{0,1},{1,0},{2,3},{3,2},{4,5},{5,4},{6,7},{7,6},{8,9},{9,8},{10,11... | collective-permute-start | bytes 1572872 | tf_op jit(solution)/shard_map/ppermute | solution.py:199
  76.6 18.5 %all-to-all-start.1 = ((f32[32,1,896]{2,1,0:T(1,128)}), f32[32,1,896]{2,1,0:T(1,128)S(1)}, u32[]{:S(2)}, u32[]{:S(2)}) async-start(f32[32,1,896]{2,1,0:T(1,128)} %broadcast_in_dim.2), calls=%async_computation.1 | async-start | bytes 229376 | tf_op jit(solution)/shard_map/all_to_all | solution.py:206
  95.1 24.4 %all-to-all-start.3 = ((bf16[32,48,128]{2,1,0:T(8,128)(2,1)}), bf16[32,48,128]{2,1,0:T(8,128)(2,1)S(1)}, u32[]{:S(2)}, u32[]{:S(2)}) async-start(bf16[32,48,128]{2,1,0:T(8,128)(2,1)} %bitcast.26), calls=%async_computation.3 | async-start | bytes 786432 | tf_op jit(solution)/shard_map/all_to_all | solution.py:237
  119.5 0.7 copy-start.2
Sparse Core Ops, SparseCore 0:
  20.4 45.3 all-gather.1

commit v5 on v4

--- a/solution.py
+++ b/solution.py
@@ -57,7 +57,7 @@
 
 def sums_kernel(scalars_ref, target_ref, grads_ref, *refs, steps_x, tiles, owners, slots):
     pairs = [(refs[2 * n], refs[2 * n + 1]) for n in range(len(steps_x))]
-    slots_ref, sums, places = refs[2 * len(steps_x) :]
+    slots_ref, sums, squares, places = refs[2 * len(steps_x) :]
     selected, flip, at_x = scalars_ref[0], scalars_ref[1], scalars_ref[2]
     groups, group_rows, width = sums.shape
     tokens = pairs[0][0].shape[2]
@@ -67,25 +67,37 @@
     @pl.when(pl.program_id(0) == 0)
     def _():
         sums[...] = jnp.zeros_like(sums)
+        squares[...] = jnp.zeros_like(squares)
 
     kept = lax.broadcasted_iota(jnp.int32, (group_rows, width), 1) // lanes == selected
-    for step_x, pair in zip(steps_x, pairs):
-        x = lax.rem(at_x + step_x, groups)
-        grads = grads_ref[pl.ds(pl.multiple_of(x * tokens, tokens), tokens), :]
-        for g in range(groups):
+    column_squares = squares[...]
+    for g in range(groups):
+        total = sums[g]
+        for step_x, pair in zip(steps_x, pairs):
+            x = lax.rem(at_x + step_x, groups)
             rows = [ref[0, g * half : (g + 1) * half, :] for ref in pair]
             partial = jnp.dot(
-                jnp.concatenate(rows, axis=0), grads, preferred_element_type=jnp.float32
+                jnp.concatenate(rows, axis=0),
+                grads_ref[pl.ds(pl.multiple_of(x * tokens, tokens), tokens), :],
+                preferred_element_type=jnp.float32,
             )
             rounded = partial.astype(jnp.bfloat16).astype(jnp.float32)
-            sums[g] = sums[g] + jnp.where(kept, partial, rounded)
+            total = total + jnp.where(kept, partial, rounded)
+            squared = (partial * partial).reshape(-1, *column_squares.shape)
+            column_squares = column_squares + squared.sum(axis=0)
+        sums[g] = total
+    squares[...] = column_squares
 
     @pl.when(pl.program_id(0) == pl.num_programs(0) - 1)
     def _():
-        place_parts(selected, flip, target_ref, sums, places, slots_ref, tiles, owners, slots)
-
-
-def place_parts(selected, flip, target_ref, sums, places, slots_ref, tiles, owners, slots):
+        place_parts(
+            selected, flip, target_ref, sums, column_squares, places, slots_ref, tiles, owners, slots
+        )
+
+
+def place_parts(
+    selected, flip, target_ref, sums, column_squares, places, slots_ref, tiles, owners, slots
+):
     groups = sums.shape[0]
     lanes = TILE // groups
     part = slots_ref.shape[1]
@@ -104,22 +116,32 @@
             for q in range(owners):
                 owner = jnp.bitwise_xor(q, flip * (owners // 2))
                 for n, term in enumerate(split_three(held[q * part : (q + 1) * part, :])):
-                    places[owner * slots + slots - 3 + n] = term
+                    places[owner * slots + slots - 5 + n] = term
+
+    terms = []
+    for term in split_three(jnp.sum(column_squares, axis=0, keepdims=True)):
+        terms += [term[:, :TILE], term[:, TILE:]]
+    terms += [jnp.zeros_like(terms[0])] * 2
+    for n in range(2):
+        rows = jnp.concatenate(terms[n * part : (n + 1) * part], axis=0)
+        for q in range(owners):
+            places[q * slots + slots - 2 + n] = rows
 
     slots_ref[...] = places[...].astype(slots_ref.dtype)
 
 
 def owner_kernel(received_ref, *refs, size_x, size_y, part):
-    states, outs, grads = refs[:6], refs[6:12], refs[12]
-    held, new, parts, arrived, sent = refs[13:19], refs[19:25], refs[25], refs[26], refs[27]
+    states, outs, norms_ref, grads = refs[:6], refs[6:12], refs[12], refs[13]
+    held, new, parts, arrived, sent = refs[14:20], refs[20:26], refs[26], refs[27], refs[28]
     fetch = pltpu.make_async_copy(received_ref, parts, arrived.at[6])
     fetch.start()
     loads = [pltpu.make_async_copy(states[n], held[n], arrived.at[n]) for n in range(6)]
     stores = [pltpu.make_async_copy(new[n], outs[n], sent.at[n]) for n in range(6)]
     for load in loads:
         load.start()
-    slots = grads.shape[0]
-    capacity = slots - 3
+    used = grads.shape[0]
+    capacity = used - 3
+    slots = used + 2
     lanes = TILE // size_x
     rows = received_ref.shape[0] // size_x
     fetch.wait()
@@ -127,10 +149,19 @@
     for g in range(size_x):
         whole = jnp.concatenate([lane_groups(source, g, lanes) for source in sources], axis=1)
         for y in range(size_y):
-            for n in range(slots):
+            for n in range(used):
                 row = (y * slots + n) * part
                 place = (y * size_x + g) * part
                 grads[n, place : place + part, :] = whole[row : row + part, :]
+    norms = []
+    for source in sources:
+        rows = sum(source[(y * slots + used) * part :][: 2 * part] for y in range(size_y))
+        norms.append(jnp.sqrt(rows[0:2] + rows[2:4] + rows[4:6]))
+    for tile in range(norms_ref.shape[0]):
+        row, group = divmod(tile, size_x)
+        norms_ref[tile : tile + 1, :] = jnp.concatenate(
+            [lane_groups(norm[row : row + 1], group, lanes) for norm in norms], axis=1
+        )
     for load in loads:
         load.wait()
     sel_sum = grads[capacity] + grads[capacity + 1] + grads[capacity + 2]
@@ -172,7 +203,7 @@
     row_block = rows_all // group_size
     part = row_block // group_size
     capacity = off_weight.shape[2]
-    slots = capacity + 3
+    slots = capacity + 5
     owner_row = owner[0, :, 0]
     width = 2 * TILE
     whole = pl.BlockSpec(memory_space=pltpu.VMEM)
@@ -193,23 +224,16 @@
     halved = jnp.transpose(halved, (1, 2, 0, 3, 4)).reshape(size_y, -1, tokens_here)
     own = lax.all_to_all(halved, DP[1], split_axis=0, concat_axis=0, tiled=True)
     steps_x = [0, size_x - 1, 1, 2]
-    swap = [(i, i ^ 1) for i in range(lax.axis_size("tensor"))]
-    acts_rows = []
-    for array in (own, shift(own, DP[0], 1), shift(own, DP[0], -1), shift(own, DP[0], 2)):
-        acts_rows += [array, lax.ppermute(array, "tensor", swap)]
-
-    acts, grad_out, _ = lax.optimization_barrier((acts, grad_out, own))
-    gram = lax.dot_general(acts, acts, (((1,), (1,)), ((), ())), preferred_element_type=jnp.float32)
-    grad_wide = grad_out.astype(jnp.float32)
-    squares = jnp.sum(grad_wide * jnp.dot(gram, grad_wide, precision=lax.Precision.HIGHEST), axis=0)
-    copies = jnp.broadcast_to(squares, (group_size, 1, cols_here))
-    squares = lax.all_to_all(copies, DP, split_axis=0, concat_axis=0, tiled=True)
-    column_norm = jnp.sqrt(squares.sum(axis=(0, 1)))
-
+    left = shift(own, DP[0], 1)
     target = owner_row * slots + slot_numbers(owner_row)
     target = target.reshape(tiles_here - 1, 2, group_size // 2)
     target = jnp.where(core == 0, target, target[:, ::-1]).reshape(-1)
     scalars = jnp.stack([selected[0, 0], core, at_x]).astype(jnp.int32)
+    left, target, scalars = lax.optimization_barrier((left, target, scalars))
+    swap = [(i, i ^ 1) for i in range(lax.axis_size("tensor"))]
+    acts_rows = []
+    for array in (own, left, shift(own, DP[0], -1), shift(own, DP[0], 2)):
+        acts_rows += [array, lax.ppermute(array, "tensor", swap)]
     rows_spec = pl.BlockSpec((1, size_x * row_block // 2, tokens_here), lambda y: (y, 0, 0))
     outgoing = pl.pallas_call(
         lambda *refs: sums_kernel(
@@ -223,6 +247,7 @@
         out_shape=jax.ShapeDtypeStruct((group_size * slots, part, TILE), jnp.bfloat16),
         scratch_shapes=[
             pltpu.VMEM((size_x, row_block, width), jnp.float32),
+            pltpu.VMEM((8, width), jnp.float32),
             pltpu.VMEM((group_size * slots, part, TILE), jnp.float32),
         ],
         cost_estimate=pl.CostEstimate(
@@ -243,9 +268,10 @@
     outs = pl.pallas_call(
         lambda *refs: owner_kernel(*refs, size_x=size_x, size_y=size_y, part=part),
         in_specs=[anywhere] * 7,
-        out_specs=[anywhere] * 6,
-        out_shape=[jax.ShapeDtypeStruct(state, jnp.float32) for state in states],
-        scratch_shapes=[pltpu.VMEM((slots, *block), jnp.float32)]
+        out_specs=[anywhere] * 6 + [whole],
+        out_shape=[jax.ShapeDtypeStruct(state, jnp.float32) for state in states]
+        + [jax.ShapeDtypeStruct((tiles_here, TILE), jnp.float32)],
+        scratch_shapes=[pltpu.VMEM((capacity + 3, *block), jnp.float32)]
         + [pltpu.VMEM(state, jnp.float32) for state in states] * 2
         + [pltpu.VMEM((group_size * slots * part, TILE), jnp.bfloat16)]
         + [pltpu.SemaphoreType.DMA((7,)), pltpu.SemaphoreType.DMA((6,))],
@@ -258,7 +284,8 @@
         sel_second,
         *(state.reshape(capacity, *block) for state in (off_weight, off_moment, off_second)),
     )
-    return (column_norm, *outs[:3], *(new.reshape(off_weight.shape) for new in outs[3:]))
+    off_new = [new.reshape(off_weight.shape) for new in outs[3:6]]
+    return (outs[6].reshape(-1), *outs[:3], *off_new)
 
 
 def solution(mesh):

time: 131 us -> 123 us (0.939)
  starting transfers between devices: 34.8 us -> 24.5 us
  waiting for transfers between devices: 24.2 us -> 27.1 us
    all_to_all x2 -> x1, starting transfers between devices: 17.6 us -> 7.55 us  [body(): own = lax.all_to_all(halved, DP[1], split_axis=0, concat_axis=0, tiled=True)]
    all_to_all x2 -> x1, waiting for transfers between devices: 13.9 us -> 18.8 us  [body(): own = lax.all_to_all(halved, DP[1], split_axis=0, concat_axis=0, tiled=True)]
    ppermute x3, waiting for transfers between devices: 10.2 us -> 8.14 us  [shift(): lax.ppermute(array, axis, [(i, (i + by) % size) for i in range(size)])]
  transfers between devices with their start and end apart: 10 -> 9, of which waited for: 2 -> 3; matrix products, arithmetic and copies ran while one was open for 3% -> 3% of each run, Pallas kernels for 7% -> 0%
where the time goes in v5:
time: 123 us
  blocking collectives  36 us (29%)
  waiting for transfers between devices  27.1 us (22%)
  starting transfers between devices  24.5 us (20%)
  Pallas kernels  15.4 us (13%)
  between operations  14.9 us (12%)
  local copies, waits for them, and re-layouts  4.01 us (3%)
    all_to_all x1, blocking collectives, body(): lax.all_to_all(outgoing.reshape(group_size, slots * part, TILE), DP, spli...  24.9 us
    all_to_all x1, waiting for transfers between devices, body(): own = lax.all_to_all(halved, DP[1], split_axis=0, concat_axis=0, tiled=True)  18.8 us
    all_to_all x1, blocking collectives, body(): lax.all_to_all(spread, DP[0], split_axis=0, concat_axis=0, tiled=True)  11.1 us
    pallas_call x1, Pallas kernels, body(): pl.pallas_call(lambda *refs: sums_kernel(*refs, steps_x=steps_x, tiles=ti...  9.34 us
    ppermute x3, starting transfers between devices, shift(): lax.ppermute(array, axis, [(i, (i + by) % size) for i in range(size)])  8.75 us
    ppermute x4, starting transfers between devices, body(): acts_rows += [array, lax.ppermute(array, 'tensor', swap)]  8.15 us
    ppermute x3, waiting for transfers between devices, shift(): lax.ppermute(array, axis, [(i, (i + by) % size) for i in range(size)])  8.14 us
    all_to_all x1, starting transfers between devices, body(): own = lax.all_to_all(halved, DP[1], split_axis=0, concat_axis=0, tiled=True)  7.55 us
  transfers between devices with their start and end apart: 9, of which 3 were waited for; matrix products, arithmetic and copies ran while one was open for 3% of the time, Pallas kernels for 0%

profile of v5, /device:TPU:456, one launch (start us, length us, event | category | flops | bytes accessed | tf_op | source)
XLA Modules:
  0.0 122.7 jit_solution(12566840884700997626)
XLA Ops:
  7.2 2.0 %spread.1 = bf16[4,128,256]{2,1,0:T(8,128)(2,1)} custom-call(bf16[128,896]{1,0:T(8,128)(2,1)} %grads_ref.1), custom_call_target="tpu_custom_call" | custom-call | tf_op jit(solution)/shard_map/spread/pallas_call | solution.py:212
  9.2 11.1 %all_to_all.15 = bf16[4,128,256]{2,1,0:T(8,128)(2,1)} all-to-all(bf16[4,128,256]{2,1,0:T(8,128)(2,1)} %spread.1), channel_id=1, replica_groups=mesh['dp_0'=4,'dp_1'=8,'tensor'=16] {'dp_0'}, dimensions={0} | all-to-all | bytes 524288 | tf_op jit(solution)/shard_map/all_to_all | solution.py:219
  20.4 0.3 copy.22
  20.7 1.1 copy.21
  21.7 7.5 %all-to-all-start = ((bf16[8,256,128]{2,1,0:T(8,128)(2,1)}), bf16[8,256,128]{2,1,0:T(8,128)(2,1)S(1)}, u32[]{:S(2)}, u32[]{:S(2)}) async-start(bf16[8,256,128]{2,1,0:T(8,128)(2,1)} %bitcast.3), calls=%async_computation | async-start | bytes 1048576 | tf_op jit(solution)/shard_map/all_to_all | solution.py:225
  29.9 18.8 %all-to-all-done.refs_3_ = bf16[8,256,128]{2,1,0:T(8,128)(2,1)S(1)} async-done(((bf16[8,256,128]{2,1,0:T(8,128)(2,1)}), bf16[8,256,128]{2,1,0:T(8,128)(2,1)S(1)}, u32[]{:S(2)}, u32[]{:S(2)}) %all-to-all-start) | async-done | bytes 524320 | tf_op jit(solution)/shard_map/all_to_all | solution.py:225
  48.7 2.3 %collective-permute-start.5 = (bf16[8,256,128]{2,1,0:T(8,128)(2,1)S(1)}, bf16[8,256,128]{2,1,0:T(8,128)(2,1)S(1)}, u32[]{:S(2)}, u32[]{:S(2)}) collective-permute-start(bf16[8,256,128]{2,1,0:T(8,128)(2,1)S(1)} %all-to-all-done.refs_3_), channel_id=1, source_target_pairs={{0,256},{128,384},{256,0},{384,128},{1,257},{129,385},{257,1},{385... | collective-permute-start | bytes 1572872 | tf_op jit(solution)/shard_map/ppermute | solution.py:181
  51.0 4.6 %collective-permute-start.3 = (bf16[8,256,128]{2,1,0:T(8,128)(2,1)S(1)}, bf16[8,256,128]{2,1,0:T(8,128)(2,1)S(1)}, u32[]{:S(2)}, u32[]{:S(2)}) collective-permute-start(bf16[8,256,128]{2,1,0:T(8,128)(2,1)S(1)} %all-to-all-done.refs_3_), channel_id=1, source_target_pairs={{0,384},{128,0},{256,128},{384,256},{1,385},{129,1},{257,129},{385... | collective-permute-start | bytes 1572872 | tf_op jit(solution)/shard_map/ppermute | solution.py:181
  55.5 1.9 %collective-permute-start = (bf16[8,256,128]{2,1,0:T(8,128)(2,1)S(1)}, bf16[8,256,128]{2,1,0:T(8,128)(2,1)S(1)}, u32[]{:S(2)}, u32[]{:S(2)}) collective-permute-start(bf16[8,256,128]{2,1,0:T(8,128)(2,1)S(1)} %all-to-all-done.refs_3_), channel_id=1, source_target_pairs={{0,128},{128,256},{256,384},{384,0},{1,129},{129,257},{257,385},{3... | collective-permute-start | bytes 1572872 | tf_op jit(solution)/shard_map/ppermute | solution.py:181
  57.6 0.2 convert_reduce_fusion
  57.9 0.7 reshape.62.refs_1_
  58.6 0.6 pad_add_fusion.refs_0_
  59.2 1.9 %collective-permute-start.1 = (bf16[8,256,128]{2,1,0:T(8,128)(2,1)S(1)}, bf16[8,256,128]{2,1,0:T(8,128)(2,1)S(1)}, u32[]{:S(2)}, u32[]{:S(2)}) collective-permute-start(bf16[8,256,128]{2,1,0:T(8,128)(2,1)S(1)} %all-to-all-done.refs_3_), channel_id=1, source_target_pairs={{0,1},{1,0},{2,3},{3,2},{4,5},{5,4},{6,7},{7,6},{8,9},{9,8},{10,11... | collective-permute-start | bytes 1572872 | tf_op jit(solution)/shard_map/ppermute | solution.py:236
  61.1 8.1 %collective-permute-done.refs_5_ = bf16[8,256,128]{2,1,0:T(8,128)(2,1)S(1)} collective-permute-done((bf16[8,256,128]{2,1,0:T(8,128)(2,1)S(1)}, bf16[8,256,128]{2,1,0:T(8,128)(2,1)S(1)}, u32[]{:S(2)}, u32[]{:S(2)}) %collective-permute-start) | collective-permute-done | bytes 524320 | tf_op jit(solution)/shard_map/ppermute | solution.py:181
  69.2 1.9 %collective-permute-start.6 = (bf16[8,256,128]{2,1,0:T(8,128)(2,1)S(1)}, bf16[8,256,128]{2,1,0:T(8,128)(2,1)S(1)}, u32[]{:S(2)}, u32[]{:S(2)}) collective-permute-start(bf16[8,256,128]{2,1,0:T(8,128)(2,1)S(1)} %collective-permute-done.5.refs_9_), channel_id=1, source_target_pairs={{0,1},{1,0},{2,3},{3,2},{4,5},{5,4},{6,7},{7,6},{8,9},{9,8},{10,11... | collective-permute-start | bytes 1572872 | tf_op jit(solution)/shard_map/ppermute | solution.py:236
  71.2 2.4 %collective-permute-start.4 = (bf16[8,256,128]{2,1,0:T(8,128)(2,1)S(1)}, bf16[8,256,128]{2,1,0:T(8,128)(2,1)S(1)}, u32[]{:S(2)}, u32[]{:S(2)}) collective-permute-start(bf16[8,256,128]{2,1,0:T(8,128)(2,1)S(1)} %collective-permute-done.3.refs_7_), channel_id=1, source_target_pairs={{0,1},{1,0},{2,3},{3,2},{4,5},{5,4},{6,7},{7,6},{8,9},{9,8},{10,11... | collective-permute-start | bytes 1572872 | tf_op jit(solution)/shard_map/ppermute | solution.py:236
  73.6 1.9 %collective-permute-start.2 = (bf16[8,256,128]{2,1,0:T(8,128)(2,1)S(1)}, bf16[8,256,128]{2,1,0:T(8,128)(2,1)}, u32[]{:S(2)}, u32[]{:S(2)}) collective-permute-start(bf16[8,256,128]{2,1,0:T(8,128)(2,1)S(1)} %collective-permute-done.refs_5_), channel_id=1, source_target_pairs={{0,1},{1,0},{2,3},{3,2},{4,5},{5,4},{6,7},{7,6},{8,9},{9,8},{10,11... | collective-permute-start | bytes 1572872 | tf_op jit(solution)/shard_map/ppermute | solution.py:236
  75.6 0.8 copy-done.5
  76.3 0.2 copy-done.6
  76.5 0.8 copy-done.7
  77.3 0.2 collective-permute-done.2.refs_6_
  77.6 9.3 %replica_sums.1 = bf16[448,4,128]{2,1,0:T(4,128)(2,1)} custom-call(s32[3]{0:T(128)} %pad_add_fusion.refs_0_, s32[192]{0:T(256)} %reshape.62.refs_1_, bf16[4096,256]{1,0:T(8,128)(2,1)} %all-gather.2.cloned.1.call-done.refs_2_, bf16[8,256,128]{2,1,0:T(8,128)(2,1)} %copy-done.1, bf16[8,256,128]{2,1,0:T(8,128)(2,1)} %copy-done.5, ...), custom_call_target="tpu_custom_call" | custom-call | flops 1073741824 | bytes 6291456 | tf_op jit(solution)/shard_map/replica_sums/pallas_call | solution.py:238
  86.9 24.9 %all_to_all.16 = bf16[32,56,128]{2,1,0:T(8,128)(2,1)} all-to-all(bf16[32,56,128]{2,1,0:T(8,128)(2,1)} %bitcast.22), channel_id=1, replica_groups=mesh['dp_0'=4,'dp_1'=8,'tensor'=16] {'dp_0','dp_1'}, dimensions={0} | all-to-all | bytes 917504 | tf_op jit(solution)/shard_map/all_to_all | solution.py:262
  111.8 4.0 %owner_adam.1 = (f32[128,128]{1,0:T(8,128)}, f32[128,128]{1,0:T(8,128)}, f32[128,128]{1,0:T(8,128)}, f32[9,128,128]{2,1,0:T(8,128)}, f32[9,128,128]{2,1,0:T(8,12...) custom-call(bf16[1792,128]{1,0:T(8,128)(2,1)} %bitcast.23, f32[128,128]{1,0:T(8,128)} %refs_1_.1, f32[128,128]{1,0:T(8,128)} %refs_2_.1, ...), custom_call_target="tpu_custom_call" | custom-call | tf_op jit(solution)/shard_map/owner_adam/pallas_call | solution.py:268
  (30 shorter events, 0.4 us)
Async XLA Ops:
  7.2 13.1 %copy-start = (bf16[128,4096]{1,0:T(8,128)(2,1)S(1)}, bf16[128,4096]{1,0:T(8,128)(2,1)}, u32[]{:S(2)}) copy-start(bf16[128,4096]{1,0:T(8,128)(2,1)} %param.10) | copy-start | bytes 3145732
  7.2 70.4 %all-gather.2.cloned.1.call-start = ((), (), s32[]{:S(2)}) async-start(), calls=%async_computation.3 | async-start | bytes 2359296 | tf_op jit(solution)/shard_map/all_gather | solution.py:220
  20.3 37.1 %copy-start.8 = (s32[1,192,1]{1,2,0:T(1,128)S(1)}, s32[1,192,1]{1,2,0:T(1,128)}, u32[]{:S(2)}) copy-start(s32[1,192,1]{1,2,0:T(1,128)} %param.13) | copy-start | bytes 2308
  21.7 27.0 %all-to-all-start = ((bf16[8,256,128]{2,1,0:T(8,128)(2,1)}), bf16[8,256,128]{2,1,0:T(8,128)(2,1)S(1)}, u32[]{:S(2)}, u32[]{:S(2)}) async-start(bf16[8,256,128]{2,1,0:T(8,128)(2,1)} %bitcast.3), calls=%async_computation | async-start | bytes 1048576 | tf_op jit(solution)/shard_map/all_to_all | solution.py:225
  48.7 28.9 %copy-start.1 = (bf16[8,256,128]{2,1,0:T(8,128)(2,1)}, bf16[8,256,128]{2,1,0:T(8,128)(2,1)S(1)}, u32[]{:S(2)}) copy-start(bf16[8,256,128]{2,1,0:T(8,128)(2,1)S(1)} %all-to-all-done.refs_3_) | copy-start | bytes 1572868
  48.7 20.5 %collective-permute-start.5 = (bf16[8,256,128]{2,1,0:T(8,128)(2,1)S(1)}, bf16[8,256,128]{2,1,0:T(8,128)(2,1)S(1)}, u32[]{:S(2)}, u32[]{:S(2)}) collective-permute-start(bf16[8,256,128]{2,1,0:T(8,128)(2,1)S(1)} %all-to-all-done.refs_3_), channel_id=1, source_target_pairs={{0,256},{128,384},{256,0},{384,128},{1,257},{129,385},{257,1},{385... | collective-permute-start | bytes 1572872 | tf_op jit(solution)/shard_map/ppermute | solution.py:181
  51.0 20.2 %collective-permute-start.3 = (bf16[8,256,128]{2,1,0:T(8,128)(2,1)S(1)}, bf16[8,256,128]{2,1,0:T(8,128)(2,1)S(1)}, u32[]{:S(2)}, u32[]{:S(2)}) collective-permute-start(bf16[8,256,128]{2,1,0:T(8,128)(2,1)S(1)} %all-to-all-done.refs_3_), channel_id=1, source_target_pairs={{0,384},{128,0},{256,128},{384,256},{1,385},{129,1},{257,129},{385... | collective-permute-start | bytes 1572872 | tf_op jit(solution)/shard_map/ppermute | solution.py:181
  55.5 13.7 %collective-permute-start = (bf16[8,256,128]{2,1,0:T(8,128)(2,1)S(1)}, bf16[8,256,128]{2,1,0:T(8,128)(2,1)S(1)}, u32[]{:S(2)}, u32[]{:S(2)}) collective-permute-start(bf16[8,256,128]{2,1,0:T(8,128)(2,1)S(1)} %all-to-all-done.refs_3_), channel_id=1, source_target_pairs={{0,128},{128,256},{256,384},{384,0},{1,129},{129,257},{257,385},{3... | collective-permute-start | bytes 1572872 | tf_op jit(solution)/shard_map/ppermute | solution.py:181
  59.2 16.4 %collective-permute-start.1 = (bf16[8,256,128]{2,1,0:T(8,128)(2,1)S(1)}, bf16[8,256,128]{2,1,0:T(8,128)(2,1)S(1)}, u32[]{:S(2)}, u32[]{:S(2)}) collective-permute-start(bf16[8,256,128]{2,1,0:T(8,128)(2,1)S(1)} %all-to-all-done.refs_3_), channel_id=1, source_target_pairs={{0,1},{1,0},{2,3},{3,2},{4,5},{5,4},{6,7},{7,6},{8,9},{9,8},{10,11... | collective-permute-start | bytes 1572872 | tf_op jit(solution)/shard_map/ppermute | solution.py:236
  69.2 8.3 %copy-start.4 = (bf16[8,256,128]{2,1,0:T(8,128)(2,1)}, bf16[8,256,128]{2,1,0:T(8,128)(2,1)S(1)}, u32[]{:S(2)}) copy-start(bf16[8,256,128]{2,1,0:T(8,128)(2,1)S(1)} %collective-permute-done.refs_5_) | copy-start | bytes 1572868
  69.2 8.3 %copy-start.2 = (bf16[8,256,128]{2,1,0:T(8,128)(2,1)}, bf16[8,256,128]{2,1,0:T(8,128)(2,1)S(1)}, u32[]{:S(2)}) copy-start(bf16[8,256,128]{2,1,0:T(8,128)(2,1)S(1)} %collective-permute-done.5.refs_9_) | copy-start | bytes 1572868
  69.2 6.3 %collective-permute-start.6 = (bf16[8,256,128]{2,1,0:T(8,128)(2,1)S(1)}, bf16[8,256,128]{2,1,0:T(8,128)(2,1)S(1)}, u32[]{:S(2)}, u32[]{:S(2)}) collective-permute-start(bf16[8,256,128]{2,1,0:T(8,128)(2,1)S(1)} %collective-permute-done.5.refs_9_), channel_id=1, source_target_pairs={{0,1},{1,0},{2,3},{3,2},{4,5},{5,4},{6,7},{7,6},{8,9},{9,8},{10,11... | collective-permute-start | bytes 1572872 | tf_op jit(solution)/shard_map/ppermute | solution.py:236
  71.2 6.4 %copy-start.3 = (bf16[8,256,128]{2,1,0:T(8,128)(2,1)}, bf16[8,256,128]{2,1,0:T(8,128)(2,1)S(1)}, u32[]{:S(2)}) copy-start(bf16[8,256,128]{2,1,0:T(8,128)(2,1)S(1)} %collective-permute-done.3.refs_7_) | copy-start | bytes 1572868
  71.2 4.4 %collective-permute-start.4 = (bf16[8,256,128]{2,1,0:T(8,128)(2,1)S(1)}, bf16[8,256,128]{2,1,0:T(8,128)(2,1)S(1)}, u32[]{:S(2)}, u32[]{:S(2)}) collective-permute-start(bf16[8,256,128]{2,1,0:T(8,128)(2,1)S(1)} %collective-permute-done.3.refs_7_), channel_id=1, source_target_pairs={{0,1},{1,0},{2,3},{3,2},{4,5},{5,4},{6,7},{7,6},{8,9},{9,8},{10,11... | collective-permute-start | bytes 1572872 | tf_op jit(solution)/shard_map/ppermute | solution.py:236
  73.6 3.9 %collective-permute-start.2 = (bf16[8,256,128]{2,1,0:T(8,128)(2,1)S(1)}, bf16[8,256,128]{2,1,0:T(8,128)(2,1)}, u32[]{:S(2)}, u32[]{:S(2)}) collective-permute-start(bf16[8,256,128]{2,1,0:T(8,128)(2,1)S(1)} %collective-permute-done.refs_5_), channel_id=1, source_target_pairs={{0,1},{1,0},{2,3},{3,2},{4,5},{5,4},{6,7},{7,6},{8,9},{9,8},{10,11... | collective-permute-start | bytes 1572872 | tf_op jit(solution)/shard_map/ppermute | solution.py:236
  75.5 0.8 copy-start.5
  75.6 1.0 copy-start.6
  76.5 0.8 copy-start.7
Sparse Core Ops, SparseCore 0:
  20.4 46.1 all-gather.1

commit v6 on v5

--- a/solution.py
+++ b/solution.py
@@ -224,7 +224,7 @@
     halved = jnp.transpose(halved, (1, 2, 0, 3, 4)).reshape(size_y, -1, tokens_here)
     own = lax.all_to_all(halved, DP[1], split_axis=0, concat_axis=0, tiled=True)
     steps_x = [0, size_x - 1, 1, 2]
-    left = shift(own, DP[0], 1)
+    left, right = shift(own, DP[0], 1), shift(own, DP[0], -1)
     target = owner_row * slots + slot_numbers(owner_row)
     target = target.reshape(tiles_here - 1, 2, group_size // 2)
     target = jnp.where(core == 0, target, target[:, ::-1]).reshape(-1)
@@ -232,7 +232,7 @@
     left, target, scalars = lax.optimization_barrier((left, target, scalars))
     swap = [(i, i ^ 1) for i in range(lax.axis_size("tensor"))]
     acts_rows = []
-    for array in (own, left, shift(own, DP[0], -1), shift(own, DP[0], 2)):
+    for array in (own, left, right, shift(right, DP[0], -1)):
         acts_rows += [array, lax.ppermute(array, "tensor", swap)]
     rows_spec = pl.BlockSpec((1, size_x * row_block // 2, tokens_here), lambda y: (y, 0, 0))
     outgoing = pl.pallas_call(

time: 123 us -> 120 us (0.976)
  blocking collectives: 36 us -> 59 us
  waiting for transfers between devices: 27.1 us -> 9.53 us
  starting transfers between devices: 24.5 us -> 16.8 us
    all_to_all x0 -> x1, blocking collectives: none -> 26.2 us  [body(): own = lax.all_to_all(halved, DP[1], split_axis=0, concat_axis=0, tiled=True)]
    all_to_all x1 -> x0, waiting for transfers between devices: 18.8 us -> none  [body(): own = lax.all_to_all(halved, DP[1], split_axis=0, concat_axis=0, tiled=True)]
    all_to_all x1 -> x0, starting transfers between devices: 7.55 us -> none  [body(): own = lax.all_to_all(halved, DP[1], split_axis=0, concat_axis=0, tiled=True)]
    all_to_all x1, blocking collectives: 24.9 us -> 21.8 us  [body(): lax.all_to_all(outgoing.reshape(group_size, slots * part, TILE), DP, spli...]
    ppermute x3, waiting for transfers between devices: 8.14 us -> 9.44 us  [shift(): lax.ppermute(array, axis, [(i, (i + by) % size) for i in range(size)])]
  transfers between devices with their start and end apart: 9 -> 8, of which waited for: 3 -> 3; matrix products, arithmetic and copies ran while one was open for 3% -> 2% of each run, Pallas kernels for 0% -> 0%
where the time goes in v6:
time: 120 us
  blocking collectives  59 us (49%)
  starting transfers between devices  16.8 us (14%)
  Pallas kernels  15.4 us (13%)
  between operations  14.9 us (12%)
  waiting for transfers between devices  9.53 us (8%)
  local copies, waits for them, and re-layouts  3.21 us (3%)
    all_to_all x1, blocking collectives, body(): own = lax.all_to_all(halved, DP[1], split_axis=0, concat_axis=0, tiled=True)  26.2 us
    all_to_all x1, blocking collectives, body(): lax.all_to_all(outgoing.reshape(group_size, slots * part, TILE), DP, spli...  21.8 us
    all_to_all x1, blocking collectives, body(): lax.all_to_all(spread, DP[0], split_axis=0, concat_axis=0, tiled=True)  11.1 us
    ppermute x3, waiting for transfers between devices, shift(): lax.ppermute(array, axis, [(i, (i + by) % size) for i in range(size)])  9.44 us
    pallas_call x1, Pallas kernels, body(): pl.pallas_call(lambda *refs: sums_kernel(*refs, steps_x=steps_x, tiles=ti...  9.34 us
    ppermute x3, starting transfers between devices, shift(): lax.ppermute(array, axis, [(i, (i + by) % size) for i in range(size)])  8.48 us
    ppermute x4, starting transfers between devices, body(): acts_rows += [array, lax.ppermute(array, 'tensor', swap)]  8.3 us
    pallas_call x1, Pallas kernels, body(): pl.pallas_call(lambda *refs: owner_kernel(*refs, size_x=size_x, size_y=si...  4.05 us
  transfers between devices with their start and end apart: 8, of which 3 were waited for; matrix products, arithmetic and copies ran while one was open for 2% of the time, Pallas kernels for 0%

profile of v6, /device:TPU:456, one launch (start us, length us, event | category | flops | bytes accessed | tf_op | source)
XLA Modules:
  0.0 119.8 jit_solution(16483812475174031274)
XLA Ops:
  7.2 2.0 %spread.1 = bf16[4,128,256]{2,1,0:T(8,128)(2,1)} custom-call(bf16[128,896]{1,0:T(8,128)(2,1)} %grads_ref.1), custom_call_target="tpu_custom_call" | custom-call | tf_op jit(solution)/shard_map/spread/pallas_call | solution.py:212
  9.2 11.1 %all_to_all.15 = bf16[4,128,256]{2,1,0:T(8,128)(2,1)} all-to-all(bf16[4,128,256]{2,1,0:T(8,128)(2,1)} %spread.1), channel_id=1, replica_groups=mesh['dp_0'=4,'dp_1'=8,'tensor'=16] {'dp_0'}, dimensions={0} | all-to-all | bytes 524288 | tf_op jit(solution)/shard_map/all_to_all | solution.py:219
  20.4 0.3 copy.22
  20.7 0.3 copy.21
  20.9 26.2 %all_to_all.16.refs_3_ = bf16[8,256,128]{2,1,0:T(8,128)(2,1)S(1)} all-to-all(bf16[8,256,128]{2,1,0:T(8,128)(2,1)S(1)} %bitcast.22), channel_id=1, replica_groups=mesh['dp_0'=4,'dp_1'=8,'tensor'=16] {'dp_1'}, dimensions={0} | all-to-all | bytes 1048576 | tf_op jit(solution)/shard_map/all_to_all | solution.py:225
  47.1 2.6 %collective-permute-start.3 = (bf16[8,256,128]{2,1,0:T(8,128)(2,1)S(1)}, bf16[8,256,128]{2,1,0:T(8,128)(2,1)S(1)}, u32[]{:S(2)}, u32[]{:S(2)}) collective-permute-start(bf16[8,256,128]{2,1,0:T(8,128)(2,1)S(1)} %all_to_all.16.refs_3_), channel_id=1, source_target_pairs={{0,384},{128,0},{256,128},{384,256},{1,385},{129,1},{257,129},{385... | collective-permute-start | bytes 1572872 | tf_op jit(solution)/shard_map/ppermute | solution.py:181
  50.4 3.2 %collective-permute-start = (bf16[8,256,128]{2,1,0:T(8,128)(2,1)S(1)}, bf16[8,256,128]{2,1,0:T(8,128)(2,1)S(1)}, u32[]{:S(2)}, u32[]{:S(2)}) collective-permute-start(bf16[8,256,128]{2,1,0:T(8,128)(2,1)S(1)} %all_to_all.16.refs_3_), channel_id=1, source_target_pairs={{0,128},{128,256},{256,384},{384,0},{1,129},{129,257},{257,385},{3... | collective-permute-start | bytes 1572872 | tf_op jit(solution)/shard_map/ppermute | solution.py:181
  53.7 9.1 %collective-permute-done.3.refs_7_ = bf16[8,256,128]{2,1,0:T(8,128)(2,1)S(1)} collective-permute-done((bf16[8,256,128]{2,1,0:T(8,128)(2,1)S(1)}, bf16[8,256,128]{2,1,0:T(8,128)(2,1)S(1)}, u32[]{:S(2)}, u32[]{:S(2)}) %collective-permute-start.3) | collective-permute-done | bytes 524320 | tf_op jit(solution)/shard_map/ppermute | solution.py:181
  62.7 2.7 %collective-permute-start.5 = (bf16[8,256,128]{2,1,0:T(8,128)(2,1)S(1)}, bf16[8,256,128]{2,1,0:T(8,128)(2,1)S(1)}, u32[]{:S(2)}, u32[]{:S(2)}) collective-permute-start(bf16[8,256,128]{2,1,0:T(8,128)(2,1)S(1)} %collective-permute-done.3.refs_7_), channel_id=1, source_target_pairs={{0,384},{128,0},{256,128},{384,256},{1,385},{129,1},{257,129},{385... | collective-permute-start | bytes 1572872 | tf_op jit(solution)/shard_map/ppermute | solution.py:181
  65.4 0.1 mul.16
  65.5 0.2 convert_reduce_fusion
  65.8 0.7 reshape.62.refs_1_
  66.5 0.7 pad_add_fusion.refs_0_
  67.1 1.9 %collective-permute-start.1 = (bf16[8,256,128]{2,1,0:T(8,128)(2,1)S(1)}, bf16[8,256,128]{2,1,0:T(8,128)(2,1)S(1)}, u32[]{:S(2)}, u32[]{:S(2)}) collective-permute-start(bf16[8,256,128]{2,1,0:T(8,128)(2,1)S(1)} %all_to_all.16.refs_3_), channel_id=1, source_target_pairs={{0,1},{1,0},{2,3},{3,2},{4,5},{5,4},{6,7},{7,6},{8,9},{9,8},{10,11... | collective-permute-start | bytes 1572872 | tf_op jit(solution)/shard_map/ppermute | solution.py:236
  69.1 2.4 %collective-permute-start.2 = (bf16[8,256,128]{2,1,0:T(8,128)(2,1)S(1)}, bf16[8,256,128]{2,1,0:T(8,128)(2,1)S(1)}, u32[]{:S(2)}, u32[]{:S(2)}) collective-permute-start(bf16[8,256,128]{2,1,0:T(8,128)(2,1)S(1)} %collective-permute-done.refs_5_), channel_id=1, source_target_pairs={{0,1},{1,0},{2,3},{3,2},{4,5},{5,4},{6,7},{7,6},{8,9},{9,8},{10,11... | collective-permute-start | bytes 1572872 | tf_op jit(solution)/shard_map/ppermute | solution.py:236
  71.5 1.9 %collective-permute-start.4 = (bf16[8,256,128]{2,1,0:T(8,128)(2,1)S(1)}, bf16[8,256,128]{2,1,0:T(8,128)(2,1)S(1)}, u32[]{:S(2)}, u32[]{:S(2)}) collective-permute-start(bf16[8,256,128]{2,1,0:T(8,128)(2,1)S(1)} %collective-permute-done.3.refs_7_), channel_id=1, source_target_pairs={{0,1},{1,0},{2,3},{3,2},{4,5},{5,4},{6,7},{7,6},{8,9},{9,8},{10,11... | collective-permute-start | bytes 1572872 | tf_op jit(solution)/shard_map/ppermute | solution.py:236
  73.4 0.4 collective-permute-done.5.refs_9_
  73.8 2.1 %collective-permute-start.6 = (bf16[8,256,128]{2,1,0:T(8,128)(2,1)S(1)}, bf16[8,256,128]{2,1,0:T(8,128)(2,1)}, u32[]{:S(2)}, u32[]{:S(2)}) collective-permute-start(bf16[8,256,128]{2,1,0:T(8,128)(2,1)S(1)} %collective-permute-done.5.refs_9_), channel_id=1, source_target_pairs={{0,1},{1,0},{2,3},{3,2},{4,5},{5,4},{6,7},{7,6},{8,9},{9,8},{10,11... | collective-permute-start | bytes 1572872 | tf_op jit(solution)/shard_map/ppermute | solution.py:236
  75.9 0.8 copy-done.5
  76.7 0.2 copy-done.7
  76.9 0.8 copy-done.6
  77.7 9.3 %replica_sums.1 = bf16[448,4,128]{2,1,0:T(4,128)(2,1)} custom-call(s32[3]{0:T(128)} %pad_add_fusion.refs_0_, s32[192]{0:T(256)} %reshape.62.refs_1_, bf16[4096,256]{1,0:T(8,128)(2,1)} %all-gather.2.cloned.1.call-done.refs_2_, bf16[8,256,128]{2,1,0:T(8,128)(2,1)} %copy-done.1, bf16[8,256,128]{2,1,0:T(8,128)(2,1)} %copy-done.5, ...), custom_call_target="tpu_custom_call" | custom-call | flops 1073741824 | bytes 6291456 | tf_op jit(solution)/shard_map/replica_sums/pallas_call | solution.py:238
  87.1 21.8 %all_to_all.17 = bf16[32,56,128]{2,1,0:T(8,128)(2,1)} all-to-all(bf16[32,56,128]{2,1,0:T(8,128)(2,1)} %bitcast.23), channel_id=1, replica_groups=mesh['dp_0'=4,'dp_1'=8,'tensor'=16] {'dp_0','dp_1'}, dimensions={0} | all-to-all | bytes 917504 | tf_op jit(solution)/shard_map/all_to_all | solution.py:262
  108.8 4.0 %owner_adam.1 = (f32[128,128]{1,0:T(8,128)}, f32[128,128]{1,0:T(8,128)}, f32[128,128]{1,0:T(8,128)}, f32[9,128,128]{2,1,0:T(8,128)}, f32[9,128,128]{2,1,0:T(8,12...) custom-call(bf16[1792,128]{1,0:T(8,128)(2,1)} %bitcast.24, f32[128,128]{1,0:T(8,128)} %refs_1_.1, f32[128,128]{1,0:T(8,128)} %refs_2_.1, ...), custom_call_target="tpu_custom_call" | custom-call | tf_op jit(solution)/shard_map/owner_adam/pallas_call | solution.py:268
  (29 shorter events, 0.4 us)
Async XLA Ops:
  7.2 13.1 %copy-start = (bf16[128,4096]{1,0:T(8,128)(2,1)S(1)}, bf16[128,4096]{1,0:T(8,128)(2,1)}, u32[]{:S(2)}) copy-start(bf16[128,4096]{1,0:T(8,128)(2,1)} %param.10) | copy-start | bytes 3145732
  7.2 70.5 %all-gather.2.cloned.1.call-start = ((), (), s32[]{:S(2)}) async-start(), calls=%async_computation.3 | async-start | bytes 2359296 | tf_op jit(solution)/shard_map/all_gather | solution.py:220
  20.3 45.1 %copy-start.8 = (s32[1,192,1]{1,2,0:T(1,128)S(1)}, s32[1,192,1]{1,2,0:T(1,128)}, u32[]{:S(2)}) copy-start(s32[1,192,1]{1,2,0:T(1,128)} %param.13) | copy-start | bytes 2308
  47.1 30.6 %copy-start.1 = (bf16[8,256,128]{2,1,0:T(8,128)(2,1)}, bf16[8,256,128]{2,1,0:T(8,128)(2,1)S(1)}, u32[]{:S(2)}) copy-start(bf16[8,256,128]{2,1,0:T(8,128)(2,1)S(1)} %all_to_all.16.refs_3_) | copy-start | bytes 1572868
  47.1 15.6 %collective-permute-start.3 = (bf16[8,256,128]{2,1,0:T(8,128)(2,1)S(1)}, bf16[8,256,128]{2,1,0:T(8,128)(2,1)S(1)}, u32[]{:S(2)}, u32[]{:S(2)}) collective-permute-start(bf16[8,256,128]{2,1,0:T(8,128)(2,1)S(1)} %all_to_all.16.refs_3_), channel_id=1, source_target_pairs={{0,384},{128,0},{256,128},{384,256},{1,385},{129,1},{257,129},{385... | collective-permute-start | bytes 1572872 | tf_op jit(solution)/shard_map/ppermute | solution.py:181
  50.4 18.6 %collective-permute-start = (bf16[8,256,128]{2,1,0:T(8,128)(2,1)S(1)}, bf16[8,256,128]{2,1,0:T(8,128)(2,1)S(1)}, u32[]{:S(2)}, u32[]{:S(2)}) collective-permute-start(bf16[8,256,128]{2,1,0:T(8,128)(2,1)S(1)} %all_to_all.16.refs_3_), channel_id=1, source_target_pairs={{0,128},{128,256},{256,384},{384,0},{1,129},{129,257},{257,385},{3... | collective-permute-start | bytes 1572872 | tf_op jit(solution)/shard_map/ppermute | solution.py:181
  62.7 15.0 %copy-start.2 = (bf16[8,256,128]{2,1,0:T(8,128)(2,1)}, bf16[8,256,128]{2,1,0:T(8,128)(2,1)S(1)}, u32[]{:S(2)}) copy-start(bf16[8,256,128]{2,1,0:T(8,128)(2,1)S(1)} %collective-permute-done.3.refs_7_) | copy-start | bytes 1572868
  62.7 11.1 %collective-permute-start.5 = (bf16[8,256,128]{2,1,0:T(8,128)(2,1)S(1)}, bf16[8,256,128]{2,1,0:T(8,128)(2,1)S(1)}, u32[]{:S(2)}, u32[]{:S(2)}) collective-permute-start(bf16[8,256,128]{2,1,0:T(8,128)(2,1)S(1)} %collective-permute-done.3.refs_7_), channel_id=1, source_target_pairs={{0,384},{128,0},{256,128},{384,256},{1,385},{129,1},{257,129},{385... | collective-permute-start | bytes 1572872 | tf_op jit(solution)/shard_map/ppermute | solution.py:181
  67.1 8.7 %collective-permute-start.1 = (bf16[8,256,128]{2,1,0:T(8,128)(2,1)S(1)}, bf16[8,256,128]{2,1,0:T(8,128)(2,1)S(1)}, u32[]{:S(2)}, u32[]{:S(2)}) collective-permute-start(bf16[8,256,128]{2,1,0:T(8,128)(2,1)S(1)} %all_to_all.16.refs_3_), channel_id=1, source_target_pairs={{0,1},{1,0},{2,3},{3,2},{4,5},{5,4},{6,7},{7,6},{8,9},{9,8},{10,11... | collective-permute-start | bytes 1572872 | tf_op jit(solution)/shard_map/ppermute | solution.py:236
  69.1 8.7 %copy-start.3 = (bf16[8,256,128]{2,1,0:T(8,128)(2,1)}, bf16[8,256,128]{2,1,0:T(8,128)(2,1)S(1)}, u32[]{:S(2)}) copy-start(bf16[8,256,128]{2,1,0:T(8,128)(2,1)S(1)} %collective-permute-done.refs_5_) | copy-start | bytes 1572868
  69.1 6.8 %collective-permute-start.2 = (bf16[8,256,128]{2,1,0:T(8,128)(2,1)S(1)}, bf16[8,256,128]{2,1,0:T(8,128)(2,1)S(1)}, u32[]{:S(2)}, u32[]{:S(2)}) collective-permute-start(bf16[8,256,128]{2,1,0:T(8,128)(2,1)S(1)} %collective-permute-done.refs_5_), channel_id=1, source_target_pairs={{0,1},{1,0},{2,3},{3,2},{4,5},{5,4},{6,7},{7,6},{8,9},{9,8},{10,11... | collective-permute-start | bytes 1572872 | tf_op jit(solution)/shard_map/ppermute | solution.py:236
  71.5 4.4 %collective-permute-start.4 = (bf16[8,256,128]{2,1,0:T(8,128)(2,1)S(1)}, bf16[8,256,128]{2,1,0:T(8,128)(2,1)S(1)}, u32[]{:S(2)}, u32[]{:S(2)}) collective-permute-start(bf16[8,256,128]{2,1,0:T(8,128)(2,1)S(1)} %collective-permute-done.3.refs_7_), channel_id=1, source_target_pairs={{0,1},{1,0},{2,3},{3,2},{4,5},{5,4},{6,7},{7,6},{8,9},{9,8},{10,11... | collective-permute-start | bytes 1572872 | tf_op jit(solution)/shard_map/ppermute | solution.py:236
  73.8 3.9 %copy-start.4 = (bf16[8,256,128]{2,1,0:T(8,128)(2,1)}, bf16[8,256,128]{2,1,0:T(8,128)(2,1)S(1)}, u32[]{:S(2)}) copy-start(bf16[8,256,128]{2,1,0:T(8,128)(2,1)S(1)} %collective-permute-done.5.refs_9_) | copy-start | bytes 1572868
  73.8 3.9 %collective-permute-start.6 = (bf16[8,256,128]{2,1,0:T(8,128)(2,1)S(1)}, bf16[8,256,128]{2,1,0:T(8,128)(2,1)}, u32[]{:S(2)}, u32[]{:S(2)}) collective-permute-start(bf16[8,256,128]{2,1,0:T(8,128)(2,1)S(1)} %collective-permute-done.5.refs_9_), channel_id=1, source_target_pairs={{0,1},{1,0},{2,3},{3,2},{4,5},{5,4},{6,7},{7,6},{8,9},{9,8},{10,11... | collective-permute-start | bytes 1572872 | tf_op jit(solution)/shard_map/ppermute | solution.py:236
  75.9 0.8 copy-start.5
  75.9 1.0 copy-start.7
  76.9 0.8 copy-start.6
Sparse Core Ops, SparseCore 0:
  20.4 45.4 all-gather.1

commit v7 on v6

--- a/solution.py
+++ b/solution.py
@@ -71,21 +71,21 @@
 
     kept = lax.broadcasted_iota(jnp.int32, (group_rows, width), 1) // lanes == selected
     column_squares = squares[...]
-    for g in range(groups):
-        total = sums[g]
+    for y in range(pairs[0][0].shape[0]):
         for step_x, pair in zip(steps_x, pairs):
             x = lax.rem(at_x + step_x, groups)
-            rows = [ref[0, g * half : (g + 1) * half, :] for ref in pair]
-            partial = jnp.dot(
-                jnp.concatenate(rows, axis=0),
-                grads_ref[pl.ds(pl.multiple_of(x * tokens, tokens), tokens), :],
-                preferred_element_type=jnp.float32,
-            )
-            rounded = partial.astype(jnp.bfloat16).astype(jnp.float32)
-            total = total + jnp.where(kept, partial, rounded)
-            squared = (partial * partial).reshape(-1, *column_squares.shape)
-            column_squares = column_squares + squared.sum(axis=0)
-        sums[g] = total
+            here = pl.ds(pl.multiple_of((y * groups + x) * tokens, tokens), tokens)
+            for g in range(groups):
+                rows = [ref[y, g * half : (g + 1) * half, :] for ref in pair]
+                partial = jnp.dot(
+                    jnp.concatenate(rows, axis=0),
+                    grads_ref[here, :],
+                    preferred_element_type=jnp.float32,
+                )
+                rounded = partial.astype(jnp.bfloat16).astype(jnp.float32)
+                sums[g] = sums[g] + jnp.where(kept, partial, rounded)
+                squared = (partial * partial).reshape(-1, *column_squares.shape)
+                column_squares = column_squares + squared.sum(axis=0)
     squares[...] = column_squares
 
     @pl.when(pl.program_id(0) == pl.num_programs(0) - 1)
@@ -234,14 +234,15 @@
     acts_rows = []
     for array in (own, left, right, shift(right, DP[0], -1)):
         acts_rows += [array, lax.ppermute(array, "tensor", swap)]
-    rows_spec = pl.BlockSpec((1, size_x * row_block // 2, tokens_here), lambda y: (y, 0, 0))
+    block_y = size_y // 2
+    rows_spec = pl.BlockSpec((block_y, size_x * row_block // 2, tokens_here), lambda y: (y, 0, 0))
     outgoing = pl.pallas_call(
         lambda *refs: sums_kernel(
             *refs, steps_x=steps_x, tiles=tiles_here, owners=group_size, slots=slots
         ),
-        grid=(size_y,),
+        grid=(size_y // block_y,),
         in_specs=[small] * 2
-        + [pl.BlockSpec((size_x * tokens_here, width), lambda y: (y, 0))]
+        + [pl.BlockSpec((block_y * size_x * tokens_here, width), lambda y: (y, 0))]
         + [rows_spec] * len(acts_rows),
         out_specs=pl.BlockSpec((group_size * slots, part, TILE), lambda y: (0, 0, 0)),
         out_shape=jax.ShapeDtypeStruct((group_size * slots, part, TILE), jnp.bfloat16),

time: 120 us -> 119 us (level)
  Pallas kernels: 15.4 us -> 13.6 us
    pallas_call x1, Pallas kernels: 9.34 us -> 7.56 us  [body(): pl.pallas_call(lambda *refs: sums_kernel(*refs, steps_x=steps_x, tiles=ti...]
where the time goes in v7:
time: 119 us; the launch traced here: 118 us
  blocking collectives  59 us (50%)
  starting transfers between devices  16.8 us (14%)
  between operations  14.9 us (13%)
  Pallas kernels  13.6 us (11%)
  waiting for transfers between devices  9.53 us (8%)
  local copies, waits for them, and re-layouts  3.21 us (3%)
    all_to_all x1, blocking collectives, body(): own = lax.all_to_all(halved, DP[1], split_axis=0, concat_axis=0, tiled=True)  26.2 us
    all_to_all x1, blocking collectives, body(): lax.all_to_all(outgoing.reshape(group_size, slots * part, TILE), DP, spli...  21.8 us
    all_to_all x1, blocking collectives, body(): lax.all_to_all(spread, DP[0], split_axis=0, concat_axis=0, tiled=True)  11.1 us
    ppermute x3, waiting for transfers between devices, shift(): lax.ppermute(array, axis, [(i, (i + by) % size) for i in range(size)])  9.44 us
    ppermute x3, starting transfers between devices, shift(): lax.ppermute(array, axis, [(i, (i + by) % size) for i in range(size)])  8.48 us
    ppermute x4, starting transfers between devices, body(): acts_rows += [array, lax.ppermute(array, 'tensor', swap)]  8.3 us
    pallas_call x1, Pallas kernels, body(): pl.pallas_call(lambda *refs: sums_kernel(*refs, steps_x=steps_x, tiles=ti...  7.56 us
    pallas_call x1, Pallas kernels, body(): pl.pallas_call(lambda *refs: owner_kernel(*refs, size_x=size_x, size_y=si...  4.05 us
  transfers between devices with their start and end apart: 8, of which 3 were waited for; matrix products, arithmetic and copies ran while one was open for 2% of the time, Pallas kernels for 0%

profile of v7, /device:TPU:456, one launch (start us, length us, event | category | flops | bytes accessed | tf_op | source)
XLA Modules:
  0.0 118.0 jit_solution(2819244743526377313)
XLA Ops:
  7.2 2.0 %spread.1 = bf16[4,128,256]{2,1,0:T(8,128)(2,1)} custom-call(bf16[128,896]{1,0:T(8,128)(2,1)} %grads_ref.1), custom_call_target="tpu_custom_call" | custom-call | tf_op jit(solution)/shard_map/spread/pallas_call | solution.py:212
  9.2 11.1 %all_to_all.15 = bf16[4,128,256]{2,1,0:T(8,128)(2,1)} all-to-all(bf16[4,128,256]{2,1,0:T(8,128)(2,1)} %spread.1), channel_id=1, replica_groups=mesh['dp_0'=4,'dp_1'=8,'tensor'=16] {'dp_0'}, dimensions={0} | all-to-all | bytes 524288 | tf_op jit(solution)/shard_map/all_to_all | solution.py:219
  20.4 0.3 copy.22
  20.7 0.3 copy.21
  20.9 26.2 %all_to_all.16.refs_3_ = bf16[8,256,128]{2,1,0:T(8,128)(2,1)S(1)} all-to-all(bf16[8,256,128]{2,1,0:T(8,128)(2,1)S(1)} %bitcast.22), channel_id=1, replica_groups=mesh['dp_0'=4,'dp_1'=8,'tensor'=16] {'dp_1'}, dimensions={0} | all-to-all | bytes 1048576 | tf_op jit(solution)/shard_map/all_to_all | solution.py:225
  47.1 2.6 %collective-permute-start.3 = (bf16[8,256,128]{2,1,0:T(8,128)(2,1)S(1)}, bf16[8,256,128]{2,1,0:T(8,128)(2,1)S(1)}, u32[]{:S(2)}, u32[]{:S(2)}) collective-permute-start(bf16[8,256,128]{2,1,0:T(8,128)(2,1)S(1)} %all_to_all.16.refs_3_), channel_id=1, source_target_pairs={{0,384},{128,0},{256,128},{384,256},{1,385},{129,1},{257,129},{385... | collective-permute-start | bytes 1572872 | tf_op jit(solution)/shard_map/ppermute | solution.py:181
  50.4 3.2 %collective-permute-start = (bf16[8,256,128]{2,1,0:T(8,128)(2,1)S(1)}, bf16[8,256,128]{2,1,0:T(8,128)(2,1)S(1)}, u32[]{:S(2)}, u32[]{:S(2)}) collective-permute-start(bf16[8,256,128]{2,1,0:T(8,128)(2,1)S(1)} %all_to_all.16.refs_3_), channel_id=1, source_target_pairs={{0,128},{128,256},{256,384},{384,0},{1,129},{129,257},{257,385},{3... | collective-permute-start | bytes 1572872 | tf_op jit(solution)/shard_map/ppermute | solution.py:181
  53.7 9.1 %collective-permute-done.3.refs_7_ = bf16[8,256,128]{2,1,0:T(8,128)(2,1)S(1)} collective-permute-done((bf16[8,256,128]{2,1,0:T(8,128)(2,1)S(1)}, bf16[8,256,128]{2,1,0:T(8,128)(2,1)S(1)}, u32[]{:S(2)}, u32[]{:S(2)}) %collective-permute-start.3) | collective-permute-done | bytes 524320 | tf_op jit(solution)/shard_map/ppermute | solution.py:181
  62.7 2.7 %collective-permute-start.5 = (bf16[8,256,128]{2,1,0:T(8,128)(2,1)S(1)}, bf16[8,256,128]{2,1,0:T(8,128)(2,1)S(1)}, u32[]{:S(2)}, u32[]{:S(2)}) collective-permute-start(bf16[8,256,128]{2,1,0:T(8,128)(2,1)S(1)} %collective-permute-done.3.refs_7_), channel_id=1, source_target_pairs={{0,384},{128,0},{256,128},{384,256},{1,385},{129,1},{257,129},{385... | collective-permute-start | bytes 1572872 | tf_op jit(solution)/shard_map/ppermute | solution.py:181
  65.4 0.1 mul.16
  65.5 0.2 convert_reduce_fusion
  65.8 0.7 reshape.62.refs_1_
  66.5 0.7 pad_add_fusion.refs_0_
  67.1 1.9 %collective-permute-start.1 = (bf16[8,256,128]{2,1,0:T(8,128)(2,1)S(1)}, bf16[8,256,128]{2,1,0:T(8,128)(2,1)S(1)}, u32[]{:S(2)}, u32[]{:S(2)}) collective-permute-start(bf16[8,256,128]{2,1,0:T(8,128)(2,1)S(1)} %all_to_all.16.refs_3_), channel_id=1, source_target_pairs={{0,1},{1,0},{2,3},{3,2},{4,5},{5,4},{6,7},{7,6},{8,9},{9,8},{10,11... | collective-permute-start | bytes 1572872 | tf_op jit(solution)/shard_map/ppermute | solution.py:236
  69.1 2.4 %collective-permute-start.2 = (bf16[8,256,128]{2,1,0:T(8,128)(2,1)S(1)}, bf16[8,256,128]{2,1,0:T(8,128)(2,1)S(1)}, u32[]{:S(2)}, u32[]{:S(2)}) collective-permute-start(bf16[8,256,128]{2,1,0:T(8,128)(2,1)S(1)} %collective-permute-done.refs_5_), channel_id=1, source_target_pairs={{0,1},{1,0},{2,3},{3,2},{4,5},{5,4},{6,7},{7,6},{8,9},{9,8},{10,11... | collective-permute-start | bytes 1572872 | tf_op jit(solution)/shard_map/ppermute | solution.py:236
  71.5 1.9 %collective-permute-start.4 = (bf16[8,256,128]{2,1,0:T(8,128)(2,1)S(1)}, bf16[8,256,128]{2,1,0:T(8,128)(2,1)S(1)}, u32[]{:S(2)}, u32[]{:S(2)}) collective-permute-start(bf16[8,256,128]{2,1,0:T(8,128)(2,1)S(1)} %collective-permute-done.3.refs_7_), channel_id=1, source_target_pairs={{0,1},{1,0},{2,3},{3,2},{4,5},{5,4},{6,7},{7,6},{8,9},{9,8},{10,11... | collective-permute-start | bytes 1572872 | tf_op jit(solution)/shard_map/ppermute | solution.py:236
  73.4 0.4 collective-permute-done.5.refs_9_
  73.8 2.1 %collective-permute-start.6 = (bf16[8,256,128]{2,1,0:T(8,128)(2,1)S(1)}, bf16[8,256,128]{2,1,0:T(8,128)(2,1)}, u32[]{:S(2)}, u32[]{:S(2)}) collective-permute-start(bf16[8,256,128]{2,1,0:T(8,128)(2,1)S(1)} %collective-permute-done.5.refs_9_), channel_id=1, source_target_pairs={{0,1},{1,0},{2,3},{3,2},{4,5},{5,4},{6,7},{7,6},{8,9},{9,8},{10,11... | collective-permute-start | bytes 1572872 | tf_op jit(solution)/shard_map/ppermute | solution.py:236
  75.9 0.8 copy-done.5
  76.7 0.2 copy-done.7
  76.9 0.8 copy-done.6
  77.7 7.6 %replica_sums.1 = bf16[448,4,128]{2,1,0:T(4,128)(2,1)} custom-call(s32[3]{0:T(128)} %pad_add_fusion.refs_0_, s32[192]{0:T(256)} %reshape.62.refs_1_, bf16[4096,256]{1,0:T(8,128)(2,1)} %all-gather.2.cloned.1.call-done.refs_2_, bf16[8,256,128]{2,1,0:T(8,128)(2,1)} %copy-done.1, bf16[8,256,128]{2,1,0:T(8,128)(2,1)} %copy-done.5, ...), custom_call_target="tpu_custom_call" | custom-call | flops 1073741824 | bytes 6291456 | tf_op jit(solution)/shard_map/replica_sums/pallas_call | solution.py:239
  85.3 21.8 %all_to_all.17 = bf16[32,56,128]{2,1,0:T(8,128)(2,1)} all-to-all(bf16[32,56,128]{2,1,0:T(8,128)(2,1)} %bitcast.23), channel_id=1, replica_groups=mesh['dp_0'=4,'dp_1'=8,'tensor'=16] {'dp_0','dp_1'}, dimensions={0} | all-to-all | bytes 917504 | tf_op jit(solution)/shard_map/all_to_all | solution.py:263
  107.1 4.0 %owner_adam.1 = (f32[128,128]{1,0:T(8,128)}, f32[128,128]{1,0:T(8,128)}, f32[128,128]{1,0:T(8,128)}, f32[9,128,128]{2,1,0:T(8,128)}, f32[9,128,128]{2,1,0:T(8,12...) custom-call(bf16[1792,128]{1,0:T(8,128)(2,1)} %bitcast.24, f32[128,128]{1,0:T(8,128)} %refs_1_.1, f32[128,128]{1,0:T(8,128)} %refs_2_.1, ...), custom_call_target="tpu_custom_call" | custom-call | tf_op jit(solution)/shard_map/owner_adam/pallas_call | solution.py:269
  (29 shorter events, 0.4 us)
Async XLA Ops:
  7.2 13.1 %copy-start = (bf16[128,4096]{1,0:T(8,128)(2,1)S(1)}, bf16[128,4096]{1,0:T(8,128)(2,1)}, u32[]{:S(2)}) copy-start(bf16[128,4096]{1,0:T(8,128)(2,1)} %param.10) | copy-start | bytes 3145732
  7.2 70.5 %all-gather.2.cloned.1.call-start = ((), (), s32[]{:S(2)}) async-start(), calls=%async_computation.3 | async-start | bytes 2359296 | tf_op jit(solution)/shard_map/all_gather | solution.py:220
  20.3 45.1 %copy-start.8 = (s32[1,192,1]{1,2,0:T(1,128)S(1)}, s32[1,192,1]{1,2,0:T(1,128)}, u32[]{:S(2)}) copy-start(s32[1,192,1]{1,2,0:T(1,128)} %param.13) | copy-start | bytes 2308
  47.1 30.6 %copy-start.1 = (bf16[8,256,128]{2,1,0:T(8,128)(2,1)}, bf16[8,256,128]{2,1,0:T(8,128)(2,1)S(1)}, u32[]{:S(2)}) copy-start(bf16[8,256,128]{2,1,0:T(8,128)(2,1)S(1)} %all_to_all.16.refs_3_) | copy-start | bytes 1572868
  47.1 15.6 %collective-permute-start.3 = (bf16[8,256,128]{2,1,0:T(8,128)(2,1)S(1)}, bf16[8,256,128]{2,1,0:T(8,128)(2,1)S(1)}, u32[]{:S(2)}, u32[]{:S(2)}) collective-permute-start(bf16[8,256,128]{2,1,0:T(8,128)(2,1)S(1)} %all_to_all.16.refs_3_), channel_id=1, source_target_pairs={{0,384},{128,0},{256,128},{384,256},{1,385},{129,1},{257,129},{385... | collective-permute-start | bytes 1572872 | tf_op jit(solution)/shard_map/ppermute | solution.py:181
  50.4 18.6 %collective-permute-start = (bf16[8,256,128]{2,1,0:T(8,128)(2,1)S(1)}, bf16[8,256,128]{2,1,0:T(8,128)(2,1)S(1)}, u32[]{:S(2)}, u32[]{:S(2)}) collective-permute-start(bf16[8,256,128]{2,1,0:T(8,128)(2,1)S(1)} %all_to_all.16.refs_3_), channel_id=1, source_target_pairs={{0,128},{128,256},{256,384},{384,0},{1,129},{129,257},{257,385},{3... | collective-permute-start | bytes 1572872 | tf_op jit(solution)/shard_map/ppermute | solution.py:181
  62.7 15.0 %copy-start.2 = (bf16[8,256,128]{2,1,0:T(8,128)(2,1)}, bf16[8,256,128]{2,1,0:T(8,128)(2,1)S(1)}, u32[]{:S(2)}) copy-start(bf16[8,256,128]{2,1,0:T(8,128)(2,1)S(1)} %collective-permute-done.3.refs_7_) | copy-start | bytes 1572868
  62.7 11.1 %collective-permute-start.5 = (bf16[8,256,128]{2,1,0:T(8,128)(2,1)S(1)}, bf16[8,256,128]{2,1,0:T(8,128)(2,1)S(1)}, u32[]{:S(2)}, u32[]{:S(2)}) collective-permute-start(bf16[8,256,128]{2,1,0:T(8,128)(2,1)S(1)} %collective-permute-done.3.refs_7_), channel_id=1, source_target_pairs={{0,384},{128,0},{256,128},{384,256},{1,385},{129,1},{257,129},{385... | collective-permute-start | bytes 1572872 | tf_op jit(solution)/shard_map/ppermute | solution.py:181
  67.1 8.7 %collective-permute-start.1 = (bf16[8,256,128]{2,1,0:T(8,128)(2,1)S(1)}, bf16[8,256,128]{2,1,0:T(8,128)(2,1)S(1)}, u32[]{:S(2)}, u32[]{:S(2)}) collective-permute-start(bf16[8,256,128]{2,1,0:T(8,128)(2,1)S(1)} %all_to_all.16.refs_3_), channel_id=1, source_target_pairs={{0,1},{1,0},{2,3},{3,2},{4,5},{5,4},{6,7},{7,6},{8,9},{9,8},{10,11... | collective-permute-start | bytes 1572872 | tf_op jit(solution)/shard_map/ppermute | solution.py:236
  69.1 8.7 %copy-start.3 = (bf16[8,256,128]{2,1,0:T(8,128)(2,1)}, bf16[8,256,128]{2,1,0:T(8,128)(2,1)S(1)}, u32[]{:S(2)}) copy-start(bf16[8,256,128]{2,1,0:T(8,128)(2,1)S(1)} %collective-permute-done.refs_5_) | copy-start | bytes 1572868
  69.1 6.8 %collective-permute-start.2 = (bf16[8,256,128]{2,1,0:T(8,128)(2,1)S(1)}, bf16[8,256,128]{2,1,0:T(8,128)(2,1)S(1)}, u32[]{:S(2)}, u32[]{:S(2)}) collective-permute-start(bf16[8,256,128]{2,1,0:T(8,128)(2,1)S(1)} %collective-permute-done.refs_5_), channel_id=1, source_target_pairs={{0,1},{1,0},{2,3},{3,2},{4,5},{5,4},{6,7},{7,6},{8,9},{9,8},{10,11... | collective-permute-start | bytes 1572872 | tf_op jit(solution)/shard_map/ppermute | solution.py:236
  71.5 4.4 %collective-permute-start.4 = (bf16[8,256,128]{2,1,0:T(8,128)(2,1)S(1)}, bf16[8,256,128]{2,1,0:T(8,128)(2,1)S(1)}, u32[]{:S(2)}, u32[]{:S(2)}) collective-permute-start(bf16[8,256,128]{2,1,0:T(8,128)(2,1)S(1)} %collective-permute-done.3.refs_7_), channel_id=1, source_target_pairs={{0,1},{1,0},{2,3},{3,2},{4,5},{5,4},{6,7},{7,6},{8,9},{9,8},{10,11... | collective-permute-start | bytes 1572872 | tf_op jit(solution)/shard_map/ppermute | solution.py:236
  73.8 3.9 %copy-start.4 = (bf16[8,256,128]{2,1,0:T(8,128)(2,1)}, bf16[8,256,128]{2,1,0:T(8,128)(2,1)S(1)}, u32[]{:S(2)}) copy-start(bf16[8,256,128]{2,1,0:T(8,128)(2,1)S(1)} %collective-permute-done.5.refs_9_) | copy-start | bytes 1572868
  73.8 3.9 %collective-permute-start.6 = (bf16[8,256,128]{2,1,0:T(8,128)(2,1)S(1)}, bf16[8,256,128]{2,1,0:T(8,128)(2,1)}, u32[]{:S(2)}, u32[]{:S(2)}) collective-permute-start(bf16[8,256,128]{2,1,0:T(8,128)(2,1)S(1)} %collective-permute-done.5.refs_9_), channel_id=1, source_target_pairs={{0,1},{1,0},{2,3},{3,2},{4,5},{5,4},{6,7},{7,6},{8,9},{9,8},{10,11... | collective-permute-start | bytes 1572872 | tf_op jit(solution)/shard_map/ppermute | solution.py:236
  75.9 0.8 copy-start.5
  75.9 1.0 copy-start.7
  76.9 0.8 copy-start.6
Sparse Core Ops, SparseCore 0:
  20.4 45.4 all-gather.1
